TPU v7x, 32 devices: a whole 2x2x4 slice. The times are simulated.
32 devices in a mesh: row: 2 (over y), col: 16 (over z, x, core).
Axes of the slice: x: 2, y: 2, z: 4, core: 2. Of those that a mesh axis runs over, the one named last changes fastest.
Arguments:
- x_field: bfloat16 [65536, 256], P('col'), may hold values from -6 to 6
- observed: bfloat16 [2048, 256], P(('row', 'col')), may hold values from -6 to 6
- sat_scale: float32 [256], replicated, may hold values from 0.5 to 4
- u_coef: bfloat16 [4, 128, 512, 256], P('row', 'col'), may hold values from -0.046875 to 0.046875
- v_coef: bfloat16 [4, 128, 512, 256], P('row', 'col'), may hold values from -0.25 to 0.25
- ranks: int32 [4, 128], P('row', 'col'), may hold values from 16 to 256
Outputs:
- gradient: bfloat16 [65536, 256], P('col')
All inputs are finite; a program needn't handle non-finite values.
Results may differ from a plain program's by a relative error of at most 0.0065.
Values may be sent and summed in bfloat16 or wider, within the bound.
No kernel may reach another device: no remote copies, remote signals or barrier semaphores. Data moves between devices by JAX's collectives and lax.ppermute only.
A program may use at most 64 MiB of HBM per device.

v0:
```python
import jax
import jax.numpy as jnp
from jax import lax
from jax.sharding import PartitionSpec as P


def saturate(predicted, observed, sat_scale):
    misfit = (predicted - observed.astype(jnp.float32)) / sat_scale
    return (sat_scale * jnp.tanh(misfit)).astype(jnp.bfloat16)


def local(x_field, observed, sat_scale, u_coef, v_coef, ranks):
    tile_rows, tile_cols, tile_width, rank_cap = u_coef.shape
    sources = x_field.shape[1]
    rank_mask = (lax.broadcasted_iota(jnp.int32, (1, 1, rank_cap), 2) < ranks[:, :, None]).astype(
        jnp.float32
    )[..., None]
    source_tiles = x_field.reshape(tile_cols, tile_width, sources)
    coeffs = jnp.einsum("ajtk,jts->ajks", v_coef, source_tiles, preferred_element_type=jnp.float32)
    coeffs = (coeffs * rank_mask).astype(jnp.bfloat16)
    predicted = jnp.einsum("ajtk,ajks->ats", u_coef, coeffs, preferred_element_type=jnp.float32)
    predicted = predicted.reshape(tile_rows * tile_width, sources)
    forward_share = lax.psum_scatter(predicted, "col", scatter_dimension=0, tiled=True)
    resid_share = saturate(forward_share, observed, sat_scale)
    group_resid = lax.all_gather(resid_share, "col", axis=0, tiled=True)
    resid_tiles = group_resid.reshape(tile_rows, tile_width, sources)
    adjoint = jnp.einsum("ajtk,ats->ajks", u_coef, resid_tiles, preferred_element_type=jnp.float32)
    adjoint = (adjoint * rank_mask).astype(jnp.bfloat16)
    partial_grad = jnp.einsum("ajtk,ajks->jts", v_coef, adjoint, preferred_element_type=jnp.float32)
    partial_grad = partial_grad.reshape(tile_cols * tile_width, sources)
    grad_share = lax.psum_scatter(partial_grad, "row", scatter_dimension=0, tiled=True).astype(
        jnp.bfloat16
    )
    gradient = lax.all_gather(grad_share, "row", axis=0, tiled=True)
    return gradient


def solution(mesh):
    return jax.shard_map(
        local,
        mesh=mesh,
        in_specs=(
            P("col", None),
            P(("row", "col"), None),
            P(),
            P("row", "col", None, None),
            P("row", "col", None, None),
            P("row", "col"),
        ),
        out_specs=P("col", None),
        check_vma=False,
    )
```

profile of v0, /device:TPU:0, one launch (start us, length us, event | category | flops | bytes accessed | tf_op | source)
XLA Modules:
  0.0 208.0 jit_solution(13282382323822441683)
XLA Ops:
  6.5 0.0 copy-start
  6.5 0.0 reduce-scatter.3.cloned.1.call-start
  6.5 0.9 copy.10
  7.4 0.1 compare_convert_fusion
  7.5 0.6 copy-done
  8.1 0.0 copy-start.1
  8.1 0.0 copy-start.2
  8.1 5.8 %convolution_bitcast_fusion = f32[2,512,256]{1,2,0:T(8,128)S(1)} fusion(bf16[2,8,512,256]{3,2,1,0:T(8,128)(2,1)} %param.9, bf16[8,512,256,1]{2,1,0,3:T(8,128)(2,1)S(1)} %bitcast.31, bf16[2,8,512,256]{3,2,1,0:T(8,128)(2,1)} %param.10, f32[2,8,256]{2,1,0:T(8,128)S(1)} %copy.11), kind=kOutput, calls=%fused_computation.9 | convolution fusion | flops 2149580800 | bytes 11550720 | tf_op jit(solution)/shard_map/ajtk,ajks->ats/dot_general | solution.py:21
  14.0 1.3 copy.12
  15.3 0.0 reduce-scatter.3.cloned.1.call-update
  15.3 0.0 reduce-scatter.5.cloned.1.call-start
  15.4 60.4 %reduce-scatter.3.cloned.1.call-done = f32[64,256]{1,0:T(8,128)} async-done(((f32[1024,256]{1,0:T(8,128)}), f32[64,256]{1,0:T(8,128)}) %reduce-scatter.3.cloned.1.call-update) | async-done | bytes 65552 | tf_op jit(solution)/shard_map/reduce_scatter | solution.py:23
  75.8 0.0 copy-done.1
  75.8 0.0 copy-done.2
  75.8 0.9 multiply_convert_fusion.1
  76.6 20.9 %all_gather.6 = bf16[1024,256]{1,0:T(8,128)(2,1)S(1)} all-gather(bf16[64,256]{1,0:T(8,128)(2,1)S(1)} %multiply_convert_fusion.1), channel_id=1, replica_groups=mesh['row'=2,'col'=16] {'col'}, dimensions={0}, use_global_device_ids=true | all-gather | bytes 557056 | tf_op jit(solution)/shard_map/all_gather | solution.py:25
  97.5 7.8 %fusion.5 = f32[8,512,256]{1,2,0:T(8,128)} fusion(bf16[2,8,512,256]{3,2,1,0:T(8,128)(2,1)} %param.10, bf16[2,512,256,1]{2,1,0,3:T(8,128)(2,1)S(1)} %bitcast.34, bf16[2,8,512,256]{3,2,1,0:T(8,128)(2,1)} %param.9, f32[2,8,256]{2,0,1:T(2,128)S(1)} %compare_convert_fusion), kind=kOutput, calls=%fused_computation.7 | convolution fusion | flops 2149580800 | bytes 13123584 | tf_op jit(solution)/shard_map/ajtk,ajks->jts/dot_general | solution.py:29
  105.3 5.4 %copy.14 = f32[8,512,256]{2,1,0:T(8,128)} copy(f32[8,512,256]{1,2,0:T(8,128)} %fusion.5) | data formatting | bytes 8388608 | tf_op jit(solution)/shard_map/ajtk,ajks->jts/dot_general | solution.py:29
  110.7 0.0 reduce-scatter.5.cloned.1.call-update
  110.7 0.0 all-gather.2.cloned.1.call-start
  110.8 51.7 %reduce-scatter.5.cloned.1.call-done = f32[2048,256]{1,0:T(8,128)} async-done(((f32[4096,256]{1,0:T(8,128)}), f32[2048,256]{1,0:T(8,128)}) %reduce-scatter.5.cloned.1.call-update) | async-done | bytes 2097168 | tf_op jit(solution)/shard_map/reduce_scatter | solution.py:31
  162.5 2.7 %convert_element_type.31 = bf16[2048,256]{1,0:T(8,128)(2,1)} convert(f32[2048,256]{1,0:T(8,128)} %reduce-scatter.5.cloned.1.call-done) | non-fusion elementwise | flops 524288 | bytes 3145728 | tf_op jit(solution)/shard_map/convert_element_type | solution.py:31
  165.2 0.0 all-gather.2.cloned.1.call-update
  165.2 33.2 %all-gather.2.cloned.1.call-done = bf16[4096,256]{1,0:T(8,128)(2,1)} async-done(((bf16[2048,256]{1,0:T(8,128)(2,1)}), bf16[4096,256]{1,0:T(8,128)(2,1)}) %all-gather.2.cloned.1.call-update) | async-done | bytes 2097168 | tf_op jit(solution)/shard_map/all_gather | solution.py:34
  198.4 3.0 %copy.31 = bf16[4096,256]{1,0:T(8,128)(2,1)} copy(bf16[4096,256]{1,0:T(8,128)(2,1)} %all-gather.2.cloned.1.call-done) | data formatting | bytes 4194304
  (1 shorter events, 0.0 us)
Async XLA Ops:
  6.5 1.6 copy-start
  6.5 69.2 %reduce-scatter.3.cloned.1.call-start = ((), (), s32[]{:S(2)}) async-start(), calls=%async_computation.2 | async-start | bytes 1114112 | tf_op jit(solution)/shard_map/reduce_scatter | solution.py:23
  8.1 67.6 %copy-start.1 = (bf16[64,256]{1,0:T(8,128)(2,1)S(1)}, bf16[64,256]{1,0:T(8,128)(2,1)}, u32[]{:S(2)}) copy-start(bf16[64,256]{1,0:T(8,128)(2,1)} %param.7) | copy-start | bytes 98308
  8.1 67.6 %copy-start.2 = (f32[256]{0:T(256)S(1)}, f32[256]{0:T(256)}, u32[]{:S(2)}) copy-start(f32[256]{0:T(256)} %param.8) | copy-start | bytes 3076
  15.3 147.2 %reduce-scatter.5.cloned.1.call-start = ((), (), s32[]{:S(2)}) async-start(), calls=%async_computation.3 | async-start | bytes 6291456 | tf_op jit(solution)/shard_map/reduce_scatter | solution.py:31
  110.7 87.7 %all-gather.2.cloned.1.call-start = ((), (), s32[]{:S(2)}) async-start(), calls=%async_computation.4 | async-start | bytes 3145728 | tf_op jit(solution)/shard_map/all_gather | solution.py:34
Sparse Core Ops, SparseCore 0:
  15.5 60.2 reduce-scatter.2
  110.8 51.6 reduce-scatter.4
  165.3 33.0 all-gather.1
where the time goes:
time: 208 us
  waiting for transfers between devices  145 us (70%)
  blocking collectives  20.9 us (10%)
  matrix products  13.7 us (7%)
  between operations  13.1 us (6%)
  local copies, waits for them, and re-layouts  11.2 us (5%)
  other arithmetic  3.6 us (2%)
    reduce_scatter x1, waiting for transfers between devices, local(): lax.psum_scatter(predicted, 'col', scatter_dimension=0, tiled=True)  60.4 us
    reduce_scatter x1, waiting for transfers between devices, local(): lax.psum_scatter(partial_grad, 'row', scatter_dimension=0, tiled=True)  51.7 us
    all_gather x1, waiting for transfers between devices, local(): gradient = lax.all_gather(grad_share, 'row', axis=0, tiled=True)  33.2 us
    all_gather x1, blocking collectives, local(): group_resid = lax.all_gather(resid_share, 'col', axis=0, tiled=True)  20.9 us
    dot_general x1, matrix products, local(): jnp.einsum('ajtk,ajks->jts', v_coef, adjoint, preferred_element_type=jnp....  7.83 us
    dot_general x1, matrix products, local(): jnp.einsum('ajtk,ajks->ats', u_coef, coeffs, preferred_element_type=jnp.f...  5.84 us
    dot_general x1, local copies, waits for them, and re-layouts, local(): jnp.einsum('ajtk,ajks->jts', v_coef, adjoint, preferred_element_type=jnp....  5.36 us
    unnamed x8, local copies, waits for them, and re-layouts  4.57 us
  transfers between devices with their start and end apart: 3, of which 3 were waited for; matrix products, arithmetic and copies ran while one was open for 0% of the time, Pallas kernels for 0%

commit v1 on v0

v1 whole, which is shorter than its diff:
```python
import functools
import math

import jax
import jax.numpy as jnp
from jax import lax
from jax.experimental import pallas as pl
from jax.experimental.pallas import tpu as pltpu
from jax.sharding import PartitionSpec as P


BF = jnp.bfloat16
F32 = jnp.float32
CUTS = (128, 128)
GROUPS = (4, 4)
VMEM_LIMIT = 26 * 2**20
IN_VMEM = pl.BlockSpec(memory_space=pltpu.VMEM)
IN_SMEM = pl.BlockSpec(memory_space=pltpu.SMEM)
IN_HBM = pl.BlockSpec(memory_space=pltpu.HBM)


def dot_nn(a, b):
    return lax.dot_general(a, b, (((1,), (0,)), ((), ())), preferred_element_type=F32)


def dot_nt(a, b):
    return lax.dot_general(a, b, (((1,), (1,)), ((), ())), preferred_element_type=F32)


def permuted_rows(tile, zs, rb):
    return jnp.concatenate(
        [tile[(z * 4 + q) * rb : (z * 4 + q + 1) * rb] for q in range(4) for z in range(zs)], axis=0
    )


def forward_kernel(dims, ranks, me, obs, x_hbm, u_hbm, v_hbm, *rest):
    tile_rows, tile_cols, width, cap, sources, rb, zs, cuts = dims
    n = len(cuts)
    keep_refs, send_refs = rest[:n], rest[n : 2 * n]
    u_vm, v_vm, x_vm, acc, sems = rest[2 * n :]

    def copies(j):
        span = pl.ds(j * width, width)
        yield pltpu.make_async_copy(x_hbm.at[span], x_vm.at[span], sems.at[j, 0])
        for a in range(tile_rows):
            yield pltpu.make_async_copy(v_hbm.at[a, j], v_vm.at[a, j], sems.at[j, 1 + a])
        for a in range(tile_rows):
            yield pltpu.make_async_copy(u_hbm.at[a, j], u_vm.at[a, j], sems.at[j, 1 + tile_rows + a])

    for j in range(tile_cols):
        for c in copies(j):
            c.start()

    mine, my_x, my_z = me[0], me[1], me[2]
    lane = lax.broadcasted_iota(jnp.int32, (sources, cap), 1)
    acc[...] = jnp.zeros_like(acc)

    def body(j, carry):
        for c in copies(j):
            c.wait()
        xt = x_vm[pl.ds(pl.multiple_of(j * width, width), width), :].T
        for a in range(tile_rows):
            c = dot_nn(xt, v_vm[a, j])
            c = jnp.where(lane < ranks[a * tile_cols + j], c, 0.0).astype(BF)
            acc[a] += dot_nt(c, permuted_rows(u_vm[a, j], zs, rb))
        return carry

    lax.fori_loop(0, tile_cols, body, 0)

    nz = zs * tile_rows
    q_lanes = width // 4
    obs_t = obs[...].astype(F32).T
    obs_t = jnp.concatenate([obs_t] * nz, axis=1)
    spot = lax.broadcasted_iota(jnp.int32, (sources, nz * rb), 1)
    obs_t = jnp.where((spot >= my_z * rb) & (spot < (my_z + 1) * rb), obs_t, 0.0)
    for q in range(4):
        qx, qc = q // 2, q % 2
        slot = qx ^ my_x
        row = 0
        for i, s in enumerate(cuts):
            val = jnp.concatenate(
                [acc[a, row : row + s, q * q_lanes : (q + 1) * q_lanes] for a in range(tile_rows)], axis=1
            )

            @pl.when(mine == qc)
            def _():
                own = jnp.where(slot == 0, 1.0, 0.0).astype(F32)
                keep_refs[i][slot] = val - own * obs_t[row : row + s]

            @pl.when(mine != qc)
            def _():
                send_refs[i][slot] = val.astype(BF)

            row += s


def forward(x, obs, u, v, ranks, me, cuts, zs):
    tile_rows, tile_cols, width, cap = u.shape
    sources = x.shape[1]
    rb = obs.shape[0]
    block = tile_rows * width // 4
    dims = (tile_rows, tile_cols, width, cap, sources, rb, zs, cuts)
    outs = [pltpu.VMEM((2, s, block), F32) for s in cuts] + [pltpu.VMEM((2, s, block), BF) for s in cuts]
    outs += [pltpu.VMEM(u.shape, BF), pltpu.VMEM(v.shape, BF)]
    room = 2**20 + sum(math.prod(o.shape) * o.dtype.itemsize for o in outs)
    res = pl.pallas_call(
        functools.partial(forward_kernel, dims),
        in_specs=[IN_SMEM, IN_SMEM, IN_VMEM, IN_HBM, IN_HBM, IN_HBM],
        out_specs=[IN_VMEM] * len(outs),
        scratch_shapes=[
            pltpu.VMEM(x.shape, BF),
            pltpu.VMEM((tile_rows, sources, width), F32),
            pltpu.SemaphoreType.DMA((tile_cols, 1 + 2 * tile_rows)),
        ],
        out_shape=outs,
        compiler_params=pltpu.CompilerParams(vmem_limit_bytes=63 * 2**20 - room),
        cost_estimate=pl.CostEstimate(
            flops=4 * tile_rows * tile_cols * width * cap * sources,
            bytes_accessed=4 * u.size + 2 * x.size,
            transcendentals=0,
        ),
        name="forward",
    )(ranks.reshape(-1), me, obs, x, u, v)
    n = len(cuts)
    return res[:n], res[n : 2 * n], res[2 * n], res[2 * n + 1]


def adjoint_kernel(dims, ranks, me, r00, r01, r10, r11, u_ref, v_ref, g_ref, held):
    tile_rows, tile_cols, start, count, width, cap, s, rb, zs = dims
    base = me[1] * 2 + me[0]
    held[base] = r00[...]
    held[base ^ 2] = r01[...]
    held[base ^ 1] = r10[...]
    held[base ^ 3] = r11[...]
    q_lanes = width // 4
    lane = lax.broadcasted_iota(jnp.int32, (s, cap), 1)
    r = [
        jnp.concatenate([held[q][:, a * q_lanes : (a + 1) * q_lanes] for q in range(4)], axis=1)
        for a in range(tile_rows)
    ]
    for j in range(count):
        total = None
        for a in range(tile_rows):
            adj = dot_nn(r[a], permuted_rows(u_ref[a, start + j], zs, rb))
            adj = jnp.where(lane < ranks[a * tile_cols + start + j], adj, 0.0).astype(BF)
            g = dot_nt(adj, v_ref[a, start + j])
            total = g if total is None else total + g
        g_ref[j] = total.astype(BF)


def adjoint(rs, u, v, ranks, me, start, count, rb, zs):
    tile_rows, tile_cols, width, cap = u.shape
    s, block = rs[0].shape
    dims = (tile_rows, tile_cols, start, count, width, cap, s, rb, zs)
    return pl.pallas_call(
        functools.partial(adjoint_kernel, dims),
        in_specs=[IN_SMEM, IN_SMEM] + [IN_VMEM] * 6,
        out_specs=IN_VMEM,
        scratch_shapes=[pltpu.VMEM((4, s, block), BF)],
        out_shape=jax.ShapeDtypeStruct((count, s, width), BF),
        compiler_params=pltpu.CompilerParams(vmem_limit_bytes=VMEM_LIMIT),
        cost_estimate=pl.CostEstimate(
            flops=4 * tile_rows * count * width * cap * s, bytes_accessed=4 * s * block, transcendentals=0
        ),
        name="adjoint",
    )(ranks.reshape(-1), me, *rs, u, v)


def finish_kernel(n, *refs):
    out = refs[-1]
    j = pl.program_id(0)
    for i in range(n):
        a, b = refs[2 * i], refs[2 * i + 1]
        s = a.shape[1]
        t = a[j].astype(F32) + b[j].astype(F32)
        out[:, i * s : (i + 1) * s] = t.T.astype(BF)


def finish(out, pairs, start, lane_block, rows, sources):
    count, s, width = pairs[0][0].shape
    n = len(pairs)
    flat = [p for pair in pairs for p in pair]
    lanes = n * s
    aliases = {}
    specs = [IN_VMEM] * len(flat)
    body = functools.partial(finish_kernel, n)
    if out is not None:
        aliases = {len(flat): 0}
        specs = specs + [IN_HBM]
        inner, m = body, len(flat)
        body = lambda *refs: inner(*refs[:m], refs[-1])
        flat = flat + [out]
    return pl.pallas_call(
        body,
        grid=(count,),
        in_specs=specs,
        out_specs=pl.BlockSpec((width, lanes), lambda j: (start + j, lane_block)),
        out_shape=jax.ShapeDtypeStruct((rows, sources), BF),
        input_output_aliases=aliases,
        compiler_params=pltpu.CompilerParams(vmem_limit_bytes=VMEM_LIMIT),
        cost_estimate=pl.CostEstimate(flops=0, bytes_accessed=2 * count * lanes * width, transcendentals=0),
        name="finish",
    )(*flat)


def solution(mesh):
    n_row, n_col = mesh.shape["row"], mesh.shape["col"]
    nz = n_col // 4
    assert n_col == 4 * nz and nz & (nz - 1) == 0
    core_swap = [(c, c ^ 1) for c in range(n_col)]
    x_swap = [(c, c ^ 2) for c in range(n_col)]
    z_swaps = [[(c, c ^ (4 * k)) for c in range(n_col)] for k in range(1, nz)]
    row_swap = [(0, 1), (1, 0)]

    def local(x_field, observed, sat_scale, u, v, ranks):
        tile_rows, tile_cols, _, _ = u.shape
        rows, sources = x_field.shape
        rb = observed.shape[0]
        zs = nz // tile_rows
        cuts = tuple(c * sources // 256 for c in CUTS)
        me_col = lax.axis_index("col")
        me = jnp.stack([me_col % 2, (me_col // 2) % 2, me_col // 4]).astype(jnp.int32)
        sat = sat_scale[:, None]
        keeps, sends, u, v = forward(x_field, observed, u, v, ranks, me, cuts, zs)

        def residual(send, keep, sc):
            got = lax.ppermute(send, "col", core_swap)
            half = keep + got.astype(F32)
            got = lax.ppermute(half[1].astype(BF), "col", x_swap)
            quarter = half[0] + got.astype(F32)
            mine = quarter.astype(BF)
            total = quarter
            for p in z_swaps:
                total = total + lax.ppermute(mine, "col", p).astype(F32)
            r00 = (sc * jnp.tanh(total / sc)).astype(BF)
            r01 = lax.ppermute(r00, "col", x_swap)
            r10 = lax.ppermute(r00, "col", core_swap)
            r11 = lax.ppermute(r01, "col", core_swap)
            return r00, r01, r10, r11

        swapped = {}
        row = 0
        for i, s in enumerate(cuts):
            resid = residual(sends[i], keeps[i], sat[row : row + s])
            row += s
            per = tile_cols // GROUPS[i]
            for g in range(GROUPS[i]):
                part = adjoint(resid, u, v, ranks, me, g * per, per, rb, zs)
                if n_row == 2:
                    swapped[i, g] = (part, lax.ppermute(part, "row", row_swap))
                else:
                    whole = lax.psum(part.astype(F32), "row").astype(BF)
                    swapped[i, g] = (whole, jnp.zeros_like(whole))
        out = None
        lane = 0
        i = 0
        while i < len(cuts):
            ids, lanes = [i], cuts[i]
            while lanes % 128 != 0:
                ids.append(ids[-1] + 1)
                lanes += cuts[ids[-1]]
            per = tile_cols // GROUPS[i]
            for g in range(GROUPS[i]):
                out = finish(out, [swapped[k, g] for k in ids], g * per, lane // lanes, rows, sources)
            lane += lanes
            i = ids[-1] + 1
        return out

    return jax.shard_map(
        local,
        mesh=mesh,
        in_specs=(
            P("col", None),
            P(("row", "col"), None),
            P(),
            P("row", "col", None, None),
            P("row", "col", None, None),
            P("row", "col"),
        ),
        out_specs=P("col", None),
        check_vma=False,
    )
```

time: 208 us -> 84.6 us (0.41)
  waiting for transfers between devices: 145 us -> 32.9 us
  Pallas kernels: 0 us -> 25 us
  starting transfers between devices: 0.09 us -> 24 us
  blocking collectives: 20.9 us -> 0 us
  matrix products: 13.7 us -> 0 us
  between operations: 13.1 us -> 0.18 us
  local copies, waits for them, and re-layouts: 11.2 us -> 1.3 us
  other arithmetic: 3.6 us -> 0.98 us
    reduce_scatter x2 -> x0, waiting for transfers between devices: 112 us -> none  [the longest x1 60.4 us: local(): lax.psum_scatter(predicted, 'col', scatter_dimension=0, tiled=True)]
    all_gather x1 -> x0, waiting for transfers between devices: 33.2 us -> none  [local(): gradient = lax.all_gather(grad_share, 'row', axis=0, tiled=True)]
    ppermute x0 -> x24, waiting for transfers between devices: none -> 32.9 us  [the longest x8 16.3 us: local(): swapped[i, g] = (part, lax.ppermute(part, 'row', row_swap))]
    pallas_call x0 -> x17, Pallas kernels: none -> 25 us  [the longest x8 10.2 us: adjoint(): pl.pallas_call(functools.partial(adjoint_kernel, dims), in_specs=[IN_SMEM...]
    ppermute x0 -> x24, starting transfers between devices: none -> 24 us  [the longest x6 9.13 us: residual(): total = total + lax.ppermute(mine, 'col', p).astype(F32)]
    all_gather x1 -> x0, blocking collectives: 20.9 us -> none  [local(): group_resid = lax.all_gather(resid_share, 'col', axis=0, tiled=True)]
    dot_general x2 -> x0, matrix products: 13.7 us -> none  [the longest x1 7.83 us: local(): jnp.einsum('ajtk,ajks->jts', v_coef, adjoint, preferred_element_type=jnp....]
    dot_general x2 -> x0, local copies, waits for them, and re-layouts: 6.67 us -> none  [the longest x1 5.36 us: local(): jnp.einsum('ajtk,ajks->jts', v_coef, adjoint, preferred_element_type=jnp....]
  transfers between devices with their start and end apart: 3 -> 24, of which waited for: 3 -> 12; matrix products, arithmetic and copies ran while one was open for 0% -> 0% of each run, Pallas kernels for 0% -> 19%
where the time goes in v1:
time: 84.6 us; the launch traced here: 84.4 us
  waiting for transfers between devices  32.9 us (39%)
  Pallas kernels  25 us (30%)
  starting transfers between devices  24 us (28%)
  local copies, waits for them, and re-layouts  1.3 us (2%)
  other arithmetic  0.98 us (1%)
    ppermute x8, waiting for transfers between devices, local(): swapped[i, g] = (part, lax.ppermute(part, 'row', row_swap))  16.3 us
    pallas_call x8, Pallas kernels, adjoint(): pl.pallas_call(functools.partial(adjoint_kernel, dims), in_specs=[IN_SMEM...  10.2 us
    ppermute x6, starting transfers between devices, residual(): total = total + lax.ppermute(mine, 'col', p).astype(F32)  9.13 us
    ppermute x8, starting transfers between devices, local(): swapped[i, g] = (part, lax.ppermute(part, 'row', row_swap))  8.5 us
    pallas_call x1, Pallas kernels, forward(): pl.pallas_call(functools.partial(forward_kernel, dims), in_specs=[IN_SMEM...  7.78 us
    pallas_call x8, Pallas kernels, finish(): pl.pallas_call(body, grid=(count,), in_specs=specs, out_specs=pl.BlockSpe...  7 us
    ppermute x2, waiting for transfers between devices, residual(): r01 = lax.ppermute(r00, 'col', x_swap)  5.81 us
    ppermute x6, waiting for transfers between devices, residual(): total = total + lax.ppermute(mine, 'col', p).astype(F32)  4.69 us
  transfers between devices with their start and end apart: 24, of which 12 were waited for; matrix products, arithmetic and copies ran while one was open for 0% of the time, Pallas kernels for 19%

profile of v1, /device:TPU:0, one launch (start us, length us, event | category | flops | bytes accessed | tf_op | source)
XLA Modules:
  0.0 84.4 jit_solution(13386102579648096309)
XLA Ops:
  0.0 1.3 %reshape.8.ranks = s32[16]{0:T(128)} reshape(s32[2,8]{1,0:T(2,128)} %param.11) | data formatting | bytes 128 | tf_op jit(solution)/shard_map/reshape | solution.py:166
  1.9 7.8 %forward.1 = (f32[2,128,256]{2,1,0:T(8,128)S(1)}, f32[2,128,256]{2,1,0:T(8,128)S(1)}, bf16[2,128,256]{2,1,0:T(8,128)(2,1)S(1)}, bf16[2,128,256]{2,1,0:T(8,128)(2...) custom-call(s32[16]{0:T(128)} %reshape.8.ranks, s32[3]{0:T(128)} %pad_add_fusion.me, ...), custom_call_target="tpu_custom_call" | custom-call | flops 2147483648 | bytes 10485760 | tf_op jit(solution)/shard_map/forward/pallas_call | solution.py:106
  10.4 0.9 %collective-permute-done.12 = bf16[2,128,256]{2,1,0:T(8,128)(2,1)S(1)} collective-permute-done((bf16[2,128,256]{2,1,0:T(8,128)(2,1)S(1)}, bf16[2,128,256]{2,1,0:T(8,128)(2,1)S(1)}, u32[]{:S(2)}, u32[]{:S(2)}) %collective-permute-start.12) | collective-permute-done | bytes 131104 | tf_op jit(solution)/shard_map/ppermute | solution.py:227
  11.3 2.9 %collective-permute-start.13 = (bf16[128,256]{1,0:T(8,128)(2,1)S(1)}, bf16[128,256]{1,0:T(8,128)(2,1)S(1)}, u32[]{:S(2)}, u32[]{:S(2)}) collective-permute-start(bf16[128,256]{1,0:T(8,128)(2,1)S(1)} %fusion.5), channel_id=1, source_target_pairs={{0,2},{1,3},{2,0},{3,1},{4,6},{5,7},{6,4},{7,5},{8,10},{9,11},{10,... | collective-permute-start | bytes 196616 | tf_op jit(solution)/shard_map/ppermute | solution.py:229
  14.3 2.4 %collective-permute-done.13 = bf16[128,256]{1,0:T(8,128)(2,1)S(1)} collective-permute-done((bf16[128,256]{1,0:T(8,128)(2,1)S(1)}, bf16[128,256]{1,0:T(8,128)(2,1)S(1)}, u32[]{:S(2)}, u32[]{:S(2)}) %collective-permute-start.13) | collective-permute-done | bytes 65568 | tf_op jit(solution)/shard_map/ppermute | solution.py:229
  16.7 4.0 %collective-permute-start.16 = (bf16[128,256]{1,0:T(8,128)(2,1)S(1)}, bf16[128,256]{1,0:T(8,128)(2,1)S(1)}, u32[]{:S(2)}, u32[]{:S(2)}) collective-permute-start(bf16[128,256]{1,0:T(8,128)(2,1)S(1)} %fusion.3), channel_id=1, source_target_pairs={{0,12},{1,13},{2,14},{3,15},{4,8},{5,9},{6,10},{7,11},{8,4},{9,5},... | collective-permute-start | bytes 196616 | tf_op jit(solution)/shard_map/ppermute | solution.py:234
  21.4 2.0 %collective-permute-done.16 = bf16[128,256]{1,0:T(8,128)(2,1)S(1)} collective-permute-done((bf16[128,256]{1,0:T(8,128)(2,1)S(1)}, bf16[128,256]{1,0:T(8,128)(2,1)S(1)}, u32[]{:S(2)}, u32[]{:S(2)}) %collective-permute-start.16) | collective-permute-done | bytes 65568 | tf_op jit(solution)/shard_map/ppermute | solution.py:234
  23.4 2.6 %collective-permute-done.15 = bf16[128,256]{1,0:T(8,128)(2,1)S(1)} collective-permute-done((bf16[128,256]{1,0:T(8,128)(2,1)S(1)}, bf16[128,256]{1,0:T(8,128)(2,1)S(1)}, u32[]{:S(2)}, u32[]{:S(2)}) %collective-permute-start.15) | collective-permute-done | bytes 65568 | tf_op jit(solution)/shard_map/ppermute | solution.py:234
  26.2 1.6 %collective-permute-start.17 = (bf16[128,256]{1,0:T(8,128)(2,1)S(1)}, bf16[128,256]{1,0:T(8,128)(2,1)S(1)}, u32[]{:S(2)}, u32[]{:S(2)}) collective-permute-start(bf16[128,256]{1,0:T(8,128)(2,1)S(1)} %multiply_convert_fusion.r00), channel_id=1, source_target_pairs={{0,2},{1,3},{2,0},{3,1},{4,6},{5,7},{6,4},{7,5},{8,10},{9,11},{10,... | collective-permute-start | bytes 196616 | tf_op jit(solution)/shard_map/ppermute | solution.py:236
  28.4 2.2 %collective-permute-done.17.r01 = bf16[128,256]{1,0:T(8,128)(2,1)S(1)} collective-permute-done((bf16[128,256]{1,0:T(8,128)(2,1)S(1)}, bf16[128,256]{1,0:T(8,128)(2,1)S(1)}, u32[]{:S(2)}, u32[]{:S(2)}) %collective-permute-start.17) | collective-permute-done | bytes 65568 | tf_op jit(solution)/shard_map/ppermute | solution.py:236
  30.5 1.6 %collective-permute-done.1 = bf16[128,256]{1,0:T(8,128)(2,1)S(1)} collective-permute-done((bf16[128,256]{1,0:T(8,128)(2,1)S(1)}, bf16[128,256]{1,0:T(8,128)(2,1)S(1)}, u32[]{:S(2)}, u32[]{:S(2)}) %collective-permute-start.1) | collective-permute-done | bytes 65568 | tf_op jit(solution)/shard_map/ppermute | solution.py:229
  32.1 2.3 %collective-permute-start.4 = (bf16[128,256]{1,0:T(8,128)(2,1)S(1)}, bf16[128,256]{1,0:T(8,128)(2,1)S(1)}, u32[]{:S(2)}, u32[]{:S(2)}) collective-permute-start(bf16[128,256]{1,0:T(8,128)(2,1)S(1)} %fusion.2), channel_id=1, source_target_pairs={{0,12},{1,13},{2,14},{3,15},{4,8},{5,9},{6,10},{7,11},{8,4},{9,5},... | collective-permute-start | bytes 196616 | tf_op jit(solution)/shard_map/ppermute | solution.py:234
  34.4 2.1 %collective-permute-start.2 = (bf16[128,256]{1,0:T(8,128)(2,1)S(1)}, bf16[128,256]{1,0:T(8,128)(2,1)S(1)}, u32[]{:S(2)}, u32[]{:S(2)}) collective-permute-start(bf16[128,256]{1,0:T(8,128)(2,1)S(1)} %fusion.2), channel_id=1, source_target_pairs={{0,4},{1,5},{2,6},{3,7},{4,0},{5,1},{6,2},{7,3},{8,12},{9,13},{10,... | collective-permute-start | bytes 196616 | tf_op jit(solution)/shard_map/ppermute | solution.py:234
  36.6 1.3 %adjoint.13.refs_0_ = bf16[2,128,512]{2,1,0:T(8,128)(2,1)S(1)} custom-call(s32[16]{0:T(128)S(1)} %copy-done.1, s32[3]{0:T(128)S(1)} %copy-done, bf16[128,256]{1,0:T(8,128)(2,1)S(1)} %multiply_convert_fusion.r00, bf16[128,256]{1,0:T(8,128)(2,1)S(1)} %collective-permute-done.17.r01, bf16[128,256]{1,0:T(8,128)(2,1)S(1)} %collective-permute-done.18.r10, ...), custom_call_target="tpu_custom_call" | custom-call | flops 268435456 | bytes 131072 | tf_op jit(solution)/shard_map/adjoint/pallas_call | solution.py:155
  37.9 1.6 %collective-permute-start.21 = (bf16[2,128,512]{2,1,0:T(8,128)(2,1)S(1)}, bf16[2,128,512]{2,1,0:T(8,128)(2,1)S(1)}, u32[]{:S(2)}, u32[]{:S(2)}) collective-permute-start(bf16[2,128,512]{2,1,0:T(8,128)(2,1)S(1)} %adjoint.13.refs_0_), channel_id=1, source_target_pairs={{0,16},{16,0},{1,17},{17,1},{2,18},{18,2},{3,19},{19,3},{4,20},{20... | collective-permute-start | bytes 786440 | tf_op jit(solution)/shard_map/ppermute | solution.py:250
  39.5 1.3 %adjoint.14.refs_0_ = bf16[2,128,512]{2,1,0:T(8,128)(2,1)S(1)} custom-call(s32[16]{0:T(128)S(1)} %copy-done.1, s32[3]{0:T(128)S(1)} %copy-done, bf16[128,256]{1,0:T(8,128)(2,1)S(1)} %multiply_convert_fusion.r00, bf16[128,256]{1,0:T(8,128)(2,1)S(1)} %collective-permute-done.17.r01, bf16[128,256]{1,0:T(8,128)(2,1)S(1)} %collective-permute-done.18.r10, ...), custom_call_target="tpu_custom_call" | custom-call | flops 268435456 | bytes 131072 | tf_op jit(solution)/shard_map/adjoint/pallas_call | solution.py:155
  41.3 1.3 %adjoint.15.refs_0_ = bf16[2,128,512]{2,1,0:T(8,128)(2,1)S(1)} custom-call(s32[16]{0:T(128)S(1)} %copy-done.1, s32[3]{0:T(128)S(1)} %copy-done, bf16[128,256]{1,0:T(8,128)(2,1)S(1)} %multiply_convert_fusion.r00, bf16[128,256]{1,0:T(8,128)(2,1)S(1)} %collective-permute-done.17.r01, bf16[128,256]{1,0:T(8,128)(2,1)S(1)} %collective-permute-done.18.r10, ...), custom_call_target="tpu_custom_call" | custom-call | flops 268435456 | bytes 131072 | tf_op jit(solution)/shard_map/adjoint/pallas_call | solution.py:155
  42.6 1.6 %collective-permute-start.23 = (bf16[2,128,512]{2,1,0:T(8,128)(2,1)S(1)}, bf16[2,128,512]{2,1,0:T(8,128)(2,1)S(1)}, u32[]{:S(2)}, u32[]{:S(2)}) collective-permute-start(bf16[2,128,512]{2,1,0:T(8,128)(2,1)S(1)} %adjoint.15.refs_0_), channel_id=1, source_target_pairs={{0,16},{16,0},{1,17},{17,1},{2,18},{18,2},{3,19},{19,3},{4,20},{20... | collective-permute-start | bytes 786440 | tf_op jit(solution)/shard_map/ppermute | solution.py:250
  45.0 3.6 %collective-permute-done.5.r01 = bf16[128,256]{1,0:T(8,128)(2,1)S(1)} collective-permute-done((bf16[128,256]{1,0:T(8,128)(2,1)S(1)}, bf16[128,256]{1,0:T(8,128)(2,1)S(1)}, u32[]{:S(2)}, u32[]{:S(2)}) %collective-permute-start.5) | collective-permute-done | bytes 65568 | tf_op jit(solution)/shard_map/ppermute | solution.py:236
  48.6 1.2 %collective-permute-done.7.r11 = bf16[128,256]{1,0:T(8,128)(2,1)S(1)} collective-permute-done((bf16[128,256]{1,0:T(8,128)(2,1)S(1)}, bf16[128,256]{1,0:T(8,128)(2,1)S(1)}, u32[]{:S(2)}, u32[]{:S(2)}) %collective-permute-start.7) | collective-permute-done | bytes 65568 | tf_op jit(solution)/shard_map/ppermute | solution.py:238
  49.9 1.3 %adjoint.11.refs_0_ = bf16[2,128,512]{2,1,0:T(8,128)(2,1)S(1)} custom-call(s32[16]{0:T(128)S(1)} %copy-done.1, s32[3]{0:T(128)S(1)} %copy-done, bf16[128,256]{1,0:T(8,128)(2,1)S(1)} %multiply_convert_fusion.1.r00, bf16[128,256]{1,0:T(8,128)(2,1)S(1)} %collective-permute-done.5.r01, bf16[128,256]{1,0:T(8,128)(2,1)S(1)} %collective-permute-done.6.r10, ...), custom_call_target="tpu_custom_call" | custom-call | flops 268435456 | bytes 131072 | tf_op jit(solution)/shard_map/adjoint/pallas_call | solution.py:155
  51.8 1.3 %adjoint.12.refs_0_ = bf16[2,128,512]{2,1,0:T(8,128)(2,1)S(1)} custom-call(s32[16]{0:T(128)S(1)} %copy-done.1, s32[3]{0:T(128)S(1)} %copy-done, bf16[128,256]{1,0:T(8,128)(2,1)S(1)} %multiply_convert_fusion.r00, bf16[128,256]{1,0:T(8,128)(2,1)S(1)} %collective-permute-done.17.r01, bf16[128,256]{1,0:T(8,128)(2,1)S(1)} %collective-permute-done.18.r10, ...), custom_call_target="tpu_custom_call" | custom-call | flops 268435456 | bytes 131072 | tf_op jit(solution)/shard_map/adjoint/pallas_call | solution.py:155
  53.1 1.5 %collective-permute-start.20 = (bf16[2,128,512]{2,1,0:T(8,128)(2,1)S(1)}, bf16[2,128,512]{2,1,0:T(8,128)(2,1)S(1)}, u32[]{:S(2)}, u32[]{:S(2)}) collective-permute-start(bf16[2,128,512]{2,1,0:T(8,128)(2,1)S(1)} %adjoint.12.refs_0_), channel_id=1, source_target_pairs={{0,16},{16,0},{1,17},{17,1},{2,18},{18,2},{3,19},{19,3},{4,20},{20... | collective-permute-start | bytes 786440 | tf_op jit(solution)/shard_map/ppermute | solution.py:250
  54.6 1.3 %adjoint.10.refs_0_ = bf16[2,128,512]{2,1,0:T(8,128)(2,1)S(1)} custom-call(s32[16]{0:T(128)S(1)} %copy-done.1, s32[3]{0:T(128)S(1)} %copy-done, bf16[128,256]{1,0:T(8,128)(2,1)S(1)} %multiply_convert_fusion.1.r00, bf16[128,256]{1,0:T(8,128)(2,1)S(1)} %collective-permute-done.5.r01, bf16[128,256]{1,0:T(8,128)(2,1)S(1)} %collective-permute-done.6.r10, ...), custom_call_target="tpu_custom_call" | custom-call | flops 268435456 | bytes 131072 | tf_op jit(solution)/shard_map/adjoint/pallas_call | solution.py:155
  55.9 1.3 %adjoint.9.refs_0_ = bf16[2,128,512]{2,1,0:T(8,128)(2,1)S(1)} custom-call(s32[16]{0:T(128)S(1)} %copy-done.1, s32[3]{0:T(128)S(1)} %copy-done, bf16[128,256]{1,0:T(8,128)(2,1)S(1)} %multiply_convert_fusion.1.r00, bf16[128,256]{1,0:T(8,128)(2,1)S(1)} %collective-permute-done.5.r01, bf16[128,256]{1,0:T(8,128)(2,1)S(1)} %collective-permute-done.6.r10, ...), custom_call_target="tpu_custom_call" | custom-call | flops 268435456 | bytes 131072 | tf_op jit(solution)/shard_map/adjoint/pallas_call | solution.py:155
  57.2 1.3 %adjoint.8.refs_0_ = bf16[2,128,512]{2,1,0:T(8,128)(2,1)S(1)} custom-call(s32[16]{0:T(128)S(1)} %copy-done.1, s32[3]{0:T(128)S(1)} %copy-done, bf16[128,256]{1,0:T(8,128)(2,1)S(1)} %multiply_convert_fusion.1.r00, bf16[128,256]{1,0:T(8,128)(2,1)S(1)} %collective-permute-done.5.r01, bf16[128,256]{1,0:T(8,128)(2,1)S(1)} %collective-permute-done.6.r10, ...), custom_call_target="tpu_custom_call" | custom-call | flops 268435456 | bytes 131072 | tf_op jit(solution)/shard_map/adjoint/pallas_call | solution.py:155
  59.1 1.5 %collective-permute-start.9 = (bf16[2,128,512]{2,1,0:T(8,128)(2,1)S(1)}, bf16[2,128,512]{2,1,0:T(8,128)(2,1)S(1)}, u32[]{:S(2)}, u32[]{:S(2)}) collective-permute-start(bf16[2,128,512]{2,1,0:T(8,128)(2,1)S(1)} %adjoint.9.refs_0_), channel_id=1, source_target_pairs={{0,16},{16,0},{1,17},{17,1},{2,18},{18,2},{3,19},{19,3},{4,20},{20... | collective-permute-start | bytes 786440 | tf_op jit(solution)/shard_map/ppermute | solution.py:250
  63.8 4.5 %collective-permute-done.20.refs_1_ = bf16[2,128,512]{2,1,0:T(8,128)(2,1)S(1)} collective-permute-done((bf16[2,128,512]{2,1,0:T(8,128)(2,1)S(1)}, bf16[2,128,512]{2,1,0:T(8,128)(2,1)S(1)}, u32[]{:S(2)}, u32[]{:S(2)}) %collective-permute-start.20) | collective-permute-done | bytes 262176 | tf_op jit(solution)/shard_map/ppermute | solution.py:250
  70.0 3.9 %collective-permute-done.10.refs_1_ = bf16[2,128,512]{2,1,0:T(8,128)(2,1)S(1)} collective-permute-done((bf16[2,128,512]{2,1,0:T(8,128)(2,1)S(1)}, bf16[2,128,512]{2,1,0:T(8,128)(2,1)S(1)}, u32[]{:S(2)}, u32[]{:S(2)}) %collective-permute-start.10) | collective-permute-done | bytes 262176 | tf_op jit(solution)/shard_map/ppermute | solution.py:250
  73.8 0.9 %finish.13.refs_2_ = bf16[4096,256]{1,0:T(8,128)(2,1)} custom-call(bf16[2,128,512]{2,1,0:T(8,128)(2,1)S(1)} %adjoint.10.refs_0_, bf16[2,128,512]{2,1,0:T(8,128)(2,1)S(1)} %collective-permute-done.10.refs_1_, bf16[4096,256]{1,0:T(8,128)(2,1)} %finish.12.refs_2_), custom_call_target="tpu_custom_call", output_to_operand_aliasing={{}: (2, {})} | custom-call | bytes 262144 | tf_op jit(solution)/shard_map/finish/pallas_call | solution.py:193
  74.7 4.7 %collective-permute-done.9.refs_1_ = bf16[2,128,512]{2,1,0:T(8,128)(2,1)S(1)} collective-permute-done((bf16[2,128,512]{2,1,0:T(8,128)(2,1)S(1)}, bf16[2,128,512]{2,1,0:T(8,128)(2,1)S(1)}, u32[]{:S(2)}, u32[]{:S(2)}) %collective-permute-start.9) | collective-permute-done | bytes 262176 | tf_op jit(solution)/shard_map/ppermute | solution.py:250
  80.3 3.2 %collective-permute-done.8.refs_1_ = bf16[2,128,512]{2,1,0:T(8,128)(2,1)S(1)} collective-permute-done((bf16[2,128,512]{2,1,0:T(8,128)(2,1)S(1)}, bf16[2,128,512]{2,1,0:T(8,128)(2,1)S(1)}, u32[]{:S(2)}, u32[]{:S(2)}) %collective-permute-start.8) | collective-permute-done | bytes 262176 | tf_op jit(solution)/shard_map/ppermute | solution.py:250
  (50 shorter events, 12.1 us)
Async XLA Ops:
  1.9 12.3 %copy-start.2 = (f32[256]{0:T(256)S(1)}, f32[256]{0:T(256)}, u32[]{:S(2)}) copy-start(f32[256]{0:T(256)} %param.8) | copy-start | bytes 3076
  9.7 26.8 %copy-start = (s32[3]{0:T(128)S(1)}, s32[3]{0:T(128)}, u32[]{:S(2)}) copy-start(s32[3]{0:T(128)} %pad_add_fusion.me) | copy-start | bytes 40
  9.7 26.8 %copy-start.1 = (s32[16]{0:T(128)S(1)}, s32[16]{0:T(128)}, u32[]{:S(2)}) copy-start(s32[16]{0:T(128)} %reshape.8.ranks) | copy-start | bytes 196
  9.8 1.5 %collective-permute-start.12 = (bf16[2,128,256]{2,1,0:T(8,128)(2,1)S(1)}, bf16[2,128,256]{2,1,0:T(8,128)(2,1)S(1)}, u32[]{:S(2)}, u32[]{:S(2)}) collective-permute-start(bf16[2,128,256]{2,1,0:T(8,128)(2,1)S(1)} %get-tuple-element.16), channel_id=1, source_target_pairs={{0,1},{1,0},{2,3},{3,2},{4,5},{5,4},{6,7},{7,6},{8,9},{9,8},{10,11... | collective-permute-start | bytes 393224 | tf_op jit(solution)/shard_map/ppermute | solution.py:227
  10.3 11.1 %collective-permute-start = (bf16[2,128,256]{2,1,0:T(8,128)(2,1)S(1)}, bf16[2,128,256]{2,1,0:T(8,128)(2,1)S(1)}, u32[]{:S(2)}, u32[]{:S(2)}) collective-permute-start(bf16[2,128,256]{2,1,0:T(8,128)(2,1)S(1)} %get-tuple-element.12), channel_id=1, source_target_pairs={{0,1},{1,0},{2,3},{3,2},{4,5},{5,4},{6,7},{7,6},{8,9},{9,8},{10,11... | collective-permute-start | bytes 393224 | tf_op jit(solution)/shard_map/ppermute | solution.py:227
  11.3 5.3 %collective-permute-start.13 = (bf16[128,256]{1,0:T(8,128)(2,1)S(1)}, bf16[128,256]{1,0:T(8,128)(2,1)S(1)}, u32[]{:S(2)}, u32[]{:S(2)}) collective-permute-start(bf16[128,256]{1,0:T(8,128)(2,1)S(1)} %fusion.5), channel_id=1, source_target_pairs={{0,2},{1,3},{2,0},{3,1},{4,6},{5,7},{6,4},{7,5},{8,10},{9,11},{10,... | collective-permute-start | bytes 196616 | tf_op jit(solution)/shard_map/ppermute | solution.py:229
  16.7 6.8 %collective-permute-start.16 = (bf16[128,256]{1,0:T(8,128)(2,1)S(1)}, bf16[128,256]{1,0:T(8,128)(2,1)S(1)}, u32[]{:S(2)}, u32[]{:S(2)}) collective-permute-start(bf16[128,256]{1,0:T(8,128)(2,1)S(1)} %fusion.3), channel_id=1, source_target_pairs={{0,12},{1,13},{2,14},{3,15},{4,8},{5,9},{6,10},{7,11},{8,4},{9,5},... | collective-permute-start | bytes 196616 | tf_op jit(solution)/shard_map/ppermute | solution.py:234
  20.7 5.4 %collective-permute-start.15 = (bf16[128,256]{1,0:T(8,128)(2,1)S(1)}, bf16[128,256]{1,0:T(8,128)(2,1)S(1)}, u32[]{:S(2)}, u32[]{:S(2)}) collective-permute-start(bf16[128,256]{1,0:T(8,128)(2,1)S(1)} %fusion.3), channel_id=1, source_target_pairs={{0,8},{1,9},{2,10},{3,11},{4,12},{5,13},{6,14},{7,15},{8,0},{9,1},... | collective-permute-start | bytes 196616 | tf_op jit(solution)/shard_map/ppermute | solution.py:234
  20.7 5.4 %collective-permute-start.14 = (bf16[128,256]{1,0:T(8,128)(2,1)S(1)}, bf16[128,256]{1,0:T(8,128)(2,1)S(1)}, u32[]{:S(2)}, u32[]{:S(2)}) collective-permute-start(bf16[128,256]{1,0:T(8,128)(2,1)S(1)} %fusion.3), channel_id=1, source_target_pairs={{0,4},{1,5},{2,6},{3,7},{4,0},{5,1},{6,2},{7,3},{8,12},{9,13},{10,... | collective-permute-start | bytes 196616 | tf_op jit(solution)/shard_map/ppermute | solution.py:234
  26.2 4.3 %collective-permute-start.17 = (bf16[128,256]{1,0:T(8,128)(2,1)S(1)}, bf16[128,256]{1,0:T(8,128)(2,1)S(1)}, u32[]{:S(2)}, u32[]{:S(2)}) collective-permute-start(bf16[128,256]{1,0:T(8,128)(2,1)S(1)} %multiply_convert_fusion.r00), channel_id=1, source_target_pairs={{0,2},{1,3},{2,0},{3,1},{4,6},{5,7},{6,4},{7,5},{8,10},{9,11},{10,... | collective-permute-start | bytes 196616 | tf_op jit(solution)/shard_map/ppermute | solution.py:236
  27.8 4.3 %collective-permute-start.1 = (bf16[128,256]{1,0:T(8,128)(2,1)S(1)}, bf16[128,256]{1,0:T(8,128)(2,1)S(1)}, u32[]{:S(2)}, u32[]{:S(2)}) collective-permute-start(bf16[128,256]{1,0:T(8,128)(2,1)S(1)} %fusion.4), channel_id=1, source_target_pairs={{0,2},{1,3},{2,0},{3,1},{4,6},{5,7},{6,4},{7,5},{8,10},{9,11},{10,... | collective-permute-start | bytes 196616 | tf_op jit(solution)/shard_map/ppermute | solution.py:229
  28.4 8.2 %collective-permute-start.18 = (bf16[128,256]{1,0:T(8,128)(2,1)S(1)}, bf16[128,256]{1,0:T(8,128)(2,1)S(1)}, u32[]{:S(2)}, u32[]{:S(2)}) collective-permute-start(bf16[128,256]{1,0:T(8,128)(2,1)S(1)} %multiply_convert_fusion.r00), channel_id=1, source_target_pairs={{0,1},{1,0},{2,3},{3,2},{4,5},{5,4},{6,7},{7,6},{8,9},{9,8},{10,11... | collective-permute-start | bytes 196616 | tf_op jit(solution)/shard_map/ppermute | solution.py:237
  30.5 6.0 %collective-permute-start.19 = (bf16[128,256]{1,0:T(8,128)(2,1)S(1)}, bf16[128,256]{1,0:T(8,128)(2,1)S(1)}, u32[]{:S(2)}, u32[]{:S(2)}) collective-permute-start(bf16[128,256]{1,0:T(8,128)(2,1)S(1)} %collective-permute-done.17.r01), channel_id=1, source_target_pairs={{0,1},{1,0},{2,3},{3,2},{4,5},{5,4},{6,7},{7,6},{8,9},{9,8},{10,11... | collective-permute-start | bytes 196616 | tf_op jit(solution)/shard_map/ppermute | solution.py:238
  32.1 10.5 %collective-permute-start.4 = (bf16[128,256]{1,0:T(8,128)(2,1)S(1)}, bf16[128,256]{1,0:T(8,128)(2,1)S(1)}, u32[]{:S(2)}, u32[]{:S(2)}) collective-permute-start(bf16[128,256]{1,0:T(8,128)(2,1)S(1)} %fusion.2), channel_id=1, source_target_pairs={{0,12},{1,13},{2,14},{3,15},{4,8},{5,9},{6,10},{7,11},{8,4},{9,5},... | collective-permute-start | bytes 196616 | tf_op jit(solution)/shard_map/ppermute | solution.py:234
  34.4 9.8 %collective-permute-start.3 = (bf16[128,256]{1,0:T(8,128)(2,1)S(1)}, bf16[128,256]{1,0:T(8,128)(2,1)S(1)}, u32[]{:S(2)}, u32[]{:S(2)}) collective-permute-start(bf16[128,256]{1,0:T(8,128)(2,1)S(1)} %fusion.2), channel_id=1, source_target_pairs={{0,8},{1,9},{2,10},{3,11},{4,12},{5,13},{6,14},{7,15},{8,0},{9,1},... | collective-permute-start | bytes 196616 | tf_op jit(solution)/shard_map/ppermute | solution.py:234
  34.4 9.8 %collective-permute-start.2 = (bf16[128,256]{1,0:T(8,128)(2,1)S(1)}, bf16[128,256]{1,0:T(8,128)(2,1)S(1)}, u32[]{:S(2)}, u32[]{:S(2)}) collective-permute-start(bf16[128,256]{1,0:T(8,128)(2,1)S(1)} %fusion.2), channel_id=1, source_target_pairs={{0,4},{1,5},{2,6},{3,7},{4,0},{5,1},{6,2},{7,3},{8,12},{9,13},{10,... | collective-permute-start | bytes 196616 | tf_op jit(solution)/shard_map/ppermute | solution.py:234
  37.9 20.6 %collective-permute-start.21 = (bf16[2,128,512]{2,1,0:T(8,128)(2,1)S(1)}, bf16[2,128,512]{2,1,0:T(8,128)(2,1)S(1)}, u32[]{:S(2)}, u32[]{:S(2)}) collective-permute-start(bf16[2,128,512]{2,1,0:T(8,128)(2,1)S(1)} %adjoint.13.refs_0_), channel_id=1, source_target_pairs={{0,16},{16,0},{1,17},{17,1},{2,18},{18,2},{3,19},{19,3},{4,20},{20... | collective-permute-start | bytes 786440 | tf_op jit(solution)/shard_map/ppermute | solution.py:250
  40.7 18.4 %collective-permute-start.22 = (bf16[2,128,512]{2,1,0:T(8,128)(2,1)S(1)}, bf16[2,128,512]{2,1,0:T(8,128)(2,1)S(1)}, u32[]{:S(2)}, u32[]{:S(2)}) collective-permute-start(bf16[2,128,512]{2,1,0:T(8,128)(2,1)S(1)} %adjoint.14.refs_0_), channel_id=1, source_target_pairs={{0,16},{16,0},{1,17},{17,1},{2,18},{18,2},{3,19},{19,3},{4,20},{20... | collective-permute-start | bytes 786440 | tf_op jit(solution)/shard_map/ppermute | solution.py:250
  42.6 17.9 %collective-permute-start.23 = (bf16[2,128,512]{2,1,0:T(8,128)(2,1)S(1)}, bf16[2,128,512]{2,1,0:T(8,128)(2,1)S(1)}, u32[]{:S(2)}, u32[]{:S(2)}) collective-permute-start(bf16[2,128,512]{2,1,0:T(8,128)(2,1)S(1)} %adjoint.15.refs_0_), channel_id=1, source_target_pairs={{0,16},{16,0},{1,17},{17,1},{2,18},{18,2},{3,19},{19,3},{4,20},{20... | collective-permute-start | bytes 786440 | tf_op jit(solution)/shard_map/ppermute | solution.py:250
  44.3 4.3 %collective-permute-start.5 = (bf16[128,256]{1,0:T(8,128)(2,1)S(1)}, bf16[128,256]{1,0:T(8,128)(2,1)S(1)}, u32[]{:S(2)}, u32[]{:S(2)}) collective-permute-start(bf16[128,256]{1,0:T(8,128)(2,1)S(1)} %multiply_convert_fusion.1.r00), channel_id=1, source_target_pairs={{0,2},{1,3},{2,0},{3,1},{4,6},{5,7},{6,4},{7,5},{8,10},{9,11},{10,... | collective-permute-start | bytes 196616 | tf_op jit(solution)/shard_map/ppermute | solution.py:236
  45.0 3.7 %collective-permute-start.6 = (bf16[128,256]{1,0:T(8,128)(2,1)S(1)}, bf16[128,256]{1,0:T(8,128)(2,1)S(1)}, u32[]{:S(2)}, u32[]{:S(2)}) collective-permute-start(bf16[128,256]{1,0:T(8,128)(2,1)S(1)} %multiply_convert_fusion.1.r00), channel_id=1, source_target_pairs={{0,1},{1,0},{2,3},{3,2},{4,5},{5,4},{6,7},{7,6},{8,9},{9,8},{10,11... | collective-permute-start | bytes 196616 | tf_op jit(solution)/shard_map/ppermute | solution.py:237
  48.6 1.3 %collective-permute-start.7 = (bf16[128,256]{1,0:T(8,128)(2,1)S(1)}, bf16[128,256]{1,0:T(8,128)(2,1)S(1)}, u32[]{:S(2)}, u32[]{:S(2)}) collective-permute-start(bf16[128,256]{1,0:T(8,128)(2,1)S(1)} %collective-permute-done.5.r01), channel_id=1, source_target_pairs={{0,1},{1,0},{2,3},{3,2},{4,5},{5,4},{6,7},{7,6},{8,9},{9,8},{10,11... | collective-permute-start | bytes 196616 | tf_op jit(solution)/shard_map/ppermute | solution.py:238
  51.2 17.9 %collective-permute-start.11 = (bf16[2,128,512]{2,1,0:T(8,128)(2,1)S(1)}, bf16[2,128,512]{2,1,0:T(8,128)(2,1)S(1)}, u32[]{:S(2)}, u32[]{:S(2)}) collective-permute-start(bf16[2,128,512]{2,1,0:T(8,128)(2,1)S(1)} %adjoint.11.refs_0_), channel_id=1, source_target_pairs={{0,16},{16,0},{1,17},{17,1},{2,18},{18,2},{3,19},{19,3},{4,20},{20... | collective-permute-start | bytes 786440 | tf_op jit(solution)/shard_map/ppermute | solution.py:250
  53.1 15.1 %collective-permute-start.20 = (bf16[2,128,512]{2,1,0:T(8,128)(2,1)S(1)}, bf16[2,128,512]{2,1,0:T(8,128)(2,1)S(1)}, u32[]{:S(2)}, u32[]{:S(2)}) collective-permute-start(bf16[2,128,512]{2,1,0:T(8,128)(2,1)S(1)} %adjoint.12.refs_0_), channel_id=1, source_target_pairs={{0,16},{16,0},{1,17},{17,1},{2,18},{18,2},{3,19},{19,3},{4,20},{20... | collective-permute-start | bytes 786440 | tf_op jit(solution)/shard_map/ppermute | solution.py:250
  58.5 15.4 %collective-permute-start.10 = (bf16[2,128,512]{2,1,0:T(8,128)(2,1)S(1)}, bf16[2,128,512]{2,1,0:T(8,128)(2,1)S(1)}, u32[]{:S(2)}, u32[]{:S(2)}) collective-permute-start(bf16[2,128,512]{2,1,0:T(8,128)(2,1)S(1)} %adjoint.10.refs_0_), channel_id=1, source_target_pairs={{0,16},{16,0},{1,17},{17,1},{2,18},{18,2},{3,19},{19,3},{4,20},{20... | collective-permute-start | bytes 786440 | tf_op jit(solution)/shard_map/ppermute | solution.py:250
  59.1 20.4 %collective-permute-start.9 = (bf16[2,128,512]{2,1,0:T(8,128)(2,1)S(1)}, bf16[2,128,512]{2,1,0:T(8,128)(2,1)S(1)}, u32[]{:S(2)}, u32[]{:S(2)}) collective-permute-start(bf16[2,128,512]{2,1,0:T(8,128)(2,1)S(1)} %adjoint.9.refs_0_), channel_id=1, source_target_pairs={{0,16},{16,0},{1,17},{17,1},{2,18},{18,2},{3,19},{19,3},{4,20},{20... | collective-permute-start | bytes 786440 | tf_op jit(solution)/shard_map/ppermute | solution.py:250
  60.6 23.0 %collective-permute-start.8 = (bf16[2,128,512]{2,1,0:T(8,128)(2,1)S(1)}, bf16[2,128,512]{2,1,0:T(8,128)(2,1)S(1)}, u32[]{:S(2)}, u32[]{:S(2)}) collective-permute-start(bf16[2,128,512]{2,1,0:T(8,128)(2,1)S(1)} %adjoint.8.refs_0_), channel_id=1, source_target_pairs={{0,16},{16,0},{1,17},{17,1},{2,18},{18,2},{3,19},{19,3},{4,20},{20... | collective-permute-start | bytes 786440 | tf_op jit(solution)/shard_map/ppermute | solution.py:250

commit v2 on v1

--- a/solution.py
+++ b/solution.py
@@ -12,7 +12,7 @@
 BF = jnp.bfloat16
 F32 = jnp.float32
 CUTS = (128, 128)
-GROUPS = (4, 4)
+GROUPS = ((2, 3, 3), (4, 3, 1))
 VMEM_LIMIT = 26 * 2**20
 IN_VMEM = pl.BlockSpec(memory_space=pltpu.VMEM)
 IN_SMEM = pl.BlockSpec(memory_space=pltpu.SMEM)
@@ -33,11 +33,16 @@
     )
 
 
-def forward_kernel(dims, ranks, me, obs, x_hbm, u_hbm, v_hbm, *rest):
+def position():
+    col = lax.axis_index("col")
+    return lax.rem(col, 2), lax.rem(lax.div(col, 2), 2), lax.div(col, 4)
+
+
+def forward_kernel(dims, ranks, obs, x_hbm, u_hbm, v_hbm, *rest):
     tile_rows, tile_cols, width, cap, sources, rb, zs, cuts = dims
     n = len(cuts)
     keep_refs, send_refs = rest[:n], rest[n : 2 * n]
-    u_vm, v_vm, x_vm, acc, sems = rest[2 * n :]
+    x_vm, u_vm, v_vm, acc, sems = rest[2 * n :]
 
     def copies(j):
         span = pl.ds(j * width, width)
@@ -51,21 +56,25 @@
         for c in copies(j):
             c.start()
 
-    mine, my_x, my_z = me[0], me[1], me[2]
+    mine, my_x, my_z = position()
     lane = lax.broadcasted_iota(jnp.int32, (sources, cap), 1)
-    acc[...] = jnp.zeros_like(acc)
-
-    def body(j, carry):
-        for c in copies(j):
-            c.wait()
-        xt = x_vm[pl.ds(pl.multiple_of(j * width, width), width), :].T
+    jb = 2 if tile_cols % 2 == 0 else 1
+    for j0 in range(0, tile_cols, jb):
+        parts = [[] for _ in range(tile_rows)]
+        for j in range(j0, j0 + jb):
+            for c in copies(j):
+                c.wait()
+            xt = x_vm[j * width : (j + 1) * width, :].T
+            for a in range(tile_rows):
+                c = dot_nn(xt, v_vm[a, j])
+                parts[a].append(jnp.where(lane < ranks[a, j], c, 0.0).astype(BF))
         for a in range(tile_rows):
-            c = dot_nn(xt, v_vm[a, j])
-            c = jnp.where(lane < ranks[a * tile_cols + j], c, 0.0).astype(BF)
-            acc[a] += dot_nt(c, permuted_rows(u_vm[a, j], zs, rb))
-        return carry
-
-    lax.fori_loop(0, tile_cols, body, 0)
+            w = jnp.concatenate([permuted_rows(u_vm[a, j], zs, rb) for j in range(j0, j0 + jb)], axis=1)
+            p = dot_nt(jnp.concatenate(parts[a], axis=1), w)
+            if j0 == 0:
+                acc[a] = p
+            else:
+                acc[a] += p
 
     nz = zs * tile_rows
     q_lanes = width // 4
@@ -94,21 +103,22 @@
             row += s
 
 
-def forward(x, obs, u, v, ranks, me, cuts, zs):
+def forward(x, obs, u, v, ranks, cuts, zs):
     tile_rows, tile_cols, width, cap = u.shape
     sources = x.shape[1]
     rb = obs.shape[0]
     block = tile_rows * width // 4
     dims = (tile_rows, tile_cols, width, cap, sources, rb, zs, cuts)
     outs = [pltpu.VMEM((2, s, block), F32) for s in cuts] + [pltpu.VMEM((2, s, block), BF) for s in cuts]
-    outs += [pltpu.VMEM(u.shape, BF), pltpu.VMEM(v.shape, BF)]
     room = 2**20 + sum(math.prod(o.shape) * o.dtype.itemsize for o in outs)
     res = pl.pallas_call(
         functools.partial(forward_kernel, dims),
-        in_specs=[IN_SMEM, IN_SMEM, IN_VMEM, IN_HBM, IN_HBM, IN_HBM],
+        in_specs=[IN_SMEM, IN_VMEM, IN_HBM, IN_HBM, IN_HBM],
         out_specs=[IN_VMEM] * len(outs),
         scratch_shapes=[
             pltpu.VMEM(x.shape, BF),
+            pltpu.VMEM(u.shape, BF),
+            pltpu.VMEM(v.shape, BF),
             pltpu.VMEM((tile_rows, sources, width), F32),
             pltpu.SemaphoreType.DMA((tile_cols, 1 + 2 * tile_rows)),
         ],
@@ -120,14 +130,35 @@
             transcendentals=0,
         ),
         name="forward",
-    )(ranks.reshape(-1), me, obs, x, u, v)
+    )(ranks, obs, x, u, v)
     n = len(cuts)
-    return res[:n], res[n : 2 * n], res[2 * n], res[2 * n + 1]
-
-
-def adjoint_kernel(dims, ranks, me, r00, r01, r10, r11, u_ref, v_ref, g_ref, held):
-    tile_rows, tile_cols, start, count, width, cap, s, rb, zs = dims
-    base = me[1] * 2 + me[0]
+    return res[:n], res[n:]
+
+
+def hold_kernel(src, dst, sem):
+    copy = pltpu.make_async_copy(src, dst, sem)
+    copy.start()
+    copy.wait()
+
+
+def hold(array, before):
+    room = before + 2 * array.size + 3 * 2**20
+    return pl.pallas_call(
+        hold_kernel,
+        in_specs=[IN_HBM],
+        out_specs=pl.BlockSpec(memory_space=pl.ANY),
+        out_shape=pltpu.VMEM(array.shape, array.dtype),
+        scratch_shapes=[pltpu.SemaphoreType.DMA],
+        compiler_params=pltpu.CompilerParams(vmem_limit_bytes=63 * 2**20 - room),
+        cost_estimate=pl.CostEstimate(flops=0, bytes_accessed=2 * array.size, transcendentals=0),
+        name="hold",
+    )(array)
+
+
+def adjoint_kernel(dims, ranks, r00, r01, r10, r11, u_ref, v_ref, g_ref, held):
+    tile_rows, _, start, count, width, cap, s, rb, zs = dims
+    mine, my_x, _ = position()
+    base = my_x * 2 + mine
     held[base] = r00[...]
     held[base ^ 2] = r01[...]
     held[base ^ 1] = r10[...]
@@ -142,19 +173,19 @@
         total = None
         for a in range(tile_rows):
             adj = dot_nn(r[a], permuted_rows(u_ref[a, start + j], zs, rb))
-            adj = jnp.where(lane < ranks[a * tile_cols + start + j], adj, 0.0).astype(BF)
+            adj = jnp.where(lane < ranks[a, start + j], adj, 0.0).astype(BF)
             g = dot_nt(adj, v_ref[a, start + j])
             total = g if total is None else total + g
         g_ref[j] = total.astype(BF)
 
 
-def adjoint(rs, u, v, ranks, me, start, count, rb, zs):
+def adjoint(rs, u, v, ranks, start, count, rb, zs):
     tile_rows, tile_cols, width, cap = u.shape
     s, block = rs[0].shape
     dims = (tile_rows, tile_cols, start, count, width, cap, s, rb, zs)
     return pl.pallas_call(
         functools.partial(adjoint_kernel, dims),
-        in_specs=[IN_SMEM, IN_SMEM] + [IN_VMEM] * 6,
+        in_specs=[IN_SMEM] + [IN_VMEM] * 6,
         out_specs=IN_VMEM,
         scratch_shapes=[pltpu.VMEM((4, s, block), BF)],
         out_shape=jax.ShapeDtypeStruct((count, s, width), BF),
@@ -163,7 +194,7 @@
             flops=4 * tile_rows * count * width * cap * s, bytes_accessed=4 * s * block, transcendentals=0
         ),
         name="adjoint",
-    )(ranks.reshape(-1), me, *rs, u, v)
+    )(ranks, *rs, u, v)
 
 
 def finish_kernel(n, *refs):
@@ -218,10 +249,10 @@
         rb = observed.shape[0]
         zs = nz // tile_rows
         cuts = tuple(c * sources // 256 for c in CUTS)
-        me_col = lax.axis_index("col")
-        me = jnp.stack([me_col % 2, (me_col // 2) % 2, me_col // 4]).astype(jnp.int32)
         sat = sat_scale[:, None]
-        keeps, sends, u, v = forward(x_field, observed, u, v, ranks, me, cuts, zs)
+        keeps, sends = forward(x_field, observed, u, v, ranks, cuts, zs)
+        u = hold(u, 0)
+        v = hold(v, 2 * u.size)
 
         def residual(send, keep, sc):
             got = lax.ppermute(send, "col", core_swap)
@@ -243,9 +274,11 @@
         for i, s in enumerate(cuts):
             resid = residual(sends[i], keeps[i], sat[row : row + s])
             row += s
-            per = tile_cols // GROUPS[i]
-            for g in range(GROUPS[i]):
-                part = adjoint(resid, u, v, ranks, me, g * per, per, rb, zs)
+            start = 0
+            for g, share in enumerate(GROUPS[i]):
+                per = share * tile_cols // 8
+                part = adjoint(resid, u, v, ranks, start, per, rb, zs)
+                start += per
                 if n_row == 2:
                     swapped[i, g] = (part, lax.ppermute(part, "row", row_swap))
                 else:
@@ -253,17 +286,12 @@
                     swapped[i, g] = (whole, jnp.zeros_like(whole))
         out = None
         lane = 0
-        i = 0
-        while i < len(cuts):
-            ids, lanes = [i], cuts[i]
-            while lanes % 128 != 0:
-                ids.append(ids[-1] + 1)
-                lanes += cuts[ids[-1]]
-            per = tile_cols // GROUPS[i]
-            for g in range(GROUPS[i]):
-                out = finish(out, [swapped[k, g] for k in ids], g * per, lane // lanes, rows, sources)
-            lane += lanes
-            i = ids[-1] + 1
+        for i, s in enumerate(cuts):
+            start = 0
+            for g, share in enumerate(GROUPS[i]):
+                out = finish(out, [swapped[i, g]], start, lane // s, rows, sources)
+                start += share * tile_cols // 8
+            lane += s
         return out
 
     return jax.shard_map(

time: 84.6 us -> 92.9 us (1.098)
  waiting for transfers between devices: 32.9 us -> 41.9 us
  Pallas kernels: 25 us -> 27.2 us
  local copies, waits for them, and re-layouts: 1.3 us -> 0.03 us
    ppermute x8 -> x6, waiting for transfers between devices: 16.3 us -> 32.3 us  [local(): swapped[i, g] = (part, lax.ppermute(part, 'row', row_swap))]
    ppermute x2, waiting for transfers between devices: 5.81 us -> 1.38 us  [residual(): r01 = lax.ppermute(r00, 'col', x_swap)]
    pallas_call x0 -> x2, Pallas kernels: none -> 4.4 us  [hold(): pl.pallas_call(hold_kernel, in_specs=[IN_HBM], out_specs=pl.BlockSpec(mem...]
    ppermute x2, waiting for transfers between devices: 3.96 us -> 2.22 us  [residual(): got = lax.ppermute(half[1].astype(BF), 'col', x_swap)]
    pallas_call x1, Pallas kernels: 7.78 us -> 6.08 us  [forward(): pl.pallas_call(functools.partial(forward_kernel, dims), in_specs=[IN_SMEM...]
    pallas_call x8 -> x6, Pallas kernels: 10.2 us -> 8.85 us  [adjoint(): pl.pallas_call(functools.partial(adjoint_kernel, dims), in_specs=[IN_SMEM...]
    reshape x1 -> x0, local copies, waits for them, and re-layouts: 1.27 us -> none  [adjoint(): ranks.reshape(-1)]
    ppermute x2, waiting for transfers between devices: 1.25 us -> 0.01 us  [residual(): r11 = lax.ppermute(r01, 'col', core_swap)]
  transfers between devices with their start and end apart: 24 -> 22, of which waited for: 12 -> 6; matrix products, arithmetic and copies ran while one was open for 0% -> 0% of each run, Pallas kernels for 19% -> 22%
where the time goes in v2:
time: 92.9 us; the launch traced here: 92.7 us
  waiting for transfers between devices  41.9 us (45%)
  Pallas kernels  27.2 us (29%)
  starting transfers between devices  23.1 us (25%)
    ppermute x6, waiting for transfers between devices, local(): swapped[i, g] = (part, lax.ppermute(part, 'row', row_swap))  32.3 us
    ppermute x6, starting transfers between devices, residual(): total = total + lax.ppermute(mine, 'col', p).astype(F32)  9.32 us
    pallas_call x6, Pallas kernels, adjoint(): pl.pallas_call(functools.partial(adjoint_kernel, dims), in_specs=[IN_SMEM...  8.85 us
    pallas_call x6, Pallas kernels, finish(): pl.pallas_call(body, grid=(count,), in_specs=specs, out_specs=pl.BlockSpe...  7.84 us
    ppermute x6, starting transfers between devices, local(): swapped[i, g] = (part, lax.ppermute(part, 'row', row_swap))  7.42 us
    pallas_call x1, Pallas kernels, forward(): pl.pallas_call(functools.partial(forward_kernel, dims), in_specs=[IN_SMEM...  6.08 us
    ppermute x6, waiting for transfers between devices, residual(): total = total + lax.ppermute(mine, 'col', p).astype(F32)  5.11 us
    pallas_call x2, Pallas kernels, hold(): pl.pallas_call(hold_kernel, in_specs=[IN_HBM], out_specs=pl.BlockSpec(mem...  4.4 us
  transfers between devices with their start and end apart: 22, of which 6 were waited for; matrix products, arithmetic and copies ran while one was open for 0% of the time, Pallas kernels for 22%

profile of v2, /device:TPU:0, one launch (start us, length us, event | category | flops | bytes accessed | tf_op | source)
XLA Modules:
  0.0 92.7 jit_solution(15787918744981652750)
XLA Ops:
  0.0 6.1 %forward.1 = (f32[2,128,256]{2,1,0:T(8,128)S(1)}, f32[2,128,256]{2,1,0:T(8,128)S(1)}, bf16[2,128,256]{2,1,0:T(8,128)(2,1)S(1)}, bf16[2,128,256]{2,1,0:T(8,128)(2,1)S(1)}) custom-call(s32[2,8]{1,0:T(2,128)} %ranks.13, bf16[64,256]{1,0:T(8,128)(2,1)} %obs.1, bf16[4096,256]{1,0:T(8,128)(2,1)} %x_hbm.1, bf16[2,8,512,256]{3,2,1,0:T(8,128)(2,1)} %src.2, ...), custom_call_target="tpu_custom_call" | custom-call | flops 2147483648 | bytes 10485760 | tf_op jit(solution)/shard_map/forward/pallas_call | solution.py:114
  6.7 0.9 collective-permute-done
  7.7 2.9 %collective-permute-start.1 = (bf16[128,256]{1,0:T(8,128)(2,1)S(1)}, bf16[128,256]{1,0:T(8,128)(2,1)S(1)}, u32[]{:S(2)}, u32[]{:S(2)}) collective-permute-start(bf16[128,256]{1,0:T(8,128)(2,1)S(1)} %fusion.4), channel_id=1, source_target_pairs={{0,2},{1,3},{2,0},{3,1},{4,6},{5,7},{6,4},{7,5},{8,10},{9,11},{10,... | collective-permute-start | bytes 196616 | tf_op jit(solution)/shard_map/ppermute | solution.py:260
  10.8 2.2 %collective-permute-done.1 = bf16[128,256]{1,0:T(8,128)(2,1)S(1)} collective-permute-done((bf16[128,256]{1,0:T(8,128)(2,1)S(1)}, bf16[128,256]{1,0:T(8,128)(2,1)S(1)}, u32[]{:S(2)}, u32[]{:S(2)}) %collective-permute-start.1) | collective-permute-done | bytes 65568 | tf_op jit(solution)/shard_map/ppermute | solution.py:260
  13.0 4.2 %collective-permute-start.4 = (bf16[128,256]{1,0:T(8,128)(2,1)S(1)}, bf16[128,256]{1,0:T(8,128)(2,1)S(1)}, u32[]{:S(2)}, u32[]{:S(2)}) collective-permute-start(bf16[128,256]{1,0:T(8,128)(2,1)S(1)} %fusion.2), channel_id=1, source_target_pairs={{0,12},{1,13},{2,14},{3,15},{4,8},{5,9},{6,10},{7,11},{8,4},{9,5},... | collective-permute-start | bytes 196616 | tf_op jit(solution)/shard_map/ppermute | solution.py:265
  17.2 0.6 collective-permute-start.2
  17.9 3.8 %collective-permute-start.15 = (bf16[128,256]{1,0:T(8,128)(2,1)S(1)}, bf16[128,256]{1,0:T(8,128)(2,1)S(1)}, u32[]{:S(2)}, u32[]{:S(2)}) collective-permute-start(bf16[128,256]{1,0:T(8,128)(2,1)S(1)} %fusion.3), channel_id=1, source_target_pairs={{0,12},{1,13},{2,14},{3,15},{4,8},{5,9},{6,10},{7,11},{8,4},{9,5},... | collective-permute-start | bytes 196616 | tf_op jit(solution)/shard_map/ppermute | solution.py:265
  21.7 0.6 collective-permute-start.13
  22.4 3.8 %collective-permute-done.3 = bf16[128,256]{1,0:T(8,128)(2,1)S(1)} collective-permute-done((bf16[128,256]{1,0:T(8,128)(2,1)S(1)}, bf16[128,256]{1,0:T(8,128)(2,1)S(1)}, u32[]{:S(2)}, u32[]{:S(2)}) %collective-permute-start.3) | collective-permute-done | bytes 65568 | tf_op jit(solution)/shard_map/ppermute | solution.py:265
  26.7 1.3 %collective-permute-done.14 = bf16[128,256]{1,0:T(8,128)(2,1)S(1)} collective-permute-done((bf16[128,256]{1,0:T(8,128)(2,1)S(1)}, bf16[128,256]{1,0:T(8,128)(2,1)S(1)}, u32[]{:S(2)}, u32[]{:S(2)}) %collective-permute-start.14) | collective-permute-done | bytes 65568 | tf_op jit(solution)/shard_map/ppermute | solution.py:265
  28.2 1.6 %collective-permute-start.16 = (bf16[128,256]{1,0:T(8,128)(2,1)S(1)}, bf16[128,256]{1,0:T(8,128)(2,1)S(1)}, u32[]{:S(2)}, u32[]{:S(2)}) collective-permute-start(bf16[128,256]{1,0:T(8,128)(2,1)S(1)} %multiply_convert_fusion.r00), channel_id=1, source_target_pairs={{0,2},{1,3},{2,0},{3,1},{4,6},{5,7},{6,4},{7,5},{8,10},{9,11},{10,... | collective-permute-start | bytes 196616 | tf_op jit(solution)/shard_map/ppermute | solution.py:267
  29.7 1.4 %collective-permute-done.5.r01 = bf16[128,256]{1,0:T(8,128)(2,1)S(1)} collective-permute-done((bf16[128,256]{1,0:T(8,128)(2,1)S(1)}, bf16[128,256]{1,0:T(8,128)(2,1)S(1)}, u32[]{:S(2)}, u32[]{:S(2)}) %collective-permute-start.5) | collective-permute-done | bytes 65568 | tf_op jit(solution)/shard_map/ppermute | solution.py:267
  31.1 2.2 %hold.2.u_ref = bf16[2,8,512,256]{3,2,1,0:T(8,128)(2,1)S(1)} custom-call(bf16[2,8,512,256]{3,2,1,0:T(8,128)(2,1)} %src.2), custom_call_target="tpu_custom_call" | custom-call | bytes 4194304 | tf_op jit(solution)/shard_map/hold/pallas_call | solution.py:146
  33.3 2.2 %hold.3.v_ref = bf16[2,8,512,256]{3,2,1,0:T(8,128)(2,1)S(1)} custom-call(bf16[2,8,512,256]{3,2,1,0:T(8,128)(2,1)} %src.3), custom_call_target="tpu_custom_call" | custom-call | bytes 4194304 | tf_op jit(solution)/shard_map/hold/pallas_call | solution.py:146
  35.6 0.6 collective-permute-start.17
  36.2 1.9 %adjoint.8.refs_0_ = bf16[4,128,512]{2,1,0:T(8,128)(2,1)S(1)} custom-call(s32[2,8]{1,0:T(2,128)S(1)} %copy-done, bf16[128,256]{1,0:T(8,128)(2,1)S(1)} %multiply_convert_fusion.1.r00, bf16[128,256]{1,0:T(8,128)(2,1)S(1)} %collective-permute-done.5.r01, bf16[128,256]{1,0:T(8,128)(2,1)S(1)} %collective-permute-done.6.r10, ...), custom_call_target="tpu_custom_call" | custom-call | flops 536870912 | bytes 131072 | tf_op jit(solution)/shard_map/adjoint/pallas_call | solution.py:186
  38.1 1.6 %collective-permute-start.10 = (bf16[4,128,512]{2,1,0:T(8,128)(2,1)S(1)}, bf16[4,128,512]{2,1,0:T(8,128)(2,1)S(1)}, u32[]{:S(2)}, u32[]{:S(2)}) collective-permute-start(bf16[4,128,512]{2,1,0:T(8,128)(2,1)S(1)} %adjoint.8.refs_0_), channel_id=1, source_target_pairs={{0,16},{16,0},{1,17},{17,1},{2,18},{18,2},{3,19},{19,3},{4,20},{20... | collective-permute-start | bytes 1572872 | tf_op jit(solution)/shard_map/ppermute | solution.py:283
  39.7 1.6 %adjoint.7.refs_0_ = bf16[3,128,512]{2,1,0:T(8,128)(2,1)S(1)} custom-call(s32[2,8]{1,0:T(2,128)S(1)} %copy-done, bf16[128,256]{1,0:T(8,128)(2,1)S(1)} %multiply_convert_fusion.1.r00, bf16[128,256]{1,0:T(8,128)(2,1)S(1)} %collective-permute-done.5.r01, bf16[128,256]{1,0:T(8,128)(2,1)S(1)} %collective-permute-done.6.r10, ...), custom_call_target="tpu_custom_call" | custom-call | flops 402653184 | bytes 131072 | tf_op jit(solution)/shard_map/adjoint/pallas_call | solution.py:186
  41.9 1.6 %adjoint.9.refs_0_ = bf16[3,128,512]{2,1,0:T(8,128)(2,1)S(1)} custom-call(s32[2,8]{1,0:T(2,128)S(1)} %copy-done, bf16[128,256]{1,0:T(8,128)(2,1)S(1)} %multiply_convert_fusion.r00, bf16[128,256]{1,0:T(8,128)(2,1)S(1)} %collective-permute-done.16.r01, bf16[128,256]{1,0:T(8,128)(2,1)S(1)} %collective-permute-done.17.r10, ...), custom_call_target="tpu_custom_call" | custom-call | flops 402653184 | bytes 131072 | tf_op jit(solution)/shard_map/adjoint/pallas_call | solution.py:186
  43.4 1.6 %collective-permute-start.19 = (bf16[3,128,512]{2,1,0:T(8,128)(2,1)S(1)}, bf16[3,128,512]{2,1,0:T(8,128)(2,1)S(1)}, u32[]{:S(2)}, u32[]{:S(2)}) collective-permute-start(bf16[3,128,512]{2,1,0:T(8,128)(2,1)S(1)} %adjoint.9.refs_0_), channel_id=1, source_target_pairs={{0,16},{16,0},{1,17},{17,1},{2,18},{18,2},{3,19},{19,3},{4,20},{20... | collective-permute-start | bytes 1179656 | tf_op jit(solution)/shard_map/ppermute | solution.py:283
  45.0 1.6 %adjoint.10.refs_0_ = bf16[3,128,512]{2,1,0:T(8,128)(2,1)S(1)} custom-call(s32[2,8]{1,0:T(2,128)S(1)} %copy-done, bf16[128,256]{1,0:T(8,128)(2,1)S(1)} %multiply_convert_fusion.r00, bf16[128,256]{1,0:T(8,128)(2,1)S(1)} %collective-permute-done.16.r01, bf16[128,256]{1,0:T(8,128)(2,1)S(1)} %collective-permute-done.17.r10, ...), custom_call_target="tpu_custom_call" | custom-call | flops 402653184 | bytes 131072 | tf_op jit(solution)/shard_map/adjoint/pallas_call | solution.py:186
  47.2 1.3 %adjoint.11.refs_0_ = bf16[2,128,512]{2,1,0:T(8,128)(2,1)S(1)} custom-call(s32[2,8]{1,0:T(2,128)S(1)} %copy-done, bf16[128,256]{1,0:T(8,128)(2,1)S(1)} %multiply_convert_fusion.r00, bf16[128,256]{1,0:T(8,128)(2,1)S(1)} %collective-permute-done.16.r01, bf16[128,256]{1,0:T(8,128)(2,1)S(1)} %collective-permute-done.17.r10, ...), custom_call_target="tpu_custom_call" | custom-call | flops 268435456 | bytes 131072 | tf_op jit(solution)/shard_map/adjoint/pallas_call | solution.py:186
  48.5 1.6 %collective-permute-start.21 = (bf16[2,128,512]{2,1,0:T(8,128)(2,1)S(1)}, bf16[2,128,512]{2,1,0:T(8,128)(2,1)S(1)}, u32[]{:S(2)}, u32[]{:S(2)}) collective-permute-start(bf16[2,128,512]{2,1,0:T(8,128)(2,1)S(1)} %adjoint.11.refs_0_), channel_id=1, source_target_pairs={{0,16},{16,0},{1,17},{17,1},{2,18},{18,2},{3,19},{19,3},{4,20},{20... | collective-permute-start | bytes 786440 | tf_op jit(solution)/shard_map/ppermute | solution.py:283
  50.0 1.0 %adjoint.6.refs_0_ = bf16[1,128,512]{2,1,0:T(8,128)(2,1)S(1)} custom-call(s32[2,8]{1,0:T(2,128)S(1)} %copy-done, bf16[128,256]{1,0:T(8,128)(2,1)S(1)} %multiply_convert_fusion.1.r00, bf16[128,256]{1,0:T(8,128)(2,1)S(1)} %collective-permute-done.5.r01, bf16[128,256]{1,0:T(8,128)(2,1)S(1)} %collective-permute-done.6.r10, ...), custom_call_target="tpu_custom_call" | custom-call | flops 134217728 | bytes 131072 | tf_op jit(solution)/shard_map/adjoint/pallas_call | solution.py:186
  51.0 32.3 %collective-permute-done.21.refs_1_ = bf16[2,128,512]{2,1,0:T(8,128)(2,1)S(1)} collective-permute-done((bf16[2,128,512]{2,1,0:T(8,128)(2,1)S(1)}, bf16[2,128,512]{2,1,0:T(8,128)(2,1)S(1)}, u32[]{:S(2)}, u32[]{:S(2)}) %collective-permute-start.21) | collective-permute-done | bytes 262176 | tf_op jit(solution)/shard_map/ppermute | solution.py:283
  83.3 1.5 %collective-permute-start.8 = (bf16[1,128,512]{2,1,0:T(8,128)(2,1)S(1)}, bf16[1,128,512]{2,1,0:T(8,128)(2,1)S(1)}, u32[]{:S(2)}, u32[]{:S(2)}) collective-permute-start(bf16[1,128,512]{2,1,0:T(8,128)(2,1)S(1)} %adjoint.6.refs_0_), channel_id=1, source_target_pairs={{0,16},{16,0},{1,17},{17,1},{2,18},{18,2},{3,19},{19,3},{4,20},{20... | collective-permute-start | bytes 393224 | tf_op jit(solution)/shard_map/ppermute | solution.py:283
  84.8 0.9 finish.6.refs_2_
  85.7 1.5 %finish.7.refs_2_ = bf16[4096,256]{1,0:T(8,128)(2,1)} custom-call(bf16[3,128,512]{2,1,0:T(8,128)(2,1)S(1)} %adjoint.10.refs_0_, bf16[3,128,512]{2,1,0:T(8,128)(2,1)S(1)} %collective-permute-done.20.refs_1_, bf16[4096,256]{1,0:T(8,128)(2,1)} %finish.6.refs_2_), custom_call_target="tpu_custom_call", output_to_operand_aliasing={{}: (2, {})} | custom-call | bytes 393216 | tf_op jit(solution)/shard_map/finish/pallas_call | solution.py:224
  87.3 1.5 %finish.8.refs_2_ = bf16[4096,256]{1,0:T(8,128)(2,1)} custom-call(bf16[3,128,512]{2,1,0:T(8,128)(2,1)S(1)} %adjoint.9.refs_0_, bf16[3,128,512]{2,1,0:T(8,128)(2,1)S(1)} %collective-permute-done.19.refs_1_, bf16[4096,256]{1,0:T(8,128)(2,1)} %finish.7.refs_2_), custom_call_target="tpu_custom_call", output_to_operand_aliasing={{}: (2, {})} | custom-call | bytes 393216 | tf_op jit(solution)/shard_map/finish/pallas_call | solution.py:224
  88.8 1.6 %finish.9.refs_2_ = bf16[4096,256]{1,0:T(8,128)(2,1)} custom-call(bf16[4,128,512]{2,1,0:T(8,128)(2,1)S(1)} %adjoint.8.refs_0_, bf16[4,128,512]{2,1,0:T(8,128)(2,1)S(1)} %collective-permute-done.10.refs_1_, bf16[4096,256]{1,0:T(8,128)(2,1)} %finish.8.refs_2_), custom_call_target="tpu_custom_call", output_to_operand_aliasing={{}: (2, {})} | custom-call | bytes 524288 | tf_op jit(solution)/shard_map/finish/pallas_call | solution.py:224
  90.4 1.5 %finish.10.refs_2_ = bf16[4096,256]{1,0:T(8,128)(2,1)} custom-call(bf16[3,128,512]{2,1,0:T(8,128)(2,1)S(1)} %adjoint.7.refs_0_, bf16[3,128,512]{2,1,0:T(8,128)(2,1)S(1)} %collective-permute-done.9.refs_1_, bf16[4096,256]{1,0:T(8,128)(2,1)} %finish.9.refs_2_), custom_call_target="tpu_custom_call", output_to_operand_aliasing={{}: (2, {})} | custom-call | bytes 393216 | tf_op jit(solution)/shard_map/finish/pallas_call | solution.py:224
  91.9 0.8 finish.11
  (40 shorter events, 2.8 us)
Async XLA Ops:
  0.0 6.7 %copy-start.1 = (f32[256]{0:T(256)S(1)}, f32[256]{0:T(256)}, u32[]{:S(2)}) copy-start(f32[256]{0:T(256)} %param.8) | copy-start | bytes 3076
  6.1 1.5 %collective-permute-start = (bf16[2,128,256]{2,1,0:T(8,128)(2,1)S(1)}, bf16[2,128,256]{2,1,0:T(8,128)(2,1)S(1)}, u32[]{:S(2)}, u32[]{:S(2)}) collective-permute-start(bf16[2,128,256]{2,1,0:T(8,128)(2,1)S(1)} %get-tuple-element.10), channel_id=1, source_target_pairs={{0,1},{1,0},{2,3},{3,2},{4,5},{5,4},{6,7},{7,6},{8,9},{9,8},{10,11... | collective-permute-start | bytes 393224 | tf_op jit(solution)/shard_map/ppermute | solution.py:258
  6.6 3.9 %collective-permute-start.11 = (bf16[2,128,256]{2,1,0:T(8,128)(2,1)S(1)}, bf16[2,128,256]{2,1,0:T(8,128)(2,1)S(1)}, u32[]{:S(2)}, u32[]{:S(2)}) collective-permute-start(bf16[2,128,256]{2,1,0:T(8,128)(2,1)S(1)} %get-tuple-element.12), channel_id=1, source_target_pairs={{0,1},{1,0},{2,3},{3,2},{4,5},{5,4},{6,7},{7,6},{8,9},{9,8},{10,11... | collective-permute-start | bytes 393224 | tf_op jit(solution)/shard_map/ppermute | solution.py:258
  7.7 5.3 %collective-permute-start.1 = (bf16[128,256]{1,0:T(8,128)(2,1)S(1)}, bf16[128,256]{1,0:T(8,128)(2,1)S(1)}, u32[]{:S(2)}, u32[]{:S(2)}) collective-permute-start(bf16[128,256]{1,0:T(8,128)(2,1)S(1)} %fusion.4), channel_id=1, source_target_pairs={{0,2},{1,3},{2,0},{3,1},{4,6},{5,7},{6,4},{7,5},{8,10},{9,11},{10,... | collective-permute-start | bytes 196616 | tf_op jit(solution)/shard_map/ppermute | solution.py:260
  10.6 7.2 %collective-permute-start.12 = (bf16[128,256]{1,0:T(8,128)(2,1)S(1)}, bf16[128,256]{1,0:T(8,128)(2,1)S(1)}, u32[]{:S(2)}, u32[]{:S(2)}) collective-permute-start(bf16[128,256]{1,0:T(8,128)(2,1)S(1)} %fusion.5), channel_id=1, source_target_pairs={{0,2},{1,3},{2,0},{3,1},{4,6},{5,7},{6,4},{7,5},{8,10},{9,11},{10,... | collective-permute-start | bytes 196616 | tf_op jit(solution)/shard_map/ppermute | solution.py:260
  13.0 8.7 %collective-permute-start.4 = (bf16[128,256]{1,0:T(8,128)(2,1)S(1)}, bf16[128,256]{1,0:T(8,128)(2,1)S(1)}, u32[]{:S(2)}, u32[]{:S(2)}) collective-permute-start(bf16[128,256]{1,0:T(8,128)(2,1)S(1)} %fusion.2), channel_id=1, source_target_pairs={{0,12},{1,13},{2,14},{3,15},{4,8},{5,9},{6,10},{7,11},{8,4},{9,5},... | collective-permute-start | bytes 196616 | tf_op jit(solution)/shard_map/ppermute | solution.py:265
  17.2 8.9 %collective-permute-start.3 = (bf16[128,256]{1,0:T(8,128)(2,1)S(1)}, bf16[128,256]{1,0:T(8,128)(2,1)S(1)}, u32[]{:S(2)}, u32[]{:S(2)}) collective-permute-start(bf16[128,256]{1,0:T(8,128)(2,1)S(1)} %fusion.2), channel_id=1, source_target_pairs={{0,8},{1,9},{2,10},{3,11},{4,12},{5,13},{6,14},{7,15},{8,0},{9,1},... | collective-permute-start | bytes 196616 | tf_op jit(solution)/shard_map/ppermute | solution.py:265
  17.2 8.9 %collective-permute-start.2 = (bf16[128,256]{1,0:T(8,128)(2,1)S(1)}, bf16[128,256]{1,0:T(8,128)(2,1)S(1)}, u32[]{:S(2)}, u32[]{:S(2)}) collective-permute-start(bf16[128,256]{1,0:T(8,128)(2,1)S(1)} %fusion.2), channel_id=1, source_target_pairs={{0,4},{1,5},{2,6},{3,7},{4,0},{5,1},{6,2},{7,3},{8,12},{9,13},{10,... | collective-permute-start | bytes 196616 | tf_op jit(solution)/shard_map/ppermute | solution.py:265
  17.9 8.8 %collective-permute-start.15 = (bf16[128,256]{1,0:T(8,128)(2,1)S(1)}, bf16[128,256]{1,0:T(8,128)(2,1)S(1)}, u32[]{:S(2)}, u32[]{:S(2)}) collective-permute-start(bf16[128,256]{1,0:T(8,128)(2,1)S(1)} %fusion.3), channel_id=1, source_target_pairs={{0,12},{1,13},{2,14},{3,15},{4,8},{5,9},{6,10},{7,11},{8,4},{9,5},... | collective-permute-start | bytes 196616 | tf_op jit(solution)/shard_map/ppermute | solution.py:265
  21.7 6.3 %collective-permute-start.14 = (bf16[128,256]{1,0:T(8,128)(2,1)S(1)}, bf16[128,256]{1,0:T(8,128)(2,1)S(1)}, u32[]{:S(2)}, u32[]{:S(2)}) collective-permute-start(bf16[128,256]{1,0:T(8,128)(2,1)S(1)} %fusion.3), channel_id=1, source_target_pairs={{0,8},{1,9},{2,10},{3,11},{4,12},{5,13},{6,14},{7,15},{8,0},{9,1},... | collective-permute-start | bytes 196616 | tf_op jit(solution)/shard_map/ppermute | solution.py:265
  21.7 6.3 %collective-permute-start.13 = (bf16[128,256]{1,0:T(8,128)(2,1)S(1)}, bf16[128,256]{1,0:T(8,128)(2,1)S(1)}, u32[]{:S(2)}, u32[]{:S(2)}) collective-permute-start(bf16[128,256]{1,0:T(8,128)(2,1)S(1)} %fusion.3), channel_id=1, source_target_pairs={{0,4},{1,5},{2,6},{3,7},{4,0},{5,1},{6,2},{7,3},{8,12},{9,13},{10,... | collective-permute-start | bytes 196616 | tf_op jit(solution)/shard_map/ppermute | solution.py:265
  26.3 4.9 %collective-permute-start.5 = (bf16[128,256]{1,0:T(8,128)(2,1)S(1)}, bf16[128,256]{1,0:T(8,128)(2,1)S(1)}, u32[]{:S(2)}, u32[]{:S(2)}) collective-permute-start(bf16[128,256]{1,0:T(8,128)(2,1)S(1)} %multiply_convert_fusion.1.r00), channel_id=1, source_target_pairs={{0,2},{1,3},{2,0},{3,1},{4,6},{5,7},{6,4},{7,5},{8,10},{9,11},{10,... | collective-permute-start | bytes 196616 | tf_op jit(solution)/shard_map/ppermute | solution.py:267
  28.2 8.0 %collective-permute-start.16 = (bf16[128,256]{1,0:T(8,128)(2,1)S(1)}, bf16[128,256]{1,0:T(8,128)(2,1)S(1)}, u32[]{:S(2)}, u32[]{:S(2)}) collective-permute-start(bf16[128,256]{1,0:T(8,128)(2,1)S(1)} %multiply_convert_fusion.r00), channel_id=1, source_target_pairs={{0,2},{1,3},{2,0},{3,1},{4,6},{5,7},{6,4},{7,5},{8,10},{9,11},{10,... | collective-permute-start | bytes 196616 | tf_op jit(solution)/shard_map/ppermute | solution.py:267
  29.7 6.5 %collective-permute-start.6 = (bf16[128,256]{1,0:T(8,128)(2,1)S(1)}, bf16[128,256]{1,0:T(8,128)(2,1)S(1)}, u32[]{:S(2)}, u32[]{:S(2)}) collective-permute-start(bf16[128,256]{1,0:T(8,128)(2,1)S(1)} %multiply_convert_fusion.1.r00), channel_id=1, source_target_pairs={{0,1},{1,0},{2,3},{3,2},{4,5},{5,4},{6,7},{7,6},{8,9},{9,8},{10,11... | collective-permute-start | bytes 196616 | tf_op jit(solution)/shard_map/ppermute | solution.py:268
  31.1 5.1 %collective-permute-start.7 = (bf16[128,256]{1,0:T(8,128)(2,1)S(1)}, bf16[128,256]{1,0:T(8,128)(2,1)S(1)}, u32[]{:S(2)}, u32[]{:S(2)}) collective-permute-start(bf16[128,256]{1,0:T(8,128)(2,1)S(1)} %collective-permute-done.5.r01), channel_id=1, source_target_pairs={{0,1},{1,0},{2,3},{3,2},{4,5},{5,4},{6,7},{7,6},{8,9},{9,8},{10,11... | collective-permute-start | bytes 196616 | tf_op jit(solution)/shard_map/ppermute | solution.py:269
  33.3 2.9 %copy-start = (s32[2,8]{1,0:T(2,128)S(1)}, s32[2,8]{1,0:T(2,128)}, u32[]{:S(2)}) copy-start(s32[2,8]{1,0:T(2,128)} %ranks.13) | copy-start | bytes 196
  35.6 6.3 %collective-permute-start.17 = (bf16[128,256]{1,0:T(8,128)(2,1)S(1)}, bf16[128,256]{1,0:T(8,128)(2,1)S(1)}, u32[]{:S(2)}, u32[]{:S(2)}) collective-permute-start(bf16[128,256]{1,0:T(8,128)(2,1)S(1)} %multiply_convert_fusion.r00), channel_id=1, source_target_pairs={{0,1},{1,0},{2,3},{3,2},{4,5},{5,4},{6,7},{7,6},{8,9},{9,8},{10,11... | collective-permute-start | bytes 196616 | tf_op jit(solution)/shard_map/ppermute | solution.py:268
  36.1 5.7 %collective-permute-start.18 = (bf16[128,256]{1,0:T(8,128)(2,1)S(1)}, bf16[128,256]{1,0:T(8,128)(2,1)S(1)}, u32[]{:S(2)}, u32[]{:S(2)}) collective-permute-start(bf16[128,256]{1,0:T(8,128)(2,1)S(1)} %collective-permute-done.16.r01), channel_id=1, source_target_pairs={{0,1},{1,0},{2,3},{3,2},{4,5},{5,4},{6,7},{7,6},{8,9},{9,8},{10,11... | collective-permute-start | bytes 196616 | tf_op jit(solution)/shard_map/ppermute | solution.py:269
  38.1 50.7 %collective-permute-start.10 = (bf16[4,128,512]{2,1,0:T(8,128)(2,1)S(1)}, bf16[4,128,512]{2,1,0:T(8,128)(2,1)S(1)}, u32[]{:S(2)}, u32[]{:S(2)}) collective-permute-start(bf16[4,128,512]{2,1,0:T(8,128)(2,1)S(1)} %adjoint.8.refs_0_), channel_id=1, source_target_pairs={{0,16},{16,0},{1,17},{17,1},{2,18},{18,2},{3,19},{19,3},{4,20},{20... | collective-permute-start | bytes 1572872 | tf_op jit(solution)/shard_map/ppermute | solution.py:283
  41.3 49.1 %collective-permute-start.9 = (bf16[3,128,512]{2,1,0:T(8,128)(2,1)S(1)}, bf16[3,128,512]{2,1,0:T(8,128)(2,1)S(1)}, u32[]{:S(2)}, u32[]{:S(2)}) collective-permute-start(bf16[3,128,512]{2,1,0:T(8,128)(2,1)S(1)} %adjoint.7.refs_0_), channel_id=1, source_target_pairs={{0,16},{16,0},{1,17},{17,1},{2,18},{18,2},{3,19},{19,3},{4,20},{20... | collective-permute-start | bytes 1179656 | tf_op jit(solution)/shard_map/ppermute | solution.py:283
  43.4 43.8 %collective-permute-start.19 = (bf16[3,128,512]{2,1,0:T(8,128)(2,1)S(1)}, bf16[3,128,512]{2,1,0:T(8,128)(2,1)S(1)}, u32[]{:S(2)}, u32[]{:S(2)}) collective-permute-start(bf16[3,128,512]{2,1,0:T(8,128)(2,1)S(1)} %adjoint.9.refs_0_), channel_id=1, source_target_pairs={{0,16},{16,0},{1,17},{17,1},{2,18},{18,2},{3,19},{19,3},{4,20},{20... | collective-permute-start | bytes 1179656 | tf_op jit(solution)/shard_map/ppermute | solution.py:283
  46.6 39.1 %collective-permute-start.20 = (bf16[3,128,512]{2,1,0:T(8,128)(2,1)S(1)}, bf16[3,128,512]{2,1,0:T(8,128)(2,1)S(1)}, u32[]{:S(2)}, u32[]{:S(2)}) collective-permute-start(bf16[3,128,512]{2,1,0:T(8,128)(2,1)S(1)} %adjoint.10.refs_0_), channel_id=1, source_target_pairs={{0,16},{16,0},{1,17},{17,1},{2,18},{18,2},{3,19},{19,3},{4,20},{20... | collective-permute-start | bytes 1179656 | tf_op jit(solution)/shard_map/ppermute | solution.py:283
  48.5 34.9 %collective-permute-start.21 = (bf16[2,128,512]{2,1,0:T(8,128)(2,1)S(1)}, bf16[2,128,512]{2,1,0:T(8,128)(2,1)S(1)}, u32[]{:S(2)}, u32[]{:S(2)}) collective-permute-start(bf16[2,128,512]{2,1,0:T(8,128)(2,1)S(1)} %adjoint.11.refs_0_), channel_id=1, source_target_pairs={{0,16},{16,0},{1,17},{17,1},{2,18},{18,2},{3,19},{19,3},{4,20},{20... | collective-permute-start | bytes 786440 | tf_op jit(solution)/shard_map/ppermute | solution.py:283
  83.3 8.6 %collective-permute-start.8 = (bf16[1,128,512]{2,1,0:T(8,128)(2,1)S(1)}, bf16[1,128,512]{2,1,0:T(8,128)(2,1)S(1)}, u32[]{:S(2)}, u32[]{:S(2)}) collective-permute-start(bf16[1,128,512]{2,1,0:T(8,128)(2,1)S(1)} %adjoint.6.refs_0_), channel_id=1, source_target_pairs={{0,16},{16,0},{1,17},{17,1},{2,18},{18,2},{3,19},{19,3},{4,20},{20... | collective-permute-start | bytes 393224 | tf_op jit(solution)/shard_map/ppermute | solution.py:283

commit v3 on v2

--- a/solution.py
+++ b/solution.py
@@ -11,8 +11,8 @@
 
 BF = jnp.bfloat16
 F32 = jnp.float32
-CUTS = (128, 128)
-GROUPS = ((2, 3, 3), (4, 3, 1))
+CUTS = (112, 144)
+GROUPS = ((3, 5), (4, 3, 1))
 VMEM_LIMIT = 26 * 2**20
 IN_VMEM = pl.BlockSpec(memory_space=pltpu.VMEM)
 IN_SMEM = pl.BlockSpec(memory_space=pltpu.SMEM)
@@ -44,16 +44,17 @@
     keep_refs, send_refs = rest[:n], rest[n : 2 * n]
     x_vm, u_vm, v_vm, acc, sems = rest[2 * n :]
 
-    def copies(j):
+    def copies(j, first):
         span = pl.ds(j * width, width)
-        yield pltpu.make_async_copy(x_hbm.at[span], x_vm.at[span], sems.at[j, 0])
-        for a in range(tile_rows):
-            yield pltpu.make_async_copy(v_hbm.at[a, j], v_vm.at[a, j], sems.at[j, 1 + a])
-        for a in range(tile_rows):
-            yield pltpu.make_async_copy(u_hbm.at[a, j], u_vm.at[a, j], sems.at[j, 1 + tile_rows + a])
+        if first:
+            pairs = [(x_hbm.at[span], x_vm.at[span])] + [(v_hbm.at[a, j], v_vm.at[a, j]) for a in range(tile_rows)]
+        else:
+            pairs = [(u_hbm.at[a, j], u_vm.at[a, j]) for a in range(tile_rows)]
+        base = 0 if first else 1 + tile_rows
+        return [pltpu.make_async_copy(src, dst, sems.at[j, base + k]) for k, (src, dst) in enumerate(pairs)]
 
     for j in range(tile_cols):
-        for c in copies(j):
+        for c in copies(j, True) + copies(j, False):
             c.start()
 
     mine, my_x, my_z = position()
@@ -62,7 +63,7 @@
     for j0 in range(0, tile_cols, jb):
         parts = [[] for _ in range(tile_rows)]
         for j in range(j0, j0 + jb):
-            for c in copies(j):
+            for c in copies(j, True) + copies(j, False):
                 c.wait()
             xt = x_vm[j * width : (j + 1) * width, :].T
             for a in range(tile_rows):
@@ -197,39 +198,48 @@
     )(ranks, *rs, u, v)
 
 
-def finish_kernel(n, *refs):
-    out = refs[-1]
-    j = pl.program_id(0)
-    for i in range(n):
-        a, b = refs[2 * i], refs[2 * i + 1]
-        s = a.shape[1]
-        t = a[j].astype(F32) + b[j].astype(F32)
-        out[:, i * s : (i + 1) * s] = t.T.astype(BF)
-
-
-def finish(out, pairs, start, lane_block, rows, sources):
-    count, s, width = pairs[0][0].shape
-    n = len(pairs)
-    flat = [p for pair in pairs for p in pair]
-    lanes = n * s
+def finish_kernel(plan, start, *refs):
+    buf, sems = refs[-2:]
+    out = refs[-3]
+    width = buf.shape[1]
+    copies = []
+    for c, chunks in enumerate(plan):
+        t = [refs[2 * k][at].astype(F32) + refs[2 * k + 1][at].astype(F32) for k, at in chunks]
+        buf[c] = jnp.concatenate(t, axis=0).astype(BF).T
+        copies.append(pltpu.make_async_copy(buf.at[c], out.at[pl.ds((start + c) * width, width)], sems.at[c]))
+        copies[-1].start()
+    for copy in copies:
+        copy.wait()
+
+
+def finish(out, chunks, start, count, rows, sources):
+    flat, index, plan = [], {}, []
+    for col in range(start, start + count):
+        where = []
+        for i, pieces in enumerate(chunks):
+            for first, mine, got in pieces:
+                if first <= col < first + mine.shape[0]:
+                    if (i, first) not in index:
+                        index[i, first] = len(flat) // 2
+                        flat += [mine, got]
+                    where.append((index[i, first], col - first))
+        plan.append(where)
+    width = flat[0].shape[2]
+    specs = [IN_VMEM] * len(flat)
     aliases = {}
-    specs = [IN_VMEM] * len(flat)
-    body = functools.partial(finish_kernel, n)
     if out is not None:
         aliases = {len(flat): 0}
-        specs = specs + [IN_HBM]
-        inner, m = body, len(flat)
-        body = lambda *refs: inner(*refs[:m], refs[-1])
-        flat = flat + [out]
+        specs.append(IN_HBM)
+        flat.append(out)
     return pl.pallas_call(
-        body,
-        grid=(count,),
+        functools.partial(finish_kernel, plan, start),
         in_specs=specs,
-        out_specs=pl.BlockSpec((width, lanes), lambda j: (start + j, lane_block)),
+        out_specs=IN_HBM,
         out_shape=jax.ShapeDtypeStruct((rows, sources), BF),
+        scratch_shapes=[pltpu.VMEM((count, width, sources), BF), pltpu.SemaphoreType.DMA((count,))],
         input_output_aliases=aliases,
         compiler_params=pltpu.CompilerParams(vmem_limit_bytes=VMEM_LIMIT),
-        cost_estimate=pl.CostEstimate(flops=0, bytes_accessed=2 * count * lanes * width, transcendentals=0),
+        cost_estimate=pl.CostEstimate(flops=0, bytes_accessed=2 * count * sources * width, transcendentals=0),
         name="finish",
     )(*flat)
 
@@ -269,29 +279,24 @@
             r11 = lax.ppermute(r01, "col", core_swap)
             return r00, r01, r10, r11
 
-        swapped = {}
+        swapped = [[] for _ in cuts]
         row = 0
         for i, s in enumerate(cuts):
             resid = residual(sends[i], keeps[i], sat[row : row + s])
             row += s
             start = 0
-            for g, share in enumerate(GROUPS[i]):
+            for share in GROUPS[i]:
                 per = share * tile_cols // 8
                 part = adjoint(resid, u, v, ranks, start, per, rb, zs)
-                start += per
                 if n_row == 2:
-                    swapped[i, g] = (part, lax.ppermute(part, "row", row_swap))
+                    swapped[i].append((start, part, lax.ppermute(part, "row", row_swap)))
                 else:
                     whole = lax.psum(part.astype(F32), "row").astype(BF)
-                    swapped[i, g] = (whole, jnp.zeros_like(whole))
+                    swapped[i].append((start, whole, jnp.zeros_like(whole)))
+                start += per
         out = None
-        lane = 0
-        for i, s in enumerate(cuts):
-            start = 0
-            for g, share in enumerate(GROUPS[i]):
-                out = finish(out, [swapped[i, g]], start, lane // s, rows, sources)
-                start += share * tile_cols // 8
-            lane += s
+        for start, part, _ in swapped[-1]:
+            out = finish(out, swapped, start, part.shape[0], rows, sources)
         return out
 
     return jax.shard_map(

time: 92.9 us -> 92.1 us (level)
  Pallas kernels: 27.2 us -> 21.7 us
  waiting for transfers between devices: 41.9 us -> 46.6 us
    pallas_call x6 -> x3, Pallas kernels: 7.84 us -> 2.99 us  [finish(): pl.pallas_call(functools.partial(finish_kernel, plan, start), in_specs=sp...]
    ppermute x2, waiting for transfers between devices: 1.38 us -> 3.51 us  [residual(): r01 = lax.ppermute(r00, 'col', x_swap)]
    ppermute x2, starting transfers between devices: 3.04 us -> 4.6 us  [residual(): got = lax.ppermute(half[1].astype(BF), 'col', x_swap)]
    ppermute x6 -> x5, starting transfers between devices: 7.42 us -> 5.91 us  [local(): swapped[i].append((start, part, lax.ppermute(part, 'row', row_swap)))]
    ppermute x6 -> x5, waiting for transfers between devices: 32.3 us -> 33.7 us  [local(): swapped[i].append((start, part, lax.ppermute(part, 'row', row_swap)))]
    pallas_call x6 -> x5, Pallas kernels: 8.85 us -> 8.21 us  [adjoint(): pl.pallas_call(functools.partial(adjoint_kernel, dims), in_specs=[IN_SMEM...]
  transfers between devices with their start and end apart: 22 -> 21, of which waited for: 6 -> 9; matrix products, arithmetic and copies ran while one was open for 0% -> 0% of each run, Pallas kernels for 22% -> 16%
where the time goes in v3:
time: 92.1 us; the launch traced here: 91.8 us
  waiting for transfers between devices  46.6 us (51%)
  starting transfers between devices  23 us (25%)
  Pallas kernels  21.7 us (24%)
    ppermute x5, waiting for transfers between devices, local(): swapped[i].append((start, part, lax.ppermute(part, 'row', row_swap)))  33.7 us
    ppermute x6, starting transfers between devices, residual(): total = total + lax.ppermute(mine, 'col', p).astype(F32)  9.05 us
    pallas_call x5, Pallas kernels, adjoint(): pl.pallas_call(functools.partial(adjoint_kernel, dims), in_specs=[IN_SMEM...  8.21 us
    pallas_call x1, Pallas kernels, forward(): pl.pallas_call(functools.partial(forward_kernel, dims), in_specs=[IN_SMEM...  6.09 us
    ppermute x6, waiting for transfers between devices, residual(): total = total + lax.ppermute(mine, 'col', p).astype(F32)  5.95 us
    ppermute x5, starting transfers between devices, local(): swapped[i].append((start, part, lax.ppermute(part, 'row', row_swap)))  5.91 us
    ppermute x2, starting transfers between devices, residual(): got = lax.ppermute(half[1].astype(BF), 'col', x_swap)  4.6 us
    pallas_call x2, Pallas kernels, hold(): pl.pallas_call(hold_kernel, in_specs=[IN_HBM], out_specs=pl.BlockSpec(mem...  4.4 us
  transfers between devices with their start and end apart: 21, of which 9 were waited for; matrix products, arithmetic and copies ran while one was open for 0% of the time, Pallas kernels for 16%

profile of v3, /device:TPU:0, one launch (start us, length us, event | category | flops | bytes accessed | tf_op | source)
XLA Modules:
  0.0 91.8 jit_solution(16416722461242963272)
XLA Ops:
  0.0 6.1 %forward.1 = (f32[2,112,256]{2,1,0:T(8,128)S(1)}, f32[2,144,256]{2,1,0:T(8,128)S(1)}, bf16[2,112,256]{2,1,0:T(8,128)(2,1)S(1)}, bf16[2,144,256]{2,1,0:T(8,128)(2,1)S(1)}) custom-call(s32[2,8]{1,0:T(2,128)} %ranks.11, bf16[64,256]{1,0:T(8,128)(2,1)} %obs.1, bf16[4096,256]{1,0:T(8,128)(2,1)} %x_hbm.1, bf16[2,8,512,256]{3,2,1,0:T(8,128)(2,1)} %src.2, ...), custom_call_target="tpu_custom_call" | custom-call | flops 2147483648 | bytes 10485760 | tf_op jit(solution)/shard_map/forward/pallas_call | solution.py:115
  6.1 0.6 collective-permute-start.9
  6.8 0.9 collective-permute-done.9
  7.7 2.9 %collective-permute-start.10 = (bf16[144,256]{1,0:T(8,128)(2,1)S(1)}, bf16[144,256]{1,0:T(8,128)(2,1)S(1)}, u32[]{:S(2)}, u32[]{:S(2)}) collective-permute-start(bf16[144,256]{1,0:T(8,128)(2,1)S(1)} %fusion.3), channel_id=1, source_target_pairs={{0,2},{1,3},{2,0},{3,1},{4,6},{5,7},{6,4},{7,5},{8,10},{9,11},{10,... | collective-permute-start | bytes 221192 | tf_op jit(solution)/shard_map/ppermute | solution.py:270
  10.7 2.5 %collective-permute-done.10 = bf16[144,256]{1,0:T(8,128)(2,1)S(1)} collective-permute-done((bf16[144,256]{1,0:T(8,128)(2,1)S(1)}, bf16[144,256]{1,0:T(8,128)(2,1)S(1)}, u32[]{:S(2)}, u32[]{:S(2)}) %collective-permute-start.10) | collective-permute-done | bytes 73760 | tf_op jit(solution)/shard_map/ppermute | solution.py:270
  13.2 4.0 %collective-permute-start.13 = (bf16[144,256]{1,0:T(8,128)(2,1)S(1)}, bf16[144,256]{1,0:T(8,128)(2,1)S(1)}, u32[]{:S(2)}, u32[]{:S(2)}) collective-permute-start(bf16[144,256]{1,0:T(8,128)(2,1)S(1)} %fusion.2), channel_id=1, source_target_pairs={{0,12},{1,13},{2,14},{3,15},{4,8},{5,9},{6,10},{7,11},{8,4},{9,5},... | collective-permute-start | bytes 221192 | tf_op jit(solution)/shard_map/ppermute | solution.py:275
  17.2 0.6 collective-permute-start.11
  17.8 1.7 %collective-permute-start.1 = (bf16[112,256]{1,0:T(8,128)(2,1)S(1)}, bf16[112,256]{1,0:T(8,128)(2,1)S(1)}, u32[]{:S(2)}, u32[]{:S(2)}) collective-permute-start(bf16[112,256]{1,0:T(8,128)(2,1)S(1)} %fusion.5), channel_id=1, source_target_pairs={{0,2},{1,3},{2,0},{3,1},{4,6},{5,7},{6,4},{7,5},{8,10},{9,11},{10,... | collective-permute-start | bytes 172040 | tf_op jit(solution)/shard_map/ppermute | solution.py:270
  20.1 2.8 %collective-permute-done.12 = bf16[144,256]{1,0:T(8,128)(2,1)S(1)} collective-permute-done((bf16[144,256]{1,0:T(8,128)(2,1)S(1)}, bf16[144,256]{1,0:T(8,128)(2,1)S(1)}, u32[]{:S(2)}, u32[]{:S(2)}) %collective-permute-start.12) | collective-permute-done | bytes 73760 | tf_op jit(solution)/shard_map/ppermute | solution.py:275
  23.0 1.6 %collective-permute-start.14 = (bf16[144,256]{1,0:T(8,128)(2,1)S(1)}, bf16[144,256]{1,0:T(8,128)(2,1)S(1)}, u32[]{:S(2)}, u32[]{:S(2)}) collective-permute-start(bf16[144,256]{1,0:T(8,128)(2,1)S(1)} %multiply_convert_fusion.r00), channel_id=1, source_target_pairs={{0,2},{1,3},{2,0},{3,1},{4,6},{5,7},{6,4},{7,5},{8,10},{9,11},{10,... | collective-permute-start | bytes 221192 | tf_op jit(solution)/shard_map/ppermute | solution.py:277
  24.6 2.5 %collective-permute-start.4 = (bf16[112,256]{1,0:T(8,128)(2,1)S(1)}, bf16[112,256]{1,0:T(8,128)(2,1)S(1)}, u32[]{:S(2)}, u32[]{:S(2)}) collective-permute-start(bf16[112,256]{1,0:T(8,128)(2,1)S(1)} %fusion.4), channel_id=1, source_target_pairs={{0,12},{1,13},{2,14},{3,15},{4,8},{5,9},{6,10},{7,11},{8,4},{9,5},... | collective-permute-start | bytes 172040 | tf_op jit(solution)/shard_map/ppermute | solution.py:275
  27.1 2.0 %collective-permute-start.2 = (bf16[112,256]{1,0:T(8,128)(2,1)S(1)}, bf16[112,256]{1,0:T(8,128)(2,1)S(1)}, u32[]{:S(2)}, u32[]{:S(2)}) collective-permute-start(bf16[112,256]{1,0:T(8,128)(2,1)S(1)} %fusion.4), channel_id=1, source_target_pairs={{0,4},{1,5},{2,6},{3,7},{4,0},{5,1},{6,2},{7,3},{8,12},{9,13},{10,... | collective-permute-start | bytes 172040 | tf_op jit(solution)/shard_map/ppermute | solution.py:275
  29.6 1.2 %collective-permute-done.4 = bf16[112,256]{1,0:T(8,128)(2,1)S(1)} collective-permute-done((bf16[112,256]{1,0:T(8,128)(2,1)S(1)}, bf16[112,256]{1,0:T(8,128)(2,1)S(1)}, u32[]{:S(2)}, u32[]{:S(2)}) %collective-permute-start.4) | collective-permute-done | bytes 57376 | tf_op jit(solution)/shard_map/ppermute | solution.py:275
  30.7 1.4 %collective-permute-done.3 = bf16[112,256]{1,0:T(8,128)(2,1)S(1)} collective-permute-done((bf16[112,256]{1,0:T(8,128)(2,1)S(1)}, bf16[112,256]{1,0:T(8,128)(2,1)S(1)}, u32[]{:S(2)}, u32[]{:S(2)}) %collective-permute-start.3) | collective-permute-done | bytes 57376 | tf_op jit(solution)/shard_map/ppermute | solution.py:275
  32.3 0.7 collective-permute-start.5
  33.0 3.5 %collective-permute-done.5.r01 = bf16[112,256]{1,0:T(8,128)(2,1)S(1)} collective-permute-done((bf16[112,256]{1,0:T(8,128)(2,1)S(1)}, bf16[112,256]{1,0:T(8,128)(2,1)S(1)}, u32[]{:S(2)}, u32[]{:S(2)}) %collective-permute-start.5) | collective-permute-done | bytes 57376 | tf_op jit(solution)/shard_map/ppermute | solution.py:277
  36.5 2.2 %hold.2.u_ref = bf16[2,8,512,256]{3,2,1,0:T(8,128)(2,1)S(1)} custom-call(bf16[2,8,512,256]{3,2,1,0:T(8,128)(2,1)} %src.2), custom_call_target="tpu_custom_call" | custom-call | bytes 4194304 | tf_op jit(solution)/shard_map/hold/pallas_call | solution.py:147
  38.7 2.2 %hold.3.v_ref = bf16[2,8,512,256]{3,2,1,0:T(8,128)(2,1)S(1)} custom-call(bf16[2,8,512,256]{3,2,1,0:T(8,128)(2,1)} %src.3), custom_call_target="tpu_custom_call" | custom-call | bytes 4194304 | tf_op jit(solution)/shard_map/hold/pallas_call | solution.py:147
  41.0 1.9 %adjoint.9.refs_2_ = bf16[4,144,512]{2,1,0:T(8,128)(2,1)S(1)} custom-call(s32[2,8]{1,0:T(2,128)S(1)} %copy-done, bf16[144,256]{1,0:T(8,128)(2,1)S(1)} %multiply_convert_fusion.r00, bf16[144,256]{1,0:T(8,128)(2,1)S(1)} %collective-permute-done.14.r01, bf16[144,256]{1,0:T(8,128)(2,1)S(1)} %collective-permute-done.15.r10, ...), custom_call_target="tpu_custom_call" | custom-call | flops 603979776 | bytes 147456 | tf_op jit(solution)/shard_map/adjoint/pallas_call | solution.py:187
  42.9 1.6 %collective-permute-start.20 = (bf16[4,144,512]{2,1,0:T(8,128)(2,1)S(1)}, bf16[4,144,512]{2,1,0:T(8,128)(2,1)S(1)}, u32[]{:S(2)}, u32[]{:S(2)}) collective-permute-start(bf16[4,144,512]{2,1,0:T(8,128)(2,1)S(1)} %adjoint.9.refs_2_), channel_id=1, source_target_pairs={{0,16},{16,0},{1,17},{17,1},{2,18},{18,2},{3,19},{19,3},{4,20},{20... | collective-permute-start | bytes 1769480 | tf_op jit(solution)/shard_map/ppermute | solution.py:292
  44.5 2.1 %adjoint.5.refs_4_.refs_0_ = bf16[5,112,512]{2,1,0:T(8,128)(2,1)S(1)} custom-call(s32[2,8]{1,0:T(2,128)S(1)} %copy-done, bf16[112,256]{1,0:T(8,128)(2,1)S(1)} %multiply_convert_fusion.1.r00, bf16[112,256]{1,0:T(8,128)(2,1)S(1)} %collective-permute-done.5.r01, bf16[112,256]{1,0:T(8,128)(2,1)S(1)} %collective-permute-done.6.r10, ...), custom_call_target="tpu_custom_call" | custom-call | flops 587202560 | bytes 114688 | tf_op jit(solution)/shard_map/adjoint/pallas_call | solution.py:187
  46.6 0.6 collective-permute-start.8
  47.2 1.6 %adjoint.7.refs_2_ = bf16[3,144,512]{2,1,0:T(8,128)(2,1)S(1)} custom-call(s32[2,8]{1,0:T(2,128)S(1)} %copy-done, bf16[144,256]{1,0:T(8,128)(2,1)S(1)} %multiply_convert_fusion.r00, bf16[144,256]{1,0:T(8,128)(2,1)S(1)} %collective-permute-done.14.r01, bf16[144,256]{1,0:T(8,128)(2,1)S(1)} %collective-permute-done.15.r10, ...), custom_call_target="tpu_custom_call" | custom-call | flops 452984832 | bytes 147456 | tf_op jit(solution)/shard_map/adjoint/pallas_call | solution.py:187
  48.8 1.6 %collective-permute-start.18 = (bf16[3,144,512]{2,1,0:T(8,128)(2,1)S(1)}, bf16[3,144,512]{2,1,0:T(8,128)(2,1)S(1)}, u32[]{:S(2)}, u32[]{:S(2)}) collective-permute-start(bf16[3,144,512]{2,1,0:T(8,128)(2,1)S(1)} %adjoint.7.refs_2_), channel_id=1, source_target_pairs={{0,16},{16,0},{1,17},{17,1},{2,18},{18,2},{3,19},{19,3},{4,20},{20... | collective-permute-start | bytes 1327112 | tf_op jit(solution)/shard_map/ppermute | solution.py:292
  50.4 1.6 %adjoint.8.refs_0_ = bf16[3,112,512]{2,1,0:T(8,128)(2,1)S(1)} custom-call(s32[2,8]{1,0:T(2,128)S(1)} %copy-done, bf16[112,256]{1,0:T(8,128)(2,1)S(1)} %multiply_convert_fusion.1.r00, bf16[112,256]{1,0:T(8,128)(2,1)S(1)} %collective-permute-done.5.r01, bf16[112,256]{1,0:T(8,128)(2,1)S(1)} %collective-permute-done.6.r10, ...), custom_call_target="tpu_custom_call" | custom-call | flops 352321536 | bytes 114688 | tf_op jit(solution)/shard_map/adjoint/pallas_call | solution.py:187
  52.0 0.6 collective-permute-start.19
  52.5 1.0 %adjoint.6.refs_2_ = bf16[1,144,512]{2,1,0:T(8,128)(2,1)S(1)} custom-call(s32[2,8]{1,0:T(2,128)S(1)} %copy-done, bf16[144,256]{1,0:T(8,128)(2,1)S(1)} %multiply_convert_fusion.r00, bf16[144,256]{1,0:T(8,128)(2,1)S(1)} %collective-permute-done.14.r01, bf16[144,256]{1,0:T(8,128)(2,1)S(1)} %collective-permute-done.15.r10, ...), custom_call_target="tpu_custom_call" | custom-call | flops 150994944 | bytes 147456 | tf_op jit(solution)/shard_map/adjoint/pallas_call | solution.py:187
  53.5 1.6 %collective-permute-start.17 = (bf16[1,144,512]{2,1,0:T(8,128)(2,1)S(1)}, bf16[1,144,512]{2,1,0:T(8,128)(2,1)S(1)}, u32[]{:S(2)}, u32[]{:S(2)}) collective-permute-start(bf16[1,144,512]{2,1,0:T(8,128)(2,1)S(1)} %adjoint.6.refs_2_), channel_id=1, source_target_pairs={{0,16},{16,0},{1,17},{17,1},{2,18},{18,2},{3,19},{19,3},{4,20},{20... | collective-permute-start | bytes 442376 | tf_op jit(solution)/shard_map/ppermute | solution.py:292
  55.1 33.2 %collective-permute-done.19.refs_1_ = bf16[3,112,512]{2,1,0:T(8,128)(2,1)S(1)} collective-permute-done((bf16[3,112,512]{2,1,0:T(8,128)(2,1)S(1)}, bf16[3,112,512]{2,1,0:T(8,128)(2,1)S(1)}, u32[]{:S(2)}, u32[]{:S(2)}) %collective-permute-start.19) | collective-permute-done | bytes 344096 | tf_op jit(solution)/shard_map/ppermute | solution.py:292
  88.3 1.1 %finish.3.refs_4_ = bf16[4096,256]{1,0:T(8,128)(2,1)} custom-call(bf16[3,112,512]{2,1,0:T(8,128)(2,1)S(1)} %adjoint.8.refs_0_, bf16[3,112,512]{2,1,0:T(8,128)(2,1)S(1)} %collective-permute-done.19.refs_1_, bf16[4,144,512]{2,1,0:T(8,128)(2,1)S(1)} %adjoint.9.refs_2_, bf16[4,144,512]{2,1,0:T(8,128)(2,1)S(1)} %collective-permute-done.20.refs_3_, ...), custom_call_target="tpu_custom_call" | custom-call | bytes 1048576 | tf_op jit(solution)/shard_map/finish/pallas_call | solution.py:234
  89.4 1.0 %finish.4.refs_4_ = bf16[4096,256]{1,0:T(8,128)(2,1)} custom-call(bf16[5,112,512]{2,1,0:T(8,128)(2,1)S(1)} %adjoint.5.refs_4_.refs_0_, bf16[5,112,512]{2,1,0:T(8,128)(2,1)S(1)} %collective-permute-done.8.refs_5_.refs_1_, bf16[3,144,512]{2,1,0:T(8,128)(2,1)S(1)} %adjoint.7.refs_2_, ...), custom_call_target="tpu_custom_call", output_to_operand_aliasing={{}: (4, {})} | custom-call | bytes 786432 | tf_op jit(solution)/shard_map/finish/pallas_call | solution.py:234
  91.0 0.8 finish.5
  (36 shorter events, 2.1 us)
Async XLA Ops:
  0.0 6.7 %copy-start.1 = (f32[256]{0:T(256)S(1)}, f32[256]{0:T(256)}, u32[]{:S(2)}) copy-start(f32[256]{0:T(256)} %param.8) | copy-start | bytes 3076
  0.0 32.1 %slice-start = ((f32[256]{0:T(256)}), f32[112]{0:T(128)S(1)}, s32[]{:S(2)}) async-start(f32[256]{0:T(256)} %param.8), calls=%async_computation | async-start | bytes 1024 | tf_op jit(solution)/shard_map/slice | solution.py:285
  6.1 1.6 %collective-permute-start.9 = (bf16[2,144,256]{2,1,0:T(8,128)(2,1)S(1)}, bf16[2,144,256]{2,1,0:T(8,128)(2,1)S(1)}, u32[]{:S(2)}, u32[]{:S(2)}) collective-permute-start(bf16[2,144,256]{2,1,0:T(8,128)(2,1)S(1)} %get-tuple-element.12), channel_id=1, source_target_pairs={{0,1},{1,0},{2,3},{3,2},{4,5},{5,4},{6,7},{7,6},{8,9},{9,8},{10,11... | collective-permute-start | bytes 442376 | tf_op jit(solution)/shard_map/ppermute | solution.py:268
  6.7 4.0 %collective-permute-start = (bf16[2,112,256]{2,1,0:T(8,128)(2,1)S(1)}, bf16[2,112,256]{2,1,0:T(8,128)(2,1)S(1)}, u32[]{:S(2)}, u32[]{:S(2)}) collective-permute-start(bf16[2,112,256]{2,1,0:T(8,128)(2,1)S(1)} %get-tuple-element.10), channel_id=1, source_target_pairs={{0,1},{1,0},{2,3},{3,2},{4,5},{5,4},{6,7},{7,6},{8,9},{9,8},{10,11... | collective-permute-start | bytes 344072 | tf_op jit(solution)/shard_map/ppermute | solution.py:268
  7.7 5.5 %collective-permute-start.10 = (bf16[144,256]{1,0:T(8,128)(2,1)S(1)}, bf16[144,256]{1,0:T(8,128)(2,1)S(1)}, u32[]{:S(2)}, u32[]{:S(2)}) collective-permute-start(bf16[144,256]{1,0:T(8,128)(2,1)S(1)} %fusion.3), channel_id=1, source_target_pairs={{0,2},{1,3},{2,0},{3,1},{4,6},{5,7},{6,4},{7,5},{8,10},{9,11},{10,... | collective-permute-start | bytes 221192 | tf_op jit(solution)/shard_map/ppermute | solution.py:270
  13.2 6.8 %collective-permute-start.13 = (bf16[144,256]{1,0:T(8,128)(2,1)S(1)}, bf16[144,256]{1,0:T(8,128)(2,1)S(1)}, u32[]{:S(2)}, u32[]{:S(2)}) collective-permute-start(bf16[144,256]{1,0:T(8,128)(2,1)S(1)} %fusion.2), channel_id=1, source_target_pairs={{0,12},{1,13},{2,14},{3,15},{4,8},{5,9},{6,10},{7,11},{8,4},{9,5},... | collective-permute-start | bytes 221192 | tf_op jit(solution)/shard_map/ppermute | solution.py:275
  17.2 5.7 %collective-permute-start.12 = (bf16[144,256]{1,0:T(8,128)(2,1)S(1)}, bf16[144,256]{1,0:T(8,128)(2,1)S(1)}, u32[]{:S(2)}, u32[]{:S(2)}) collective-permute-start(bf16[144,256]{1,0:T(8,128)(2,1)S(1)} %fusion.2), channel_id=1, source_target_pairs={{0,8},{1,9},{2,10},{3,11},{4,12},{5,13},{6,14},{7,15},{8,0},{9,1},... | collective-permute-start | bytes 221192 | tf_op jit(solution)/shard_map/ppermute | solution.py:275
  17.2 5.7 %collective-permute-start.11 = (bf16[144,256]{1,0:T(8,128)(2,1)S(1)}, bf16[144,256]{1,0:T(8,128)(2,1)S(1)}, u32[]{:S(2)}, u32[]{:S(2)}) collective-permute-start(bf16[144,256]{1,0:T(8,128)(2,1)S(1)} %fusion.2), channel_id=1, source_target_pairs={{0,4},{1,5},{2,6},{3,7},{4,0},{5,1},{6,2},{7,3},{8,12},{9,13},{10,... | collective-permute-start | bytes 221192 | tf_op jit(solution)/shard_map/ppermute | solution.py:275
  17.8 6.7 %collective-permute-start.1 = (bf16[112,256]{1,0:T(8,128)(2,1)S(1)}, bf16[112,256]{1,0:T(8,128)(2,1)S(1)}, u32[]{:S(2)}, u32[]{:S(2)}) collective-permute-start(bf16[112,256]{1,0:T(8,128)(2,1)S(1)} %fusion.5), channel_id=1, source_target_pairs={{0,2},{1,3},{2,0},{3,1},{4,6},{5,7},{6,4},{7,5},{8,10},{9,11},{10,... | collective-permute-start | bytes 172040 | tf_op jit(solution)/shard_map/ppermute | solution.py:270
  23.0 6.0 %collective-permute-start.14 = (bf16[144,256]{1,0:T(8,128)(2,1)S(1)}, bf16[144,256]{1,0:T(8,128)(2,1)S(1)}, u32[]{:S(2)}, u32[]{:S(2)}) collective-permute-start(bf16[144,256]{1,0:T(8,128)(2,1)S(1)} %multiply_convert_fusion.r00), channel_id=1, source_target_pairs={{0,2},{1,3},{2,0},{3,1},{4,6},{5,7},{6,4},{7,5},{8,10},{9,11},{10,... | collective-permute-start | bytes 221192 | tf_op jit(solution)/shard_map/ppermute | solution.py:277
  24.6 6.1 %collective-permute-start.4 = (bf16[112,256]{1,0:T(8,128)(2,1)S(1)}, bf16[112,256]{1,0:T(8,128)(2,1)S(1)}, u32[]{:S(2)}, u32[]{:S(2)}) collective-permute-start(bf16[112,256]{1,0:T(8,128)(2,1)S(1)} %fusion.4), channel_id=1, source_target_pairs={{0,12},{1,13},{2,14},{3,15},{4,8},{5,9},{6,10},{7,11},{8,4},{9,5},... | collective-permute-start | bytes 172040 | tf_op jit(solution)/shard_map/ppermute | solution.py:275
  27.1 5.1 %collective-permute-start.3 = (bf16[112,256]{1,0:T(8,128)(2,1)S(1)}, bf16[112,256]{1,0:T(8,128)(2,1)S(1)}, u32[]{:S(2)}, u32[]{:S(2)}) collective-permute-start(bf16[112,256]{1,0:T(8,128)(2,1)S(1)} %fusion.4), channel_id=1, source_target_pairs={{0,8},{1,9},{2,10},{3,11},{4,12},{5,13},{6,14},{7,15},{8,0},{9,1},... | collective-permute-start | bytes 172040 | tf_op jit(solution)/shard_map/ppermute | solution.py:275
  27.1 5.1 %collective-permute-start.2 = (bf16[112,256]{1,0:T(8,128)(2,1)S(1)}, bf16[112,256]{1,0:T(8,128)(2,1)S(1)}, u32[]{:S(2)}, u32[]{:S(2)}) collective-permute-start(bf16[112,256]{1,0:T(8,128)(2,1)S(1)} %fusion.4), channel_id=1, source_target_pairs={{0,4},{1,5},{2,6},{3,7},{4,0},{5,1},{6,2},{7,3},{8,12},{9,13},{10,... | collective-permute-start | bytes 172040 | tf_op jit(solution)/shard_map/ppermute | solution.py:275
  29.0 11.9 %collective-permute-start.15 = (bf16[144,256]{1,0:T(8,128)(2,1)S(1)}, bf16[144,256]{1,0:T(8,128)(2,1)S(1)}, u32[]{:S(2)}, u32[]{:S(2)}) collective-permute-start(bf16[144,256]{1,0:T(8,128)(2,1)S(1)} %multiply_convert_fusion.r00), channel_id=1, source_target_pairs={{0,1},{1,0},{2,3},{3,2},{4,5},{5,4},{6,7},{7,6},{8,9},{9,8},{10,11... | collective-permute-start | bytes 221192 | tf_op jit(solution)/shard_map/ppermute | solution.py:278
  29.0 11.9 %collective-permute-start.16 = (bf16[144,256]{1,0:T(8,128)(2,1)S(1)}, bf16[144,256]{1,0:T(8,128)(2,1)S(1)}, u32[]{:S(2)}, u32[]{:S(2)}) collective-permute-start(bf16[144,256]{1,0:T(8,128)(2,1)S(1)} %collective-permute-done.14.r01), channel_id=1, source_target_pairs={{0,1},{1,0},{2,3},{3,2},{4,5},{5,4},{6,7},{7,6},{8,9},{9,8},{10,11... | collective-permute-start | bytes 221192 | tf_op jit(solution)/shard_map/ppermute | solution.py:279
  32.3 4.2 %collective-permute-start.5 = (bf16[112,256]{1,0:T(8,128)(2,1)S(1)}, bf16[112,256]{1,0:T(8,128)(2,1)S(1)}, u32[]{:S(2)}, u32[]{:S(2)}) collective-permute-start(bf16[112,256]{1,0:T(8,128)(2,1)S(1)} %multiply_convert_fusion.1.r00), channel_id=1, source_target_pairs={{0,2},{1,3},{2,0},{3,1},{4,6},{5,7},{6,4},{7,5},{8,10},{9,11},{10,... | collective-permute-start | bytes 172040 | tf_op jit(solution)/shard_map/ppermute | solution.py:277
  33.0 11.5 %collective-permute-start.6 = (bf16[112,256]{1,0:T(8,128)(2,1)S(1)}, bf16[112,256]{1,0:T(8,128)(2,1)S(1)}, u32[]{:S(2)}, u32[]{:S(2)}) collective-permute-start(bf16[112,256]{1,0:T(8,128)(2,1)S(1)} %multiply_convert_fusion.1.r00), channel_id=1, source_target_pairs={{0,1},{1,0},{2,3},{3,2},{4,5},{5,4},{6,7},{7,6},{8,9},{9,8},{10,11... | collective-permute-start | bytes 172040 | tf_op jit(solution)/shard_map/ppermute | solution.py:278
  36.5 8.0 %collective-permute-start.7 = (bf16[112,256]{1,0:T(8,128)(2,1)S(1)}, bf16[112,256]{1,0:T(8,128)(2,1)S(1)}, u32[]{:S(2)}, u32[]{:S(2)}) collective-permute-start(bf16[112,256]{1,0:T(8,128)(2,1)S(1)} %collective-permute-done.5.r01), channel_id=1, source_target_pairs={{0,1},{1,0},{2,3},{3,2},{4,5},{5,4},{6,7},{7,6},{8,9},{9,8},{10,11... | collective-permute-start | bytes 172040 | tf_op jit(solution)/shard_map/ppermute | solution.py:279
  38.7 2.2 %copy-start = (s32[2,8]{1,0:T(2,128)S(1)}, s32[2,8]{1,0:T(2,128)}, u32[]{:S(2)}) copy-start(s32[2,8]{1,0:T(2,128)} %ranks.11) | copy-start | bytes 196
  42.9 45.4 %collective-permute-start.20 = (bf16[4,144,512]{2,1,0:T(8,128)(2,1)S(1)}, bf16[4,144,512]{2,1,0:T(8,128)(2,1)S(1)}, u32[]{:S(2)}, u32[]{:S(2)}) collective-permute-start(bf16[4,144,512]{2,1,0:T(8,128)(2,1)S(1)} %adjoint.9.refs_2_), channel_id=1, source_target_pairs={{0,16},{16,0},{1,17},{17,1},{2,18},{18,2},{3,19},{19,3},{4,20},{20... | collective-permute-start | bytes 1769480 | tf_op jit(solution)/shard_map/ppermute | solution.py:292
  46.6 41.7 %collective-permute-start.8 = (bf16[5,112,512]{2,1,0:T(8,128)(2,1)S(1)}, bf16[5,112,512]{2,1,0:T(8,128)(2,1)S(1)}, u32[]{:S(2)}, u32[]{:S(2)}) collective-permute-start(bf16[5,112,512]{2,1,0:T(8,128)(2,1)S(1)} %adjoint.5.refs_4_.refs_0_), channel_id=1, source_target_pairs={{0,16},{16,0},{1,17},{17,1},{2,18},{18,2},{3,19},{19,3},{4,20},{20... | collective-permute-start | bytes 1720328 | tf_op jit(solution)/shard_map/ppermute | solution.py:292
  48.8 40.6 %collective-permute-start.18 = (bf16[3,144,512]{2,1,0:T(8,128)(2,1)S(1)}, bf16[3,144,512]{2,1,0:T(8,128)(2,1)S(1)}, u32[]{:S(2)}, u32[]{:S(2)}) collective-permute-start(bf16[3,144,512]{2,1,0:T(8,128)(2,1)S(1)} %adjoint.7.refs_2_), channel_id=1, source_target_pairs={{0,16},{16,0},{1,17},{17,1},{2,18},{18,2},{3,19},{19,3},{4,20},{20... | collective-permute-start | bytes 1327112 | tf_op jit(solution)/shard_map/ppermute | solution.py:292
  52.0 36.3 %collective-permute-start.19 = (bf16[3,112,512]{2,1,0:T(8,128)(2,1)S(1)}, bf16[3,112,512]{2,1,0:T(8,128)(2,1)S(1)}, u32[]{:S(2)}, u32[]{:S(2)}) collective-permute-start(bf16[3,112,512]{2,1,0:T(8,128)(2,1)S(1)} %adjoint.8.refs_0_), channel_id=1, source_target_pairs={{0,16},{16,0},{1,17},{17,1},{2,18},{18,2},{3,19},{19,3},{4,20},{20... | collective-permute-start | bytes 1032200 | tf_op jit(solution)/shard_map/ppermute | solution.py:292
  53.5 37.5 %collective-permute-start.17 = (bf16[1,144,512]{2,1,0:T(8,128)(2,1)S(1)}, bf16[1,144,512]{2,1,0:T(8,128)(2,1)S(1)}, u32[]{:S(2)}, u32[]{:S(2)}) collective-permute-start(bf16[1,144,512]{2,1,0:T(8,128)(2,1)S(1)} %adjoint.6.refs_2_), channel_id=1, source_target_pairs={{0,16},{16,0},{1,17},{17,1},{2,18},{18,2},{3,19},{19,3},{4,20},{20... | collective-permute-start | bytes 442376 | tf_op jit(solution)/shard_map/ppermute | solution.py:292

commit v4 on v3

--- a/solution.py
+++ b/solution.py
@@ -11,8 +11,8 @@
 
 BF = jnp.bfloat16
 F32 = jnp.float32
-CUTS = (112, 144)
-GROUPS = ((3, 5), (4, 3, 1))
+CUTS = (144, 112)
+GROUPS = ((3, 3), (3, 2, 1))
 VMEM_LIMIT = 26 * 2**20
 IN_VMEM = pl.BlockSpec(memory_space=pltpu.VMEM)
 IN_SMEM = pl.BlockSpec(memory_space=pltpu.SMEM)
@@ -39,10 +39,10 @@
 
 
 def forward_kernel(dims, ranks, obs, x_hbm, u_hbm, v_hbm, *rest):
-    tile_rows, tile_cols, width, cap, sources, rb, zs, cuts = dims
+    tile_rows, tile_cols, width, cap, sources, rb, zs, cuts, shared = dims
     n = len(cuts)
     keep_refs, send_refs = rest[:n], rest[n : 2 * n]
-    x_vm, u_vm, v_vm, acc, sems = rest[2 * n :]
+    x_vm, u_vm, v_vm, acc, sems = rest[-5:]
 
     def copies(j, first):
         span = pl.ds(j * width, width)
@@ -53,14 +53,17 @@
         base = 0 if first else 1 + tile_rows
         return [pltpu.make_async_copy(src, dst, sems.at[j, base + k]) for k, (src, dst) in enumerate(pairs)]
 
-    for j in range(tile_cols):
-        for c in copies(j, True) + copies(j, False):
-            c.start()
+    jb = 2 if tile_cols % 2 == 0 else 1
+    steps = list(range(0, tile_cols, jb))[::-1]
+    for j0 in steps:
+        for j in range(j0, j0 + jb):
+            for c in copies(j, True) + copies(j, False):
+                c.start()
 
     mine, my_x, my_z = position()
     lane = lax.broadcasted_iota(jnp.int32, (sources, cap), 1)
-    jb = 2 if tile_cols % 2 == 0 else 1
-    for j0 in range(0, tile_cols, jb):
+    early_copies = []
+    for j0 in steps:
         parts = [[] for _ in range(tile_rows)]
         for j in range(j0, j0 + jb):
             for c in copies(j, True) + copies(j, False):
@@ -72,10 +75,20 @@
         for a in range(tile_rows):
             w = jnp.concatenate([permuted_rows(u_vm[a, j], zs, rb) for j in range(j0, j0 + jb)], axis=1)
             p = dot_nt(jnp.concatenate(parts[a], axis=1), w)
-            if j0 == 0:
+            if j0 == steps[0]:
                 acc[a] = p
             else:
                 acc[a] += p
+        if shared and j0 == steps[0]:
+            early, masked, early_sems = rest[2 * n : 2 * n + 3]
+            col = tile_cols - 1 - lax.axis_index("row")
+            rank_lane = lax.broadcasted_iota(jnp.int32, (width, cap), 1)
+            for a in range(tile_rows):
+                masked[a] = jnp.where(rank_lane < ranks[a, col], u_vm[a, col], jnp.zeros((), BF))
+                early_copies.append(pltpu.make_async_copy(masked.at[a], early.at[0, a], early_sems.at[0, a]))
+                early_copies.append(pltpu.make_async_copy(v_vm.at[a, col], early.at[1, a], early_sems.at[1, a]))
+            for c in early_copies:
+                c.start()
 
     nz = zs * tile_rows
     q_lanes = width // 4
@@ -102,21 +115,30 @@
                 send_refs[i][slot] = val.astype(BF)
 
             row += s
-
-
-def forward(x, obs, u, v, ranks, cuts, zs):
+    for c in early_copies:
+        c.wait()
+
+
+def forward(x, obs, u, v, ranks, cuts, zs, shared):
     tile_rows, tile_cols, width, cap = u.shape
     sources = x.shape[1]
     rb = obs.shape[0]
     block = tile_rows * width // 4
-    dims = (tile_rows, tile_cols, width, cap, sources, rb, zs, cuts)
+    dims = (tile_rows, tile_cols, width, cap, sources, rb, zs, cuts, shared)
     outs = [pltpu.VMEM((2, s, block), F32) for s in cuts] + [pltpu.VMEM((2, s, block), BF) for s in cuts]
+    out_specs = [IN_VMEM] * len(outs)
+    extra = []
+    if shared:
+        outs.append(pltpu.VMEM((2, tile_rows, width, cap), BF))
+        out_specs.append(pl.BlockSpec(memory_space=pl.ANY))
+        extra = [pltpu.VMEM((tile_rows, width, cap), BF), pltpu.SemaphoreType.DMA((2, tile_rows))]
     room = 2**20 + sum(math.prod(o.shape) * o.dtype.itemsize for o in outs)
     res = pl.pallas_call(
         functools.partial(forward_kernel, dims),
         in_specs=[IN_SMEM, IN_VMEM, IN_HBM, IN_HBM, IN_HBM],
-        out_specs=[IN_VMEM] * len(outs),
-        scratch_shapes=[
+        out_specs=out_specs,
+        scratch_shapes=extra
+        + [
             pltpu.VMEM(x.shape, BF),
             pltpu.VMEM(u.shape, BF),
             pltpu.VMEM(v.shape, BF),
@@ -133,7 +155,7 @@
         name="forward",
     )(ranks, obs, x, u, v)
     n = len(cuts)
-    return res[:n], res[n:]
+    return res[:n], res[n : 2 * n], res[2 * n :]
 
 
 def hold_kernel(src, dst, sem):
@@ -198,6 +220,102 @@
     )(ranks, *rs, u, v)
 
 
+def pair_kernel(dims, ranks, *refs):
+    tile_rows, tile_cols, width, cap, cuts, rb, zs = dims
+    n = len(cuts)
+    other = refs[4 * n : 4 * n + 4]
+    got, u_ref, v_ref, g_ref, held, theirs = refs[4 * n + 4 :]
+    mine, my_x, _ = position()
+    base = my_x * 2 + mine
+    for k, bits in enumerate((0, 2, 1, 3)):
+        row = 0
+        for i, s in enumerate(cuts):
+            held[base ^ bits, row : row + s] = refs[4 * i + k][...]
+            row += s
+        theirs[base ^ bits] = other[k][...]
+    col = tile_cols - 2 + lax.axis_index("row")
+    q_lanes = width // 4
+    sources = held.shape[1]
+    lane = lax.broadcasted_iota(jnp.int32, (sources, cap), 1)
+    total = None
+    for a in range(tile_rows):
+        span = slice(a * q_lanes, (a + 1) * q_lanes)
+        r = jnp.concatenate([held[q][:, span] for q in range(4)], axis=1)
+        adj = dot_nn(r, permuted_rows(u_ref[a, col], zs, rb))
+        adj = jnp.where(lane < ranks[a, col], adj, 0.0).astype(BF)
+        g = dot_nt(adj, v_ref[a, col])
+        total = g if total is None else total + g
+        r = jnp.concatenate([theirs[q][:, span] for q in range(4)], axis=1)
+        adj = dot_nn(r, permuted_rows(got[0, a], zs, rb)).astype(BF)
+        total = total + dot_nt(adj, got[1, a])
+    g_ref[...] = total.astype(BF)
+
+
+def pair_column(resid, other, got, u, v, ranks, rb, zs):
+    tile_rows, tile_cols, width, cap = u.shape
+    cuts = tuple(rs[0].shape[0] for rs in resid)
+    sources, block = other[0].shape
+    dims = (tile_rows, tile_cols, width, cap, cuts, rb, zs)
+    flat = [r for rs in resid for r in rs] + list(other)
+    return pl.pallas_call(
+        functools.partial(pair_kernel, dims),
+        in_specs=[IN_SMEM] + [IN_VMEM] * (len(flat) + 3),
+        out_specs=IN_VMEM,
+        scratch_shapes=[pltpu.VMEM((4, sources, block), BF)] * 2,
+        out_shape=pltpu.VMEM((sources, width), BF),
+        compiler_params=pltpu.CompilerParams(vmem_limit_bytes=VMEM_LIMIT),
+        cost_estimate=pl.CostEstimate(
+            flops=8 * tile_rows * width * cap * sources, bytes_accessed=4 * sources * block, transcendentals=0
+        ),
+        name="pair",
+    )(ranks, *flat, got, u, v)
+
+
+def join_kernel(*refs):
+    row = 0
+    for r in refs[:-1]:
+        refs[-1][row : row + r.shape[0]] = r[...]
+        row += r.shape[0]
+
+
+def join(parts):
+    shape = (sum(p.shape[0] for p in parts), parts[0].shape[1])
+    return pl.pallas_call(
+        join_kernel,
+        in_specs=[IN_VMEM] * len(parts),
+        out_specs=IN_VMEM,
+        out_shape=pltpu.VMEM(shape, BF),
+        compiler_params=pltpu.CompilerParams(vmem_limit_bytes=VMEM_LIMIT),
+        cost_estimate=pl.CostEstimate(flops=0, bytes_accessed=4 * shape[0] * shape[1], transcendentals=0),
+        name="join",
+    )(*parts)
+
+
+def place_kernel(tile_cols, flip, g_ref, _, out, buf, sem):
+    row = lax.axis_index("row")
+    width = buf.shape[0]
+    col = tile_cols - 2 + (1 - row if flip else row)
+    buf[...] = g_ref[...].T
+    copy = pltpu.make_async_copy(buf, out.at[pl.ds(pl.multiple_of(col * width, width), width)], sem)
+    copy.start()
+    copy.wait()
+
+
+def place(out, column, tile_cols, flip):
+    sources, width = column.shape
+    return pl.pallas_call(
+        functools.partial(place_kernel, tile_cols, flip),
+        in_specs=[IN_VMEM, IN_HBM],
+        out_specs=IN_HBM,
+        out_shape=jax.ShapeDtypeStruct(out.shape, BF),
+        scratch_shapes=[pltpu.VMEM((width, sources), BF), pltpu.SemaphoreType.DMA],
+        input_output_aliases={1: 0},
+        compiler_params=pltpu.CompilerParams(vmem_limit_bytes=VMEM_LIMIT),
+        cost_estimate=pl.CostEstimate(flops=0, bytes_accessed=2 * sources * width, transcendentals=0),
+        name="place",
+    )(column, out)
+
+
 def finish_kernel(plan, start, *refs):
     buf, sems = refs[-2:]
     out = refs[-3]
@@ -260,7 +378,11 @@
         zs = nz // tile_rows
         cuts = tuple(c * sources // 256 for c in CUTS)
         sat = sat_scale[:, None]
-        keeps, sends = forward(x_field, observed, u, v, ranks, cuts, zs)
+        shared = n_row == 2
+        keeps, sends, early = forward(x_field, observed, u, v, ranks, cuts, zs, shared)
+        cols = tile_cols - 2 if shared else tile_cols
+        if shared:
+            theirs = lax.ppermute(early[0], "row", row_swap)
         u = hold(u, 0)
         v = hold(v, 2 * u.size)
 
@@ -275,18 +397,23 @@
                 total = total + lax.ppermute(mine, "col", p).astype(F32)
             r00 = (sc * jnp.tanh(total / sc)).astype(BF)
             r01 = lax.ppermute(r00, "col", x_swap)
-            r10 = lax.ppermute(r00, "col", core_swap)
-            r11 = lax.ppermute(r01, "col", core_swap)
-            return r00, r01, r10, r11
+            if shared:
+                other.append(lax.ppermute(r00, "row", row_swap))
+            return (r00, r01) + gather(r00, r01)
+
+        def gather(r00, r01):
+            return lax.ppermute(r00, "col", core_swap), lax.ppermute(r01, "col", core_swap)
 
         swapped = [[] for _ in cuts]
+        resids, other = [], []
         row = 0
         for i, s in enumerate(cuts):
             resid = residual(sends[i], keeps[i], sat[row : row + s])
+            resids.append(resid)
             row += s
             start = 0
-            for share in GROUPS[i]:
-                per = share * tile_cols // 8
+            for g in range(len(GROUPS[i])):
+                per = sum(GROUPS[i][: g + 1]) * cols // sum(GROUPS[i]) - start
                 part = adjoint(resid, u, v, ranks, start, per, rb, zs)
                 if n_row == 2:
                     swapped[i].append((start, part, lax.ppermute(part, "row", row_swap)))
@@ -294,9 +421,18 @@
                     whole = lax.psum(part.astype(F32), "row").astype(BF)
                     swapped[i].append((start, whole, jnp.zeros_like(whole)))
                 start += per
+        if shared:
+            r00 = join(other)
+            r01 = lax.ppermute(r00, "col", x_swap)
+            blocks = (r00, r01) + gather(r00, r01)
+            column = pair_column(resids, blocks, theirs, u, v, ranks, rb, zs)
+            column_got = lax.ppermute(column, "row", row_swap)
         out = None
         for start, part, _ in swapped[-1]:
             out = finish(out, swapped, start, part.shape[0], rows, sources)
+        if shared:
+            out = place(out, column, tile_cols, False)
+            out = place(out, column_got, tile_cols, True)
         return out
 
     return jax.shard_map(

time: 92.1 us -> 89.6 us (0.973)
  waiting for transfers between devices: 46.6 us -> 38.1 us
  starting transfers between devices: 23 us -> 26.9 us
  Pallas kernels: 21.7 us -> 23.8 us
    ppermute x4 -> x11, starting transfers between devices: 0.52 us -> 8.03 us  [the longest x1 2.93 us: local(): theirs = lax.ppermute(early[0], 'row', row_swap)]
    ppermute x5, waiting for transfers between devices: 33.7 us -> 26.8 us  [local(): swapped[i].append((start, part, lax.ppermute(part, 'row', row_swap)))]
    pallas_call x0 -> x4, Pallas kernels: none -> 3.35 us  [the longest x2 1.67 us: place(): pl.pallas_call(functools.partial(place_kernel, tile_cols, flip), in_specs...]
    ppermute x2, waiting for transfers between devices: 3.51 us -> 0.56 us  [residual(): r01 = lax.ppermute(r00, 'col', x_swap)]
    ppermute x2, starting transfers between devices: 4.6 us -> 2.16 us  [residual(): got = lax.ppermute(half[1].astype(BF), 'col', x_swap)]
    ppermute x4 -> x11, waiting for transfers between devices: 0.01 us -> 2.02 us  [the longest x2 1.99 us: residual(): other.append(lax.ppermute(r00, 'row', row_swap))]
    pallas_call x5, Pallas kernels: 8.21 us -> 7 us  [adjoint(): pl.pallas_call(functools.partial(adjoint_kernel, dims), in_specs=[IN_SMEM...]
  transfers between devices with their start and end apart: 21 -> 28, of which waited for: 9 -> 10; matrix products, arithmetic and copies ran while one was open for 0% -> 0% of each run, Pallas kernels for 16% -> 19%
where the time goes in v4:
time: 89.6 us; the launch traced here: 89.4 us
  waiting for transfers between devices  38.1 us (43%)
  starting transfers between devices  26.9 us (30%)
  Pallas kernels  23.8 us (27%)
    ppermute x5, waiting for transfers between devices, local(): swapped[i].append((start, part, lax.ppermute(part, 'row', row_swap)))  26.8 us
    ppermute x6, starting transfers between devices, residual(): total = total + lax.ppermute(mine, 'col', p).astype(F32)  8.13 us
    pallas_call x5, Pallas kernels, adjoint(): pl.pallas_call(functools.partial(adjoint_kernel, dims), in_specs=[IN_SMEM...  7 us
    pallas_call x1, Pallas kernels, forward(): pl.pallas_call(functools.partial(forward_kernel, dims), in_specs=[IN_SMEM...  6.24 us
    ppermute x6, waiting for transfers between devices, residual(): total = total + lax.ppermute(mine, 'col', p).astype(F32)  6.22 us
    ppermute x5, starting transfers between devices, local(): swapped[i].append((start, part, lax.ppermute(part, 'row', row_swap)))  5.91 us
    pallas_call x2, Pallas kernels, hold(): pl.pallas_call(hold_kernel, in_specs=[IN_HBM], out_specs=pl.BlockSpec(mem...  4.4 us
    ppermute x1, starting transfers between devices, local(): theirs = lax.ppermute(early[0], 'row', row_swap)  2.93 us
  transfers between devices with their start and end apart: 28, of which 10 were waited for; matrix products, arithmetic and copies ran while one was open for 0% of the time, Pallas kernels for 19%

profile of v4, /device:TPU:0, one launch (start us, length us, event | category | flops | bytes accessed | tf_op | source)
XLA Modules:
  0.0 89.4 jit_solution(5206623272708617107)
XLA Ops:
  0.0 6.2 %forward.1 = (f32[2,144,256]{2,1,0:T(8,128)S(1)}, f32[2,112,256]{2,1,0:T(8,128)S(1)}, bf16[2,144,256]{2,1,0:T(8,128)(2,1)S(1)}, bf16[2,112,256]{2,1,0:T(8,128)(2,1)S(1)}, bf16[2,2,512,256]{3,2,1,0:T(8,128)(2,1)S(1)}) custom-call(s32[2,8]{1,0:T(2,128)} %ranks.13, bf16[64,256]{1,0:T(8,128)(2,1)} %obs.1, bf16[4096,256]{1,0:T(8,128)(2,1)} %x_hbm.1, ...), custom_call_target="tpu_custom_call" | custom-call | flops 2147483648 | bytes 10485760 | tf_op jit(solution)/shard_map/forward/pallas_call | solution.py:136
  6.9 2.9 %collective-permute-start.21 = (bf16[2,2,512,256]{3,2,1,0:T(8,128)(2,1)S(1)}, bf16[2,2,512,256]{3,2,1,0:T(8,128)(2,1)S(1)}, u32[]{:S(2)}, u32[]{:S(2)}) collective-permute-start(bf16[2,2,512,256]{3,2,1,0:T(8,128)(2,1)S(1)} %get-tuple-element.14), channel_id=1, source_target_pairs={{0,16},{16,0},{1,17},{17,1},{2,18},{18,2},{3,19},{19,3},{4,20},{20... | collective-permute-start | bytes 3145736 | tf_op jit(solution)/shard_map/ppermute | solution.py:385
  9.9 1.6 %collective-permute-start.9 = (bf16[112,256]{1,0:T(8,128)(2,1)S(1)}, bf16[112,256]{1,0:T(8,128)(2,1)S(1)}, u32[]{:S(2)}, u32[]{:S(2)}) collective-permute-start(bf16[112,256]{1,0:T(8,128)(2,1)S(1)} %fusion.5), channel_id=1, source_target_pairs={{0,2},{1,3},{2,0},{3,1},{4,6},{5,7},{6,4},{7,5},{8,10},{9,11},{10,... | collective-permute-start | bytes 172040 | tf_op jit(solution)/shard_map/ppermute | solution.py:392
  12.1 2.5 %collective-permute-done.9 = bf16[112,256]{1,0:T(8,128)(2,1)S(1)} collective-permute-done((bf16[112,256]{1,0:T(8,128)(2,1)S(1)}, bf16[112,256]{1,0:T(8,128)(2,1)S(1)}, u32[]{:S(2)}, u32[]{:S(2)}) %collective-permute-start.9) | collective-permute-done | bytes 57376 | tf_op jit(solution)/shard_map/ppermute | solution.py:392
  14.6 3.7 %collective-permute-start.12 = (bf16[112,256]{1,0:T(8,128)(2,1)S(1)}, bf16[112,256]{1,0:T(8,128)(2,1)S(1)}, u32[]{:S(2)}, u32[]{:S(2)}) collective-permute-start(bf16[112,256]{1,0:T(8,128)(2,1)S(1)} %fusion.4), channel_id=1, source_target_pairs={{0,12},{1,13},{2,14},{3,15},{4,8},{5,9},{6,10},{7,11},{8,4},{9,5},... | collective-permute-start | bytes 172040 | tf_op jit(solution)/shard_map/ppermute | solution.py:397
  19.1 3.7 %collective-permute-start.4 = (bf16[144,256]{1,0:T(8,128)(2,1)S(1)}, bf16[144,256]{1,0:T(8,128)(2,1)S(1)}, u32[]{:S(2)}, u32[]{:S(2)}) collective-permute-start(bf16[144,256]{1,0:T(8,128)(2,1)S(1)} %fusion.2), channel_id=1, source_target_pairs={{0,12},{1,13},{2,14},{3,15},{4,8},{5,9},{6,10},{7,11},{8,4},{9,5},... | collective-permute-start | bytes 221192 | tf_op jit(solution)/shard_map/ppermute | solution.py:397
  22.8 3.1 %collective-permute-done.11 = bf16[112,256]{1,0:T(8,128)(2,1)S(1)} collective-permute-done((bf16[112,256]{1,0:T(8,128)(2,1)S(1)}, bf16[112,256]{1,0:T(8,128)(2,1)S(1)}, u32[]{:S(2)}, u32[]{:S(2)}) %collective-permute-start.11) | collective-permute-done | bytes 57376 | tf_op jit(solution)/shard_map/ppermute | solution.py:397
  26.0 1.1 %collective-permute-start.17 = (bf16[112,256]{1,0:T(8,128)(2,1)S(1)}, bf16[112,256]{1,0:T(8,128)(2,1)S(1)}, u32[]{:S(2)}, u32[]{:S(2)}) collective-permute-start(bf16[112,256]{1,0:T(8,128)(2,1)S(1)} %multiply_convert_fusion.1.refs_4_.r00), channel_id=1, source_target_pairs={{0,16},{16,0},{1,17},{17,1},{2,18},{18,2},{3,19},{19,3},{4,20},{20... | collective-permute-start | bytes 172040 | tf_op jit(solution)/shard_map/ppermute | solution.py:401
  27.1 2.0 %collective-permute-done.3 = bf16[144,256]{1,0:T(8,128)(2,1)S(1)} collective-permute-done((bf16[144,256]{1,0:T(8,128)(2,1)S(1)}, bf16[144,256]{1,0:T(8,128)(2,1)S(1)}, u32[]{:S(2)}, u32[]{:S(2)}) %collective-permute-start.3) | collective-permute-done | bytes 73760 | tf_op jit(solution)/shard_map/ppermute | solution.py:397
  29.1 1.2 %collective-permute-done.2 = bf16[144,256]{1,0:T(8,128)(2,1)S(1)} collective-permute-done((bf16[144,256]{1,0:T(8,128)(2,1)S(1)}, bf16[144,256]{1,0:T(8,128)(2,1)S(1)}, u32[]{:S(2)}, u32[]{:S(2)}) %collective-permute-start.2) | collective-permute-done | bytes 73760 | tf_op jit(solution)/shard_map/ppermute | solution.py:397
  30.3 1.1 %collective-permute-start.16 = (bf16[144,256]{1,0:T(8,128)(2,1)S(1)}, bf16[144,256]{1,0:T(8,128)(2,1)S(1)}, u32[]{:S(2)}, u32[]{:S(2)}) collective-permute-start(bf16[144,256]{1,0:T(8,128)(2,1)S(1)} %multiply_convert_fusion.refs_0_.r00), channel_id=1, source_target_pairs={{0,16},{16,0},{1,17},{17,1},{2,18},{18,2},{3,19},{19,3},{4,20},{20... | collective-permute-start | bytes 221192 | tf_op jit(solution)/shard_map/ppermute | solution.py:401
  31.4 1.8 %collective-permute-start.13 = (bf16[112,256]{1,0:T(8,128)(2,1)S(1)}, bf16[112,256]{1,0:T(8,128)(2,1)S(1)}, u32[]{:S(2)}, u32[]{:S(2)}) collective-permute-start(bf16[112,256]{1,0:T(8,128)(2,1)S(1)} %multiply_convert_fusion.1.refs_4_.r00), channel_id=1, source_target_pairs={{0,2},{1,3},{2,0},{3,1},{4,6},{5,7},{6,4},{7,5},{8,10},{9,11},{10,... | collective-permute-start | bytes 172040 | tf_op jit(solution)/shard_map/ppermute | solution.py:399
  33.5 1.6 %collective-permute-done.17.refs_1_ = bf16[112,256]{1,0:T(8,128)(2,1)S(1)} collective-permute-done((bf16[112,256]{1,0:T(8,128)(2,1)S(1)}, bf16[112,256]{1,0:T(8,128)(2,1)S(1)}, u32[]{:S(2)}, u32[]{:S(2)}) %collective-permute-start.17) | collective-permute-done | bytes 57376 | tf_op jit(solution)/shard_map/ppermute | solution.py:401
  36.0 1.8 %collective-permute-start.18 = (bf16[256,256]{1,0:T(8,128)(2,1)S(1)}, bf16[256,256]{1,0:T(8,128)(2,1)S(1)}, u32[]{:S(2)}, u32[]{:S(2)}) collective-permute-start(bf16[256,256]{1,0:T(8,128)(2,1)S(1)} %join.1.refs_8_), channel_id=1, source_target_pairs={{0,2},{1,3},{2,0},{3,1},{4,6},{5,7},{6,4},{7,5},{8,10},{9,11},{10,... | collective-permute-start | bytes 393224 | tf_op jit(solution)/shard_map/ppermute | solution.py:426
  38.4 2.2 %hold.2.refs_13_.u_ref = bf16[2,8,512,256]{3,2,1,0:T(8,128)(2,1)S(1)} custom-call(bf16[2,8,512,256]{3,2,1,0:T(8,128)(2,1)} %src.2), custom_call_target="tpu_custom_call" | custom-call | bytes 4194304 | tf_op jit(solution)/shard_map/hold/pallas_call | solution.py:169
  40.6 2.2 %hold.3.refs_14_.v_ref = bf16[2,8,512,256]{3,2,1,0:T(8,128)(2,1)S(1)} custom-call(bf16[2,8,512,256]{3,2,1,0:T(8,128)(2,1)} %src.3), custom_call_target="tpu_custom_call" | custom-call | bytes 4194304 | tf_op jit(solution)/shard_map/hold/pallas_call | solution.py:169
  42.8 1.6 %adjoint.9.refs_2_ = bf16[3,112,512]{2,1,0:T(8,128)(2,1)S(1)} custom-call(s32[2,8]{1,0:T(2,128)S(1)} %copy-done, bf16[112,256]{1,0:T(8,128)(2,1)S(1)} %multiply_convert_fusion.1.refs_4_.r00, bf16[112,256]{1,0:T(8,128)(2,1)S(1)} %collective-permute-done.13.refs_5_.r01, bf16[112,256]{1,0:T(8,128)(2,1)S(1)} %collective-permute-done.14.refs_6_.r10, ...), custom_call_target="tpu_custom_call" | custom-call | flops 352321536 | bytes 114688 | tf_op jit(solution)/shard_map/adjoint/pallas_call | solution.py:209
  44.4 1.6 %collective-permute-start.27 = (bf16[3,112,512]{2,1,0:T(8,128)(2,1)S(1)}, bf16[3,112,512]{2,1,0:T(8,128)(2,1)S(1)}, u32[]{:S(2)}, u32[]{:S(2)}) collective-permute-start(bf16[3,112,512]{2,1,0:T(8,128)(2,1)S(1)} %adjoint.9.refs_2_), channel_id=1, source_target_pairs={{0,16},{16,0},{1,17},{17,1},{2,18},{18,2},{3,19},{19,3},{4,20},{20... | collective-permute-start | bytes 1032200 | tf_op jit(solution)/shard_map/ppermute | solution.py:419
  46.0 1.6 %adjoint.8.refs_0_ = bf16[3,144,512]{2,1,0:T(8,128)(2,1)S(1)} custom-call(s32[2,8]{1,0:T(2,128)S(1)} %copy-done, bf16[144,256]{1,0:T(8,128)(2,1)S(1)} %multiply_convert_fusion.refs_0_.r00, bf16[144,256]{1,0:T(8,128)(2,1)S(1)} %collective-permute-done.5.refs_1_.r01, bf16[144,256]{1,0:T(8,128)(2,1)S(1)} %collective-permute-done.6.refs_2_.r10, ...), custom_call_target="tpu_custom_call" | custom-call | flops 452984832 | bytes 147456 | tf_op jit(solution)/shard_map/adjoint/pallas_call | solution.py:209
  48.2 1.6 %adjoint.5.refs_0_ = bf16[3,144,512]{2,1,0:T(8,128)(2,1)S(1)} custom-call(s32[2,8]{1,0:T(2,128)S(1)} %copy-done, bf16[144,256]{1,0:T(8,128)(2,1)S(1)} %multiply_convert_fusion.refs_0_.r00, bf16[144,256]{1,0:T(8,128)(2,1)S(1)} %collective-permute-done.5.refs_1_.r01, bf16[144,256]{1,0:T(8,128)(2,1)S(1)} %collective-permute-done.6.refs_2_.r10, ...), custom_call_target="tpu_custom_call" | custom-call | flops 452984832 | bytes 147456 | tf_op jit(solution)/shard_map/adjoint/pallas_call | solution.py:209
  49.8 1.6 %collective-permute-start.23 = (bf16[3,144,512]{2,1,0:T(8,128)(2,1)S(1)}, bf16[3,144,512]{2,1,0:T(8,128)(2,1)S(1)}, u32[]{:S(2)}, u32[]{:S(2)}) collective-permute-start(bf16[3,144,512]{2,1,0:T(8,128)(2,1)S(1)} %adjoint.5.refs_0_), channel_id=1, source_target_pairs={{0,16},{16,0},{1,17},{17,1},{2,18},{18,2},{3,19},{19,3},{4,20},{20... | collective-permute-start | bytes 1327112 | tf_op jit(solution)/shard_map/ppermute | solution.py:419
  51.4 1.7 %pair.1.g_ref = bf16[256,512]{1,0:T(8,128)(2,1)S(1)} custom-call(s32[2,8]{1,0:T(2,128)S(1)} %copy-done, bf16[144,256]{1,0:T(8,128)(2,1)S(1)} %multiply_convert_fusion.refs_0_.r00, bf16[144,256]{1,0:T(8,128)(2,1)S(1)} %collective-permute-done.5.refs_1_.r01, bf16[144,256]{1,0:T(8,128)(2,1)S(1)} %collective-permute-done.6.refs_2_.r10, ...), custom_call_target="tpu_custom_call" | custom-call | flops 536870912 | bytes 262144 | tf_op jit(solution)/shard_map/pair/pallas_call | solution.py:260
  53.7 1.3 %adjoint.7.refs_2_ = bf16[2,112,512]{2,1,0:T(8,128)(2,1)S(1)} custom-call(s32[2,8]{1,0:T(2,128)S(1)} %copy-done, bf16[112,256]{1,0:T(8,128)(2,1)S(1)} %multiply_convert_fusion.1.refs_4_.r00, bf16[112,256]{1,0:T(8,128)(2,1)S(1)} %collective-permute-done.13.refs_5_.r01, bf16[112,256]{1,0:T(8,128)(2,1)S(1)} %collective-permute-done.14.refs_6_.r10, ...), custom_call_target="tpu_custom_call" | custom-call | flops 234881024 | bytes 114688 | tf_op jit(solution)/shard_map/adjoint/pallas_call | solution.py:209
  54.9 1.6 %collective-permute-start.25 = (bf16[2,112,512]{2,1,0:T(8,128)(2,1)S(1)}, bf16[2,112,512]{2,1,0:T(8,128)(2,1)S(1)}, u32[]{:S(2)}, u32[]{:S(2)}) collective-permute-start(bf16[2,112,512]{2,1,0:T(8,128)(2,1)S(1)} %adjoint.7.refs_2_), channel_id=1, source_target_pairs={{0,16},{16,0},{1,17},{17,1},{2,18},{18,2},{3,19},{19,3},{4,20},{20... | collective-permute-start | bytes 688136 | tf_op jit(solution)/shard_map/ppermute | solution.py:419
  56.5 1.0 %adjoint.6.refs_2_ = bf16[1,112,512]{2,1,0:T(8,128)(2,1)S(1)} custom-call(s32[2,8]{1,0:T(2,128)S(1)} %copy-done, bf16[112,256]{1,0:T(8,128)(2,1)S(1)} %multiply_convert_fusion.1.refs_4_.r00, bf16[112,256]{1,0:T(8,128)(2,1)S(1)} %collective-permute-done.13.refs_5_.r01, bf16[112,256]{1,0:T(8,128)(2,1)S(1)} %collective-permute-done.14.refs_6_.r10, ...), custom_call_target="tpu_custom_call" | custom-call | flops 117440512 | bytes 114688 | tf_op jit(solution)/shard_map/adjoint/pallas_call | solution.py:209
  58.1 6.8 %collective-permute-done.26.refs_1_ = bf16[3,144,512]{2,1,0:T(8,128)(2,1)S(1)} collective-permute-done((bf16[3,144,512]{2,1,0:T(8,128)(2,1)S(1)}, bf16[3,144,512]{2,1,0:T(8,128)(2,1)S(1)}, u32[]{:S(2)}, u32[]{:S(2)}) %collective-permute-start.26) | collective-permute-done | bytes 442400 | tf_op jit(solution)/shard_map/ppermute | solution.py:419
  64.9 1.0 %finish.3.refs_4_ = bf16[4096,256]{1,0:T(8,128)(2,1)} custom-call(bf16[3,144,512]{2,1,0:T(8,128)(2,1)S(1)} %adjoint.8.refs_0_, bf16[3,144,512]{2,1,0:T(8,128)(2,1)S(1)} %collective-permute-done.26.refs_1_, bf16[3,112,512]{2,1,0:T(8,128)(2,1)S(1)} %adjoint.9.refs_2_, bf16[3,112,512]{2,1,0:T(8,128)(2,1)S(1)} %collective-permute-done.27.refs_3_), custom_call_target="tpu_custom_call" | custom-call | bytes 786432 | tf_op jit(solution)/shard_map/finish/pallas_call | solution.py:352
  65.9 19.0 %collective-permute-done.25.refs_3_ = bf16[2,112,512]{2,1,0:T(8,128)(2,1)S(1)} collective-permute-done((bf16[2,112,512]{2,1,0:T(8,128)(2,1)S(1)}, bf16[2,112,512]{2,1,0:T(8,128)(2,1)S(1)}, u32[]{:S(2)}, u32[]{:S(2)}) %collective-permute-start.25) | collective-permute-done | bytes 229408 | tf_op jit(solution)/shard_map/ppermute | solution.py:419
  84.9 0.9 %finish.4.refs_4_ = bf16[4096,256]{1,0:T(8,128)(2,1)} custom-call(bf16[3,144,512]{2,1,0:T(8,128)(2,1)S(1)} %adjoint.5.refs_0_, bf16[3,144,512]{2,1,0:T(8,128)(2,1)S(1)} %collective-permute-done.23.refs_1_, bf16[2,112,512]{2,1,0:T(8,128)(2,1)S(1)} %adjoint.7.refs_2_, ...), custom_call_target="tpu_custom_call", output_to_operand_aliasing={{}: (4, {})} | custom-call | bytes 524288 | tf_op jit(solution)/shard_map/finish/pallas_call | solution.py:352
  85.9 1.0 %collective-permute-done.24.refs_3_ = bf16[1,112,512]{2,1,0:T(8,128)(2,1)S(1)} collective-permute-done((bf16[1,112,512]{2,1,0:T(8,128)(2,1)S(1)}, bf16[1,112,512]{2,1,0:T(8,128)(2,1)S(1)}, u32[]{:S(2)}, u32[]{:S(2)}) %collective-permute-start.24) | collective-permute-done | bytes 114720 | tf_op jit(solution)/shard_map/ppermute | solution.py:419
  86.8 0.8 finish.5._
  87.7 0.8 place.2._
  (52 shorter events, 6.7 us)
Async XLA Ops:
  0.0 9.8 %copy-start.1 = (f32[256]{0:T(256)S(1)}, f32[256]{0:T(256)}, u32[]{:S(2)}) copy-start(f32[256]{0:T(256)} %param.8) | copy-start | bytes 3076
  6.2 3.6 %collective-permute-start.8 = (bf16[2,112,256]{2,1,0:T(8,128)(2,1)S(1)}, bf16[2,112,256]{2,1,0:T(8,128)(2,1)S(1)}, u32[]{:S(2)}, u32[]{:S(2)}) collective-permute-start(bf16[2,112,256]{2,1,0:T(8,128)(2,1)S(1)} %get-tuple-element.13), channel_id=1, source_target_pairs={{0,1},{1,0},{2,3},{3,2},{4,5},{5,4},{6,7},{7,6},{8,9},{9,8},{10,11... | collective-permute-start | bytes 344072 | tf_op jit(solution)/shard_map/ppermute | solution.py:390
  6.8 4.7 %collective-permute-start = (bf16[2,144,256]{2,1,0:T(8,128)(2,1)S(1)}, bf16[2,144,256]{2,1,0:T(8,128)(2,1)S(1)}, u32[]{:S(2)}, u32[]{:S(2)}) collective-permute-start(bf16[2,144,256]{2,1,0:T(8,128)(2,1)S(1)} %get-tuple-element.11), channel_id=1, source_target_pairs={{0,1},{1,0},{2,3},{3,2},{4,5},{5,4},{6,7},{7,6},{8,9},{9,8},{10,11... | collective-permute-start | bytes 442376 | tf_op jit(solution)/shard_map/ppermute | solution.py:390
  6.9 44.5 %collective-permute-start.21 = (bf16[2,2,512,256]{3,2,1,0:T(8,128)(2,1)S(1)}, bf16[2,2,512,256]{3,2,1,0:T(8,128)(2,1)S(1)}, u32[]{:S(2)}, u32[]{:S(2)}) collective-permute-start(bf16[2,2,512,256]{3,2,1,0:T(8,128)(2,1)S(1)} %get-tuple-element.14), channel_id=1, source_target_pairs={{0,16},{16,0},{1,17},{17,1},{2,18},{18,2},{3,19},{19,3},{4,20},{20... | collective-permute-start | bytes 3145736 | tf_op jit(solution)/shard_map/ppermute | solution.py:385
  9.9 4.7 %collective-permute-start.9 = (bf16[112,256]{1,0:T(8,128)(2,1)S(1)}, bf16[112,256]{1,0:T(8,128)(2,1)S(1)}, u32[]{:S(2)}, u32[]{:S(2)}) collective-permute-start(bf16[112,256]{1,0:T(8,128)(2,1)S(1)} %fusion.5), channel_id=1, source_target_pairs={{0,2},{1,3},{2,0},{3,1},{4,6},{5,7},{6,4},{7,5},{8,10},{9,11},{10,... | collective-permute-start | bytes 172040 | tf_op jit(solution)/shard_map/ppermute | solution.py:392
  11.6 7.6 %collective-permute-start.1 = (bf16[144,256]{1,0:T(8,128)(2,1)S(1)}, bf16[144,256]{1,0:T(8,128)(2,1)S(1)}, u32[]{:S(2)}, u32[]{:S(2)}) collective-permute-start(bf16[144,256]{1,0:T(8,128)(2,1)S(1)} %fusion.3), channel_id=1, source_target_pairs={{0,2},{1,3},{2,0},{3,1},{4,6},{5,7},{6,4},{7,5},{8,10},{9,11},{10,... | collective-permute-start | bytes 221192 | tf_op jit(solution)/shard_map/ppermute | solution.py:392
  14.6 8.2 %collective-permute-start.12 = (bf16[112,256]{1,0:T(8,128)(2,1)S(1)}, bf16[112,256]{1,0:T(8,128)(2,1)S(1)}, u32[]{:S(2)}, u32[]{:S(2)}) collective-permute-start(bf16[112,256]{1,0:T(8,128)(2,1)S(1)} %fusion.4), channel_id=1, source_target_pairs={{0,12},{1,13},{2,14},{3,15},{4,8},{5,9},{6,10},{7,11},{8,4},{9,5},... | collective-permute-start | bytes 172040 | tf_op jit(solution)/shard_map/ppermute | solution.py:397
  18.3 7.6 %collective-permute-start.11 = (bf16[112,256]{1,0:T(8,128)(2,1)S(1)}, bf16[112,256]{1,0:T(8,128)(2,1)S(1)}, u32[]{:S(2)}, u32[]{:S(2)}) collective-permute-start(bf16[112,256]{1,0:T(8,128)(2,1)S(1)} %fusion.4), channel_id=1, source_target_pairs={{0,8},{1,9},{2,10},{3,11},{4,12},{5,13},{6,14},{7,15},{8,0},{9,1},... | collective-permute-start | bytes 172040 | tf_op jit(solution)/shard_map/ppermute | solution.py:397
  18.3 7.6 %collective-permute-start.10 = (bf16[112,256]{1,0:T(8,128)(2,1)S(1)}, bf16[112,256]{1,0:T(8,128)(2,1)S(1)}, u32[]{:S(2)}, u32[]{:S(2)}) collective-permute-start(bf16[112,256]{1,0:T(8,128)(2,1)S(1)} %fusion.4), channel_id=1, source_target_pairs={{0,4},{1,5},{2,6},{3,7},{4,0},{5,1},{6,2},{7,3},{8,12},{9,13},{10,... | collective-permute-start | bytes 172040 | tf_op jit(solution)/shard_map/ppermute | solution.py:397
  19.1 8.0 %collective-permute-start.4 = (bf16[144,256]{1,0:T(8,128)(2,1)S(1)}, bf16[144,256]{1,0:T(8,128)(2,1)S(1)}, u32[]{:S(2)}, u32[]{:S(2)}) collective-permute-start(bf16[144,256]{1,0:T(8,128)(2,1)S(1)} %fusion.2), channel_id=1, source_target_pairs={{0,12},{1,13},{2,14},{3,15},{4,8},{5,9},{6,10},{7,11},{8,4},{9,5},... | collective-permute-start | bytes 221192 | tf_op jit(solution)/shard_map/ppermute | solution.py:397
  22.8 6.3 %collective-permute-start.3 = (bf16[144,256]{1,0:T(8,128)(2,1)S(1)}, bf16[144,256]{1,0:T(8,128)(2,1)S(1)}, u32[]{:S(2)}, u32[]{:S(2)}) collective-permute-start(bf16[144,256]{1,0:T(8,128)(2,1)S(1)} %fusion.2), channel_id=1, source_target_pairs={{0,8},{1,9},{2,10},{3,11},{4,12},{5,13},{6,14},{7,15},{8,0},{9,1},... | collective-permute-start | bytes 221192 | tf_op jit(solution)/shard_map/ppermute | solution.py:397
  25.9 4.4 %collective-permute-start.2 = (bf16[144,256]{1,0:T(8,128)(2,1)S(1)}, bf16[144,256]{1,0:T(8,128)(2,1)S(1)}, u32[]{:S(2)}, u32[]{:S(2)}) collective-permute-start(bf16[144,256]{1,0:T(8,128)(2,1)S(1)} %fusion.2), channel_id=1, source_target_pairs={{0,4},{1,5},{2,6},{3,7},{4,0},{5,1},{6,2},{7,3},{8,12},{9,13},{10,... | collective-permute-start | bytes 221192 | tf_op jit(solution)/shard_map/ppermute | solution.py:397
  26.0 9.1 %collective-permute-start.17 = (bf16[112,256]{1,0:T(8,128)(2,1)S(1)}, bf16[112,256]{1,0:T(8,128)(2,1)S(1)}, u32[]{:S(2)}, u32[]{:S(2)}) collective-permute-start(bf16[112,256]{1,0:T(8,128)(2,1)S(1)} %multiply_convert_fusion.1.refs_4_.r00), channel_id=1, source_target_pairs={{0,16},{16,0},{1,17},{17,1},{2,18},{18,2},{3,19},{19,3},{4,20},{20... | collective-permute-start | bytes 172040 | tf_op jit(solution)/shard_map/ppermute | solution.py:401
  30.3 5.7 %collective-permute-start.16 = (bf16[144,256]{1,0:T(8,128)(2,1)S(1)}, bf16[144,256]{1,0:T(8,128)(2,1)S(1)}, u32[]{:S(2)}, u32[]{:S(2)}) collective-permute-start(bf16[144,256]{1,0:T(8,128)(2,1)S(1)} %multiply_convert_fusion.refs_0_.r00), channel_id=1, source_target_pairs={{0,16},{16,0},{1,17},{17,1},{2,18},{18,2},{3,19},{19,3},{4,20},{20... | collective-permute-start | bytes 221192 | tf_op jit(solution)/shard_map/ppermute | solution.py:401
  31.4 4.2 %collective-permute-start.13 = (bf16[112,256]{1,0:T(8,128)(2,1)S(1)}, bf16[112,256]{1,0:T(8,128)(2,1)S(1)}, u32[]{:S(2)}, u32[]{:S(2)}) collective-permute-start(bf16[112,256]{1,0:T(8,128)(2,1)S(1)} %multiply_convert_fusion.1.refs_4_.r00), channel_id=1, source_target_pairs={{0,2},{1,3},{2,0},{3,1},{4,6},{5,7},{6,4},{7,5},{8,10},{9,11},{10,... | collective-permute-start | bytes 172040 | tf_op jit(solution)/shard_map/ppermute | solution.py:399
  33.3 4.5 %collective-permute-start.5 = (bf16[144,256]{1,0:T(8,128)(2,1)S(1)}, bf16[144,256]{1,0:T(8,128)(2,1)S(1)}, u32[]{:S(2)}, u32[]{:S(2)}) collective-permute-start(bf16[144,256]{1,0:T(8,128)(2,1)S(1)} %multiply_convert_fusion.refs_0_.r00), channel_id=1, source_target_pairs={{0,2},{1,3},{2,0},{3,1},{4,6},{5,7},{6,4},{7,5},{8,10},{9,11},{10,... | collective-permute-start | bytes 221192 | tf_op jit(solution)/shard_map/ppermute | solution.py:399
  35.1 2.8 %collective-permute-start.14 = (bf16[112,256]{1,0:T(8,128)(2,1)S(1)}, bf16[112,256]{1,0:T(8,128)(2,1)S(1)}, u32[]{:S(2)}, u32[]{:S(2)}) collective-permute-start(bf16[112,256]{1,0:T(8,128)(2,1)S(1)} %multiply_convert_fusion.1.refs_4_.r00), channel_id=1, source_target_pairs={{0,1},{1,0},{2,3},{3,2},{4,5},{5,4},{6,7},{7,6},{8,9},{9,8},{10,11... | collective-permute-start | bytes 172040 | tf_op jit(solution)/shard_map/ppermute | solution.py:405
  35.6 2.7 %collective-permute-start.15 = (bf16[112,256]{1,0:T(8,128)(2,1)S(1)}, bf16[112,256]{1,0:T(8,128)(2,1)S(1)}, u32[]{:S(2)}, u32[]{:S(2)}) collective-permute-start(bf16[112,256]{1,0:T(8,128)(2,1)S(1)} %collective-permute-done.13.refs_5_.r01), channel_id=1, source_target_pairs={{0,1},{1,0},{2,3},{3,2},{4,5},{5,4},{6,7},{7,6},{8,9},{9,8},{10,11... | collective-permute-start | bytes 172040 | tf_op jit(solution)/shard_map/ppermute | solution.py:405
  36.0 12.2 %collective-permute-start.18 = (bf16[256,256]{1,0:T(8,128)(2,1)S(1)}, bf16[256,256]{1,0:T(8,128)(2,1)S(1)}, u32[]{:S(2)}, u32[]{:S(2)}) collective-permute-start(bf16[256,256]{1,0:T(8,128)(2,1)S(1)} %join.1.refs_8_), channel_id=1, source_target_pairs={{0,2},{1,3},{2,0},{3,1},{4,6},{5,7},{6,4},{7,5},{8,10},{9,11},{10,... | collective-permute-start | bytes 393224 | tf_op jit(solution)/shard_map/ppermute | solution.py:426
  37.8 6.6 %collective-permute-start.6 = (bf16[144,256]{1,0:T(8,128)(2,1)S(1)}, bf16[144,256]{1,0:T(8,128)(2,1)S(1)}, u32[]{:S(2)}, u32[]{:S(2)}) collective-permute-start(bf16[144,256]{1,0:T(8,128)(2,1)S(1)} %multiply_convert_fusion.refs_0_.r00), channel_id=1, source_target_pairs={{0,1},{1,0},{2,3},{3,2},{4,5},{5,4},{6,7},{7,6},{8,9},{9,8},{10,11... | collective-permute-start | bytes 221192 | tf_op jit(solution)/shard_map/ppermute | solution.py:405
  37.8 8.2 %collective-permute-start.7 = (bf16[144,256]{1,0:T(8,128)(2,1)S(1)}, bf16[144,256]{1,0:T(8,128)(2,1)S(1)}, u32[]{:S(2)}, u32[]{:S(2)}) collective-permute-start(bf16[144,256]{1,0:T(8,128)(2,1)S(1)} %collective-permute-done.5.refs_1_.r01), channel_id=1, source_target_pairs={{0,1},{1,0},{2,3},{3,2},{4,5},{5,4},{6,7},{7,6},{8,9},{9,8},{10,11... | collective-permute-start | bytes 221192 | tf_op jit(solution)/shard_map/ppermute | solution.py:405
  38.3 11.5 %collective-permute-start.19 = (bf16[256,256]{1,0:T(8,128)(2,1)S(1)}, bf16[256,256]{1,0:T(8,128)(2,1)S(1)}, u32[]{:S(2)}, u32[]{:S(2)}) collective-permute-start(bf16[256,256]{1,0:T(8,128)(2,1)S(1)} %join.1.refs_8_), channel_id=1, source_target_pairs={{0,1},{1,0},{2,3},{3,2},{4,5},{5,4},{6,7},{7,6},{8,9},{9,8},{10,11... | collective-permute-start | bytes 393224 | tf_op jit(solution)/shard_map/ppermute | solution.py:405
  40.6 2.2 %copy-start = (s32[2,8]{1,0:T(2,128)S(1)}, s32[2,8]{1,0:T(2,128)}, u32[]{:S(2)}) copy-start(s32[2,8]{1,0:T(2,128)} %ranks.13) | copy-start | bytes 196
  44.4 13.1 %collective-permute-start.27 = (bf16[3,112,512]{2,1,0:T(8,128)(2,1)S(1)}, bf16[3,112,512]{2,1,0:T(8,128)(2,1)S(1)}, u32[]{:S(2)}, u32[]{:S(2)}) collective-permute-start(bf16[3,112,512]{2,1,0:T(8,128)(2,1)S(1)} %adjoint.9.refs_2_), channel_id=1, source_target_pairs={{0,16},{16,0},{1,17},{17,1},{2,18},{18,2},{3,19},{19,3},{4,20},{20... | collective-permute-start | bytes 1032200 | tf_op jit(solution)/shard_map/ppermute | solution.py:419
  47.6 17.3 %collective-permute-start.26 = (bf16[3,144,512]{2,1,0:T(8,128)(2,1)S(1)}, bf16[3,144,512]{2,1,0:T(8,128)(2,1)S(1)}, u32[]{:S(2)}, u32[]{:S(2)}) collective-permute-start(bf16[3,144,512]{2,1,0:T(8,128)(2,1)S(1)} %adjoint.8.refs_0_), channel_id=1, source_target_pairs={{0,16},{16,0},{1,17},{17,1},{2,18},{18,2},{3,19},{19,3},{4,20},{20... | collective-permute-start | bytes 1327112 | tf_op jit(solution)/shard_map/ppermute | solution.py:419
  48.2 3.2 %collective-permute-start.20 = (bf16[256,256]{1,0:T(8,128)(2,1)S(1)}, bf16[256,256]{1,0:T(8,128)(2,1)S(1)}, u32[]{:S(2)}, u32[]{:S(2)}) collective-permute-start(bf16[256,256]{1,0:T(8,128)(2,1)S(1)} %collective-permute-done.18.refs_9_), channel_id=1, source_target_pairs={{0,1},{1,0},{2,3},{3,2},{4,5},{5,4},{6,7},{7,6},{8,9},{9,8},{10,11... | collective-permute-start | bytes 393224 | tf_op jit(solution)/shard_map/ppermute | solution.py:405
  49.8 35.1 %collective-permute-start.23 = (bf16[3,144,512]{2,1,0:T(8,128)(2,1)S(1)}, bf16[3,144,512]{2,1,0:T(8,128)(2,1)S(1)}, u32[]{:S(2)}, u32[]{:S(2)}) collective-permute-start(bf16[3,144,512]{2,1,0:T(8,128)(2,1)S(1)} %adjoint.5.refs_0_), channel_id=1, source_target_pairs={{0,16},{16,0},{1,17},{17,1},{2,18},{18,2},{3,19},{19,3},{4,20},{20... | collective-permute-start | bytes 1327112 | tf_op jit(solution)/shard_map/ppermute | solution.py:419
  53.1 35.4 %collective-permute-start.22 = (bf16[256,512]{1,0:T(8,128)(2,1)S(1)}, bf16[256,512]{1,0:T(8,128)(2,1)S(1)}, u32[]{:S(2)}, u32[]{:S(2)}) collective-permute-start(bf16[256,512]{1,0:T(8,128)(2,1)S(1)} %pair.1.g_ref), channel_id=1, source_target_pairs={{0,16},{16,0},{1,17},{17,1},{2,18},{18,2},{3,19},{19,3},{4,20},{20... | collective-permute-start | bytes 786440 | tf_op jit(solution)/shard_map/ppermute | solution.py:429
  54.9 30.0 %collective-permute-start.25 = (bf16[2,112,512]{2,1,0:T(8,128)(2,1)S(1)}, bf16[2,112,512]{2,1,0:T(8,128)(2,1)S(1)}, u32[]{:S(2)}, u32[]{:S(2)}) collective-permute-start(bf16[2,112,512]{2,1,0:T(8,128)(2,1)S(1)} %adjoint.7.refs_2_), channel_id=1, source_target_pairs={{0,16},{16,0},{1,17},{17,1},{2,18},{18,2},{3,19},{19,3},{4,20},{20... | collective-permute-start | bytes 688136 | tf_op jit(solution)/shard_map/ppermute | solution.py:419
  57.5 29.3 %collective-permute-start.24 = (bf16[1,112,512]{2,1,0:T(8,128)(2,1)S(1)}, bf16[1,112,512]{2,1,0:T(8,128)(2,1)S(1)}, u32[]{:S(2)}, u32[]{:S(2)}) collective-permute-start(bf16[1,112,512]{2,1,0:T(8,128)(2,1)S(1)} %adjoint.6.refs_2_), channel_id=1, source_target_pairs={{0,16},{16,0},{1,17},{17,1},{2,18},{18,2},{3,19},{19,3},{4,20},{20... | collective-permute-start | bytes 344072 | tf_op jit(solution)/shard_map/ppermute | solution.py:419

commit v5 on v4

--- a/solution.py
+++ b/solution.py
@@ -11,8 +11,8 @@
 
 BF = jnp.bfloat16
 F32 = jnp.float32
-CUTS = (144, 112)
-GROUPS = ((3, 3), (3, 2, 1))
+CUTS = (128, 128)
+GROUPS = ((3, 3), (3, 3))
 VMEM_LIMIT = 26 * 2**20
 IN_VMEM = pl.BlockSpec(memory_space=pltpu.VMEM)
 IN_SMEM = pl.BlockSpec(memory_space=pltpu.SMEM)
@@ -54,18 +54,21 @@
         return [pltpu.make_async_copy(src, dst, sems.at[j, base + k]) for k, (src, dst) in enumerate(pairs)]
 
     jb = 2 if tile_cols % 2 == 0 else 1
-    steps = list(range(0, tile_cols, jb))[::-1]
-    for j0 in steps:
-        for j in range(j0, j0 + jb):
+    steps = [tuple(range(j, j + jb)) for j in range(0, tile_cols, jb)][::-1]
+    if jb == 2:
+        steps[-1:] = [(1,), (0,)]
+    for step in steps:
+        for j in step:
             for c in copies(j, True) + copies(j, False):
                 c.start()
 
     mine, my_x, my_z = position()
     lane = lax.broadcasted_iota(jnp.int32, (sources, cap), 1)
     early_copies = []
-    for j0 in steps:
+    last = []
+    for step in steps:
         parts = [[] for _ in range(tile_rows)]
-        for j in range(j0, j0 + jb):
+        for j in step:
             for c in copies(j, True) + copies(j, False):
                 c.wait()
             xt = x_vm[j * width : (j + 1) * width, :].T
@@ -73,13 +76,15 @@
                 c = dot_nn(xt, v_vm[a, j])
                 parts[a].append(jnp.where(lane < ranks[a, j], c, 0.0).astype(BF))
         for a in range(tile_rows):
-            w = jnp.concatenate([permuted_rows(u_vm[a, j], zs, rb) for j in range(j0, j0 + jb)], axis=1)
+            w = jnp.concatenate([permuted_rows(u_vm[a, j], zs, rb) for j in step], axis=1)
             p = dot_nt(jnp.concatenate(parts[a], axis=1), w)
-            if j0 == steps[0]:
+            if step == steps[0]:
                 acc[a] = p
+            elif step == steps[-1]:
+                last.append(p)
             else:
                 acc[a] += p
-        if shared and j0 == steps[0]:
+        if shared and step == steps[0]:
             early, masked, early_sems = rest[2 * n : 2 * n + 3]
             col = tile_cols - 1 - lax.axis_index("row")
             rank_lane = lax.broadcasted_iota(jnp.int32, (width, cap), 1)
@@ -102,7 +107,12 @@
         row = 0
         for i, s in enumerate(cuts):
             val = jnp.concatenate(
-                [acc[a, row : row + s, q * q_lanes : (q + 1) * q_lanes] for a in range(tile_rows)], axis=1
+                [
+                    acc[a, row : row + s, q * q_lanes : (q + 1) * q_lanes]
+                    + last[a][row : row + s, q * q_lanes : (q + 1) * q_lanes]
+                    for a in range(tile_rows)
+                ],
+                axis=1,
             )
 
             @pl.when(mine == qc)
@@ -291,14 +301,44 @@
     )(*parts)
 
 
-def place_kernel(tile_cols, flip, g_ref, _, out, buf, sem):
+def interleave_kernel(cuts, own, rest, out):
+    odd = lax.rem(lax.div(lax.axis_index("col"), 4), 2)
+    row = 0
+    for s in cuts:
+        half = s // 2
+        span = slice(row // 2, row // 2 + half)
+        out[pl.ds(pl.multiple_of(row + odd * half, 16), half)] = own[span]
+        out[pl.ds(pl.multiple_of(row + (1 - odd) * half, 16), half)] = rest[span]
+        row += s
+
+
+def interleave(own, rest, cuts):
+    shape = (2 * own.shape[0], own.shape[1])
+    return pl.pallas_call(
+        functools.partial(interleave_kernel, cuts),
+        in_specs=[IN_VMEM] * 2,
+        out_specs=IN_VMEM,
+        out_shape=pltpu.VMEM(shape, BF),
+        compiler_params=pltpu.CompilerParams(vmem_limit_bytes=VMEM_LIMIT),
+        cost_estimate=pl.CostEstimate(flops=0, bytes_accessed=4 * shape[0] * shape[1], transcendentals=0),
+        name="interleave",
+    )(own, rest)
+
+
+def place_kernel(tile_cols, flip, g_ref, _, out, buf, sems):
     row = lax.axis_index("row")
     width = buf.shape[0]
     col = tile_cols - 2 + (1 - row if flip else row)
-    buf[...] = g_ref[...].T
-    copy = pltpu.make_async_copy(buf, out.at[pl.ds(pl.multiple_of(col * width, width), width)], sem)
-    copy.start()
-    copy.wait()
+    part = width // 2
+    copies = []
+    for k in range(2):
+        span = slice(k * part, (k + 1) * part)
+        buf[span] = g_ref[:, span].T
+        to = pl.ds(pl.multiple_of(col * width + k * part, part), part)
+        copies.append(pltpu.make_async_copy(buf.at[span], out.at[to], sems.at[k]))
+        copies[-1].start()
+    for copy in copies:
+        copy.wait()
 
 
 def place(out, column, tile_cols, flip):
@@ -308,7 +348,7 @@
         in_specs=[IN_VMEM, IN_HBM],
         out_specs=IN_HBM,
         out_shape=jax.ShapeDtypeStruct(out.shape, BF),
-        scratch_shapes=[pltpu.VMEM((width, sources), BF), pltpu.SemaphoreType.DMA],
+        scratch_shapes=[pltpu.VMEM((width, sources), BF), pltpu.SemaphoreType.DMA((2,))],
         input_output_aliases={1: 0},
         compiler_params=pltpu.CompilerParams(vmem_limit_bytes=VMEM_LIMIT),
         cost_estimate=pl.CostEstimate(flops=0, bytes_accessed=2 * sources * width, transcendentals=0),
@@ -378,6 +418,7 @@
         zs = nz // tile_rows
         cuts = tuple(c * sources // 256 for c in CUTS)
         sat = sat_scale[:, None]
+        odd = lax.rem(lax.div(lax.axis_index("col"), 4), 2) == 1
         shared = n_row == 2
         keeps, sends, early = forward(x_field, observed, u, v, ranks, cuts, zs, shared)
         cols = tile_cols - 2 if shared else tile_cols
@@ -398,7 +439,8 @@
             r00 = (sc * jnp.tanh(total / sc)).astype(BF)
             r01 = lax.ppermute(r00, "col", x_swap)
             if shared:
-                other.append(lax.ppermute(r00, "row", row_swap))
+                part = jnp.where(odd, r00[r00.shape[0] // 2 :], r00[: r00.shape[0] // 2]) if nz > 1 else r00
+                other.append(lax.ppermute(part, "row", row_swap))
             return (r00, r01) + gather(r00, r01)
 
         def gather(r00, r01):
@@ -423,6 +465,9 @@
                 start += per
         if shared:
             r00 = join(other)
+            if nz > 1:
+                rest = lax.ppermute(r00, "col", z_swaps[0])
+                r00 = interleave(r00, rest, cuts)
             r01 = lax.ppermute(r00, "col", x_swap)
             blocks = (r00, r01) + gather(r00, r01)
             column = pair_column(resids, blocks, theirs, u, v, ranks, rb, zs)

time: 89.6 us -> 95.5 us (1.066)
  waiting for transfers between devices: 38.1 us -> 43.9 us
  Pallas kernels: 23.8 us -> 22.2 us
  starting transfers between devices: 26.9 us -> 28.5 us
    ppermute x1, waiting for transfers between devices: 0.01 us -> 3.23 us  [local(): column_got = lax.ppermute(column, 'row', row_swap)]
    ppermute x2, waiting for transfers between devices: 0.56 us -> 3.63 us  [residual(): r01 = lax.ppermute(r00, 'col', x_swap)]
    ppermute x5 -> x4, waiting for transfers between devices: 26.8 us -> 23.8 us  [local(): swapped[i].append((start, part, lax.ppermute(part, 'row', row_swap)))]
    ppermute x2 -> x3, waiting for transfers between devices: 1.99 us -> 4.12 us  [the longest x2 3.15 us: residual(): other.append(lax.ppermute(part, 'row', row_swap))]
    ppermute x2 -> x3, starting transfers between devices: 2.18 us -> 4.12 us  [the longest x2 2.32 us: residual(): other.append(lax.ppermute(part, 'row', row_swap))]
    ppermute x5 -> x4, starting transfers between devices: 5.91 us -> 4.25 us  [local(): swapped[i].append((start, part, lax.ppermute(part, 'row', row_swap)))]
    ppermute x1, starting transfers between devices: 0.56 us -> 1.81 us  [local(): column_got = lax.ppermute(column, 'row', row_swap)]
    pallas_call x3 -> x2, Pallas kernels: 2.8 us -> 2.05 us  [finish(): pl.pallas_call(functools.partial(finish_kernel, plan, start), in_specs=sp...]
  transfers between devices with their start and end apart: 28 -> 28, of which waited for: 10 -> 14; matrix products, arithmetic and copies ran while one was open for 0% -> 0% of each run, Pallas kernels for 19% -> 16%
where the time goes in v5:
time: 95.5 us; the launch traced here: 95.2 us
  waiting for transfers between devices  43.9 us (46%)
  starting transfers between devices  28.5 us (30%)
  Pallas kernels  22.2 us (23%)
    ppermute x4, waiting for transfers between devices, local(): swapped[i].append((start, part, lax.ppermute(part, 'row', row_swap)))  23.8 us
    ppermute x6, starting transfers between devices, residual(): total = total + lax.ppermute(mine, 'col', p).astype(F32)  8.21 us
    pallas_call x4, Pallas kernels, adjoint(): pl.pallas_call(functools.partial(adjoint_kernel, dims), in_specs=[IN_SMEM...  6.28 us
    pallas_call x1, Pallas kernels, forward(): pl.pallas_call(functools.partial(forward_kernel, dims), in_specs=[IN_SMEM...  6.22 us
    ppermute x6, waiting for transfers between devices, residual(): total = total + lax.ppermute(mine, 'col', p).astype(F32)  5.89 us
    pallas_call x2, Pallas kernels, hold(): pl.pallas_call(hold_kernel, in_specs=[IN_HBM], out_specs=pl.BlockSpec(mem...  4.4 us
    ppermute x4, starting transfers between devices, local(): swapped[i].append((start, part, lax.ppermute(part, 'row', row_swap)))  4.25 us
    ppermute x2, waiting for transfers between devices, residual(): r01 = lax.ppermute(r00, 'col', x_swap)  3.63 us
  transfers between devices with their start and end apart: 28, of which 14 were waited for; matrix products, arithmetic and copies ran while one was open for 0% of the time, Pallas kernels for 16%

profile of v5, /device:TPU:0, one launch (start us, length us, event | category | flops | bytes accessed | tf_op | source)
XLA Modules:
  0.0 95.2 jit_solution(9228251606657127051)
XLA Ops:
  0.0 6.2 %forward.1 = (f32[2,128,256]{2,1,0:T(8,128)S(1)}, f32[2,128,256]{2,1,0:T(8,128)S(1)}, bf16[2,128,256]{2,1,0:T(8,128)(2,1)S(1)}, bf16[2,128,256]{2,1,0:T(8,128)(2,1)S(1)}, bf16[2,2,512,256]{3,2,1,0:T(8,128)(2,1)S(1)}) custom-call(s32[2,8]{1,0:T(2,128)} %ranks.11, bf16[64,256]{1,0:T(8,128)(2,1)} %obs.1, bf16[4096,256]{1,0:T(8,128)(2,1)} %x_hbm.1, ...), custom_call_target="tpu_custom_call" | custom-call | flops 2147483648 | bytes 10485760 | tf_op jit(solution)/shard_map/forward/pallas_call | solution.py:146
  6.9 2.9 %collective-permute-start.22 = (bf16[2,2,512,256]{3,2,1,0:T(8,128)(2,1)S(1)}, bf16[2,2,512,256]{3,2,1,0:T(8,128)(2,1)S(1)}, u32[]{:S(2)}, u32[]{:S(2)}) collective-permute-start(bf16[2,2,512,256]{3,2,1,0:T(8,128)(2,1)S(1)} %get-tuple-element.14), channel_id=1, source_target_pairs={{0,16},{16,0},{1,17},{17,1},{2,18},{18,2},{3,19},{19,3},{4,20},{20... | collective-permute-start | bytes 3145736 | tf_op jit(solution)/shard_map/ppermute | solution.py:426
  9.9 1.6 %collective-permute-start.1 = (bf16[128,256]{1,0:T(8,128)(2,1)S(1)}, bf16[128,256]{1,0:T(8,128)(2,1)S(1)}, u32[]{:S(2)}, u32[]{:S(2)}) collective-permute-start(bf16[128,256]{1,0:T(8,128)(2,1)S(1)} %fusion.4), channel_id=1, source_target_pairs={{0,2},{1,3},{2,0},{3,1},{4,6},{5,7},{6,4},{7,5},{8,10},{9,11},{10,... | collective-permute-start | bytes 196616 | tf_op jit(solution)/shard_map/ppermute | solution.py:433
  12.1 2.7 %collective-permute-done.1 = bf16[128,256]{1,0:T(8,128)(2,1)S(1)} collective-permute-done((bf16[128,256]{1,0:T(8,128)(2,1)S(1)}, bf16[128,256]{1,0:T(8,128)(2,1)S(1)}, u32[]{:S(2)}, u32[]{:S(2)}) %collective-permute-start.1) | collective-permute-done | bytes 65568 | tf_op jit(solution)/shard_map/ppermute | solution.py:433
  14.8 3.7 %collective-permute-start.4 = (bf16[128,256]{1,0:T(8,128)(2,1)S(1)}, bf16[128,256]{1,0:T(8,128)(2,1)S(1)}, u32[]{:S(2)}, u32[]{:S(2)}) collective-permute-start(bf16[128,256]{1,0:T(8,128)(2,1)S(1)} %fusion.2), channel_id=1, source_target_pairs={{0,12},{1,13},{2,14},{3,15},{4,8},{5,9},{6,10},{7,11},{8,4},{9,5},... | collective-permute-start | bytes 196616 | tf_op jit(solution)/shard_map/ppermute | solution.py:438
  19.2 3.7 %collective-permute-start.12 = (bf16[128,256]{1,0:T(8,128)(2,1)S(1)}, bf16[128,256]{1,0:T(8,128)(2,1)S(1)}, u32[]{:S(2)}, u32[]{:S(2)}) collective-permute-start(bf16[128,256]{1,0:T(8,128)(2,1)S(1)} %fusion.3), channel_id=1, source_target_pairs={{0,12},{1,13},{2,14},{3,15},{4,8},{5,9},{6,10},{7,11},{8,4},{9,5},... | collective-permute-start | bytes 196616 | tf_op jit(solution)/shard_map/ppermute | solution.py:438
  23.0 2.9 %collective-permute-done.3 = bf16[128,256]{1,0:T(8,128)(2,1)S(1)} collective-permute-done((bf16[128,256]{1,0:T(8,128)(2,1)S(1)}, bf16[128,256]{1,0:T(8,128)(2,1)S(1)}, u32[]{:S(2)}, u32[]{:S(2)}) %collective-permute-start.3) | collective-permute-done | bytes 65568 | tf_op jit(solution)/shard_map/ppermute | solution.py:438
  26.0 1.2 %collective-permute-start.16 = (bf16[64,256]{1,0:T(8,128)(2,1)S(1)}, bf16[64,256]{1,0:T(8,128)(2,1)S(1)}, u32[]{:S(2)}, u32[]{:S(2)}) collective-permute-start(bf16[64,256]{1,0:T(8,128)(2,1)S(1)} %slice_select_fusion.1), channel_id=1, source_target_pairs={{0,16},{16,0},{1,17},{17,1},{2,18},{18,2},{3,19},{19,3},{4,20},{20... | collective-permute-start | bytes 98312 | tf_op jit(solution)/shard_map/ppermute | solution.py:443
  27.2 1.7 %collective-permute-done.11 = bf16[128,256]{1,0:T(8,128)(2,1)S(1)} collective-permute-done((bf16[128,256]{1,0:T(8,128)(2,1)S(1)}, bf16[128,256]{1,0:T(8,128)(2,1)S(1)}, u32[]{:S(2)}, u32[]{:S(2)}) %collective-permute-start.11) | collective-permute-done | bytes 65568 | tf_op jit(solution)/shard_map/ppermute | solution.py:438
  28.9 1.3 %collective-permute-done.10 = bf16[128,256]{1,0:T(8,128)(2,1)S(1)} collective-permute-done((bf16[128,256]{1,0:T(8,128)(2,1)S(1)}, bf16[128,256]{1,0:T(8,128)(2,1)S(1)}, u32[]{:S(2)}, u32[]{:S(2)}) %collective-permute-start.10) | collective-permute-done | bytes 65568 | tf_op jit(solution)/shard_map/ppermute | solution.py:438
  30.3 1.2 %collective-permute-start.17 = (bf16[64,256]{1,0:T(8,128)(2,1)S(1)}, bf16[64,256]{1,0:T(8,128)(2,1)S(1)}, u32[]{:S(2)}, u32[]{:S(2)}) collective-permute-start(bf16[64,256]{1,0:T(8,128)(2,1)S(1)} %slice_select_fusion), channel_id=1, source_target_pairs={{0,16},{16,0},{1,17},{17,1},{2,18},{18,2},{3,19},{19,3},{4,20},{20... | collective-permute-start | bytes 98312 | tf_op jit(solution)/shard_map/ppermute | solution.py:443
  31.5 2.8 %collective-permute-done.16.refs_0_ = bf16[64,256]{1,0:T(8,128)(2,1)S(1)} collective-permute-done((bf16[64,256]{1,0:T(8,128)(2,1)S(1)}, bf16[64,256]{1,0:T(8,128)(2,1)S(1)}, u32[]{:S(2)}, u32[]{:S(2)}) %collective-permute-start.16) | collective-permute-done | bytes 32800 | tf_op jit(solution)/shard_map/ppermute | solution.py:443
  34.6 1.8 %collective-permute-start.18 = (bf16[128,256]{1,0:T(8,128)(2,1)S(1)}, bf16[128,256]{1,0:T(8,128)(2,1)S(1)}, u32[]{:S(2)}, u32[]{:S(2)}) collective-permute-start(bf16[128,256]{1,0:T(8,128)(2,1)S(1)} %join.1.own), channel_id=1, source_target_pairs={{0,4},{1,5},{2,6},{3,7},{4,0},{5,1},{6,2},{7,3},{8,12},{9,13},{10,... | collective-permute-start | bytes 196616 | tf_op jit(solution)/shard_map/ppermute | solution.py:469
  36.4 1.5 %collective-permute-start.5 = (bf16[128,256]{1,0:T(8,128)(2,1)S(1)}, bf16[128,256]{1,0:T(8,128)(2,1)S(1)}, u32[]{:S(2)}, u32[]{:S(2)}) collective-permute-start(bf16[128,256]{1,0:T(8,128)(2,1)S(1)} %multiply_convert_fusion.1.refs_0_.r00), channel_id=1, source_target_pairs={{0,2},{1,3},{2,0},{3,1},{4,6},{5,7},{6,4},{7,5},{8,10},{9,11},{10,... | collective-permute-start | bytes 196616 | tf_op jit(solution)/shard_map/ppermute | solution.py:440
  38.9 1.8 %collective-permute-start.19 = (bf16[256,256]{1,0:T(8,128)(2,1)S(1)}, bf16[256,256]{1,0:T(8,128)(2,1)S(1)}, u32[]{:S(2)}, u32[]{:S(2)}) collective-permute-start(bf16[256,256]{1,0:T(8,128)(2,1)S(1)} %interleave.1.refs_8_), channel_id=1, source_target_pairs={{0,2},{1,3},{2,0},{3,1},{4,6},{5,7},{6,4},{7,5},{8,10},{9,11},{10,... | collective-permute-start | bytes 393224 | tf_op jit(solution)/shard_map/ppermute | solution.py:471
  42.1 3.2 %collective-permute-done.13.refs_5_.r01 = bf16[128,256]{1,0:T(8,128)(2,1)S(1)} collective-permute-done((bf16[128,256]{1,0:T(8,128)(2,1)S(1)}, bf16[128,256]{1,0:T(8,128)(2,1)S(1)}, u32[]{:S(2)}, u32[]{:S(2)}) %collective-permute-start.13) | collective-permute-done | bytes 65568 | tf_op jit(solution)/shard_map/ppermute | solution.py:440
  45.3 2.2 %hold.2.refs_13_.u_ref = bf16[2,8,512,256]{3,2,1,0:T(8,128)(2,1)S(1)} custom-call(bf16[2,8,512,256]{3,2,1,0:T(8,128)(2,1)} %src.2), custom_call_target="tpu_custom_call" | custom-call | bytes 4194304 | tf_op jit(solution)/shard_map/hold/pallas_call | solution.py:179
  47.6 2.2 %hold.3.refs_14_.v_ref = bf16[2,8,512,256]{3,2,1,0:T(8,128)(2,1)S(1)} custom-call(bf16[2,8,512,256]{3,2,1,0:T(8,128)(2,1)} %src.3), custom_call_target="tpu_custom_call" | custom-call | bytes 4194304 | tf_op jit(solution)/shard_map/hold/pallas_call | solution.py:179
  50.4 1.6 %adjoint.6.refs_0_ = bf16[3,128,512]{2,1,0:T(8,128)(2,1)S(1)} custom-call(s32[2,8]{1,0:T(2,128)S(1)} %copy-done, bf16[128,256]{1,0:T(8,128)(2,1)S(1)} %multiply_convert_fusion.1.refs_0_.r00, bf16[128,256]{1,0:T(8,128)(2,1)S(1)} %collective-permute-done.5.refs_1_.r01, bf16[128,256]{1,0:T(8,128)(2,1)S(1)} %collective-permute-done.6.refs_2_.r10, ...), custom_call_target="tpu_custom_call" | custom-call | flops 402653184 | bytes 131072 | tf_op jit(solution)/shard_map/adjoint/pallas_call | solution.py:219
  52.0 1.8 %collective-permute-start.26 = (bf16[3,128,512]{2,1,0:T(8,128)(2,1)S(1)}, bf16[3,128,512]{2,1,0:T(8,128)(2,1)S(1)}, u32[]{:S(2)}, u32[]{:S(2)}) collective-permute-start(bf16[3,128,512]{2,1,0:T(8,128)(2,1)S(1)} %adjoint.6.refs_0_), channel_id=1, source_target_pairs={{0,16},{16,0},{1,17},{17,1},{2,18},{18,2},{3,19},{19,3},{4,20},{20... | collective-permute-start | bytes 1179656 | tf_op jit(solution)/shard_map/ppermute | solution.py:461
  53.8 1.6 %adjoint.7.refs_2_ = bf16[3,128,512]{2,1,0:T(8,128)(2,1)S(1)} custom-call(s32[2,8]{1,0:T(2,128)S(1)} %copy-done, bf16[128,256]{1,0:T(8,128)(2,1)S(1)} %multiply_convert_fusion.refs_4_.r00, bf16[128,256]{1,0:T(8,128)(2,1)S(1)} %collective-permute-done.13.refs_5_.r01, bf16[128,256]{1,0:T(8,128)(2,1)S(1)} %collective-permute-done.14.refs_6_.r10, ...), custom_call_target="tpu_custom_call" | custom-call | flops 402653184 | bytes 131072 | tf_op jit(solution)/shard_map/adjoint/pallas_call | solution.py:219
  55.8 1.6 %adjoint.5.refs_2_ = bf16[3,128,512]{2,1,0:T(8,128)(2,1)S(1)} custom-call(s32[2,8]{1,0:T(2,128)S(1)} %copy-done, bf16[128,256]{1,0:T(8,128)(2,1)S(1)} %multiply_convert_fusion.refs_4_.r00, bf16[128,256]{1,0:T(8,128)(2,1)S(1)} %collective-permute-done.13.refs_5_.r01, bf16[128,256]{1,0:T(8,128)(2,1)S(1)} %collective-permute-done.14.refs_6_.r10, ...), custom_call_target="tpu_custom_call" | custom-call | flops 402653184 | bytes 131072 | tf_op jit(solution)/shard_map/adjoint/pallas_call | solution.py:219
  57.3 1.6 %adjoint.4.refs_0_ = bf16[3,128,512]{2,1,0:T(8,128)(2,1)S(1)} custom-call(s32[2,8]{1,0:T(2,128)S(1)} %copy-done, bf16[128,256]{1,0:T(8,128)(2,1)S(1)} %multiply_convert_fusion.1.refs_0_.r00, bf16[128,256]{1,0:T(8,128)(2,1)S(1)} %collective-permute-done.5.refs_1_.r01, bf16[128,256]{1,0:T(8,128)(2,1)S(1)} %collective-permute-done.6.refs_2_.r10, ...), custom_call_target="tpu_custom_call" | custom-call | flops 402653184 | bytes 131072 | tf_op jit(solution)/shard_map/adjoint/pallas_call | solution.py:219
  58.9 1.8 %collective-permute-start.24 = (bf16[3,128,512]{2,1,0:T(8,128)(2,1)S(1)}, bf16[3,128,512]{2,1,0:T(8,128)(2,1)S(1)}, u32[]{:S(2)}, u32[]{:S(2)}) collective-permute-start(bf16[3,128,512]{2,1,0:T(8,128)(2,1)S(1)} %adjoint.4.refs_0_), channel_id=1, source_target_pairs={{0,16},{16,0},{1,17},{17,1},{2,18},{18,2},{3,19},{19,3},{4,20},{20... | collective-permute-start | bytes 1179656 | tf_op jit(solution)/shard_map/ppermute | solution.py:461
  61.0 1.7 %pair.1.g_ref = bf16[256,512]{1,0:T(8,128)(2,1)S(1)} custom-call(s32[2,8]{1,0:T(2,128)S(1)} %copy-done, bf16[128,256]{1,0:T(8,128)(2,1)S(1)} %multiply_convert_fusion.1.refs_0_.r00, bf16[128,256]{1,0:T(8,128)(2,1)S(1)} %collective-permute-done.5.refs_1_.r01, bf16[128,256]{1,0:T(8,128)(2,1)S(1)} %collective-permute-done.6.refs_2_.r10, ...), custom_call_target="tpu_custom_call" | custom-call | flops 536870912 | bytes 262144 | tf_op jit(solution)/shard_map/pair/pallas_call | solution.py:270
  62.7 1.8 %collective-permute-start.23 = (bf16[256,512]{1,0:T(8,128)(2,1)S(1)}, bf16[256,512]{1,0:T(8,128)(2,1)S(1)}, u32[]{:S(2)}, u32[]{:S(2)}) collective-permute-start(bf16[256,512]{1,0:T(8,128)(2,1)S(1)} %pair.1.g_ref), channel_id=1, source_target_pairs={{0,16},{16,0},{1,17},{17,1},{2,18},{18,2},{3,19},{19,3},{4,20},{20... | collective-permute-start | bytes 786440 | tf_op jit(solution)/shard_map/ppermute | solution.py:474
  64.5 8.0 %collective-permute-done.27.refs_3_ = bf16[3,128,512]{2,1,0:T(8,128)(2,1)S(1)} collective-permute-done((bf16[3,128,512]{2,1,0:T(8,128)(2,1)S(1)}, bf16[3,128,512]{2,1,0:T(8,128)(2,1)S(1)}, u32[]{:S(2)}, u32[]{:S(2)}) %collective-permute-start.27) | collective-permute-done | bytes 393248 | tf_op jit(solution)/shard_map/ppermute | solution.py:461
  72.5 1.0 %finish.2.refs_4_ = bf16[4096,256]{1,0:T(8,128)(2,1)} custom-call(bf16[3,128,512]{2,1,0:T(8,128)(2,1)S(1)} %adjoint.6.refs_0_, bf16[3,128,512]{2,1,0:T(8,128)(2,1)S(1)} %collective-permute-done.26.refs_1_, bf16[3,128,512]{2,1,0:T(8,128)(2,1)S(1)} %adjoint.7.refs_2_, bf16[3,128,512]{2,1,0:T(8,128)(2,1)S(1)} %collective-permute-done.27.refs_3_), custom_call_target="tpu_custom_call" | custom-call | bytes 786432 | tf_op jit(solution)/shard_map/finish/pallas_call | solution.py:392
  73.5 7.4 %collective-permute-done.24.refs_1_ = bf16[3,128,512]{2,1,0:T(8,128)(2,1)S(1)} collective-permute-done((bf16[3,128,512]{2,1,0:T(8,128)(2,1)S(1)}, bf16[3,128,512]{2,1,0:T(8,128)(2,1)S(1)}, u32[]{:S(2)}, u32[]{:S(2)}) %collective-permute-start.24) | collective-permute-done | bytes 393248 | tf_op jit(solution)/shard_map/ppermute | solution.py:461
  80.9 8.4 %collective-permute-done.25.refs_3_ = bf16[3,128,512]{2,1,0:T(8,128)(2,1)S(1)} collective-permute-done((bf16[3,128,512]{2,1,0:T(8,128)(2,1)S(1)}, bf16[3,128,512]{2,1,0:T(8,128)(2,1)S(1)}, u32[]{:S(2)}, u32[]{:S(2)}) %collective-permute-start.25) | collective-permute-done | bytes 393248 | tf_op jit(solution)/shard_map/ppermute | solution.py:461
  89.4 1.0 %finish.3._ = bf16[4096,256]{1,0:T(8,128)(2,1)} custom-call(bf16[3,128,512]{2,1,0:T(8,128)(2,1)S(1)} %adjoint.4.refs_0_, bf16[3,128,512]{2,1,0:T(8,128)(2,1)S(1)} %collective-permute-done.24.refs_1_, bf16[3,128,512]{2,1,0:T(8,128)(2,1)S(1)} %adjoint.5.refs_2_, ...), custom_call_target="tpu_custom_call", output_to_operand_aliasing={{}: (4, {})} | custom-call | bytes 786432 | tf_op jit(solution)/shard_map/finish/pallas_call | solution.py:392
  91.2 3.2 %collective-permute-done.23.g_ref = bf16[256,512]{1,0:T(8,128)(2,1)S(1)} collective-permute-done((bf16[256,512]{1,0:T(8,128)(2,1)S(1)}, bf16[256,512]{1,0:T(8,128)(2,1)S(1)}, u32[]{:S(2)}, u32[]{:S(2)}) %collective-permute-start.23) | collective-permute-done | bytes 262176 | tf_op jit(solution)/shard_map/ppermute | solution.py:474
  (53 shorter events, 8.1 us)
Async XLA Ops:
  0.0 9.8 %copy-start.1 = (f32[256]{0:T(256)S(1)}, f32[256]{0:T(256)}, u32[]{:S(2)}) copy-start(f32[256]{0:T(256)} %param.8) | copy-start | bytes 3076
  6.2 3.6 %collective-permute-start = (bf16[2,128,256]{2,1,0:T(8,128)(2,1)S(1)}, bf16[2,128,256]{2,1,0:T(8,128)(2,1)S(1)}, u32[]{:S(2)}, u32[]{:S(2)}) collective-permute-start(bf16[2,128,256]{2,1,0:T(8,128)(2,1)S(1)} %get-tuple-element.11), channel_id=1, source_target_pairs={{0,1},{1,0},{2,3},{3,2},{4,5},{5,4},{6,7},{7,6},{8,9},{9,8},{10,11... | collective-permute-start | bytes 393224 | tf_op jit(solution)/shard_map/ppermute | solution.py:431
  6.8 4.6 %collective-permute-start.8 = (bf16[2,128,256]{2,1,0:T(8,128)(2,1)S(1)}, bf16[2,128,256]{2,1,0:T(8,128)(2,1)S(1)}, u32[]{:S(2)}, u32[]{:S(2)}) collective-permute-start(bf16[2,128,256]{2,1,0:T(8,128)(2,1)S(1)} %get-tuple-element.13), channel_id=1, source_target_pairs={{0,1},{1,0},{2,3},{3,2},{4,5},{5,4},{6,7},{7,6},{8,9},{9,8},{10,11... | collective-permute-start | bytes 393224 | tf_op jit(solution)/shard_map/ppermute | solution.py:431
  6.9 54.2 %collective-permute-start.22 = (bf16[2,2,512,256]{3,2,1,0:T(8,128)(2,1)S(1)}, bf16[2,2,512,256]{3,2,1,0:T(8,128)(2,1)S(1)}, u32[]{:S(2)}, u32[]{:S(2)}) collective-permute-start(bf16[2,2,512,256]{3,2,1,0:T(8,128)(2,1)S(1)} %get-tuple-element.14), channel_id=1, source_target_pairs={{0,16},{16,0},{1,17},{17,1},{2,18},{18,2},{3,19},{19,3},{4,20},{20... | collective-permute-start | bytes 3145736 | tf_op jit(solution)/shard_map/ppermute | solution.py:426
  9.9 4.9 %collective-permute-start.1 = (bf16[128,256]{1,0:T(8,128)(2,1)S(1)}, bf16[128,256]{1,0:T(8,128)(2,1)S(1)}, u32[]{:S(2)}, u32[]{:S(2)}) collective-permute-start(bf16[128,256]{1,0:T(8,128)(2,1)S(1)} %fusion.4), channel_id=1, source_target_pairs={{0,2},{1,3},{2,0},{3,1},{4,6},{5,7},{6,4},{7,5},{8,10},{9,11},{10,... | collective-permute-start | bytes 196616 | tf_op jit(solution)/shard_map/ppermute | solution.py:433
  11.5 7.7 %collective-permute-start.9 = (bf16[128,256]{1,0:T(8,128)(2,1)S(1)}, bf16[128,256]{1,0:T(8,128)(2,1)S(1)}, u32[]{:S(2)}, u32[]{:S(2)}) collective-permute-start(bf16[128,256]{1,0:T(8,128)(2,1)S(1)} %fusion.5), channel_id=1, source_target_pairs={{0,2},{1,3},{2,0},{3,1},{4,6},{5,7},{6,4},{7,5},{8,10},{9,11},{10,... | collective-permute-start | bytes 196616 | tf_op jit(solution)/shard_map/ppermute | solution.py:433
  14.8 8.2 %collective-permute-start.4 = (bf16[128,256]{1,0:T(8,128)(2,1)S(1)}, bf16[128,256]{1,0:T(8,128)(2,1)S(1)}, u32[]{:S(2)}, u32[]{:S(2)}) collective-permute-start(bf16[128,256]{1,0:T(8,128)(2,1)S(1)} %fusion.2), channel_id=1, source_target_pairs={{0,12},{1,13},{2,14},{3,15},{4,8},{5,9},{6,10},{7,11},{8,4},{9,5},... | collective-permute-start | bytes 196616 | tf_op jit(solution)/shard_map/ppermute | solution.py:438
  18.4 7.5 %collective-permute-start.3 = (bf16[128,256]{1,0:T(8,128)(2,1)S(1)}, bf16[128,256]{1,0:T(8,128)(2,1)S(1)}, u32[]{:S(2)}, u32[]{:S(2)}) collective-permute-start(bf16[128,256]{1,0:T(8,128)(2,1)S(1)} %fusion.2), channel_id=1, source_target_pairs={{0,8},{1,9},{2,10},{3,11},{4,12},{5,13},{6,14},{7,15},{8,0},{9,1},... | collective-permute-start | bytes 196616 | tf_op jit(solution)/shard_map/ppermute | solution.py:438
  18.4 7.5 %collective-permute-start.2 = (bf16[128,256]{1,0:T(8,128)(2,1)S(1)}, bf16[128,256]{1,0:T(8,128)(2,1)S(1)}, u32[]{:S(2)}, u32[]{:S(2)}) collective-permute-start(bf16[128,256]{1,0:T(8,128)(2,1)S(1)} %fusion.2), channel_id=1, source_target_pairs={{0,4},{1,5},{2,6},{3,7},{4,0},{5,1},{6,2},{7,3},{8,12},{9,13},{10,... | collective-permute-start | bytes 196616 | tf_op jit(solution)/shard_map/ppermute | solution.py:438
  19.2 8.0 %collective-permute-start.12 = (bf16[128,256]{1,0:T(8,128)(2,1)S(1)}, bf16[128,256]{1,0:T(8,128)(2,1)S(1)}, u32[]{:S(2)}, u32[]{:S(2)}) collective-permute-start(bf16[128,256]{1,0:T(8,128)(2,1)S(1)} %fusion.3), channel_id=1, source_target_pairs={{0,12},{1,13},{2,14},{3,15},{4,8},{5,9},{6,10},{7,11},{8,4},{9,5},... | collective-permute-start | bytes 196616 | tf_op jit(solution)/shard_map/ppermute | solution.py:438
  22.9 5.9 %collective-permute-start.11 = (bf16[128,256]{1,0:T(8,128)(2,1)S(1)}, bf16[128,256]{1,0:T(8,128)(2,1)S(1)}, u32[]{:S(2)}, u32[]{:S(2)}) collective-permute-start(bf16[128,256]{1,0:T(8,128)(2,1)S(1)} %fusion.3), channel_id=1, source_target_pairs={{0,8},{1,9},{2,10},{3,11},{4,12},{5,13},{6,14},{7,15},{8,0},{9,1},... | collective-permute-start | bytes 196616 | tf_op jit(solution)/shard_map/ppermute | solution.py:438
  25.9 4.3 %collective-permute-start.10 = (bf16[128,256]{1,0:T(8,128)(2,1)S(1)}, bf16[128,256]{1,0:T(8,128)(2,1)S(1)}, u32[]{:S(2)}, u32[]{:S(2)}) collective-permute-start(bf16[128,256]{1,0:T(8,128)(2,1)S(1)} %fusion.3), channel_id=1, source_target_pairs={{0,4},{1,5},{2,6},{3,7},{4,0},{5,1},{6,2},{7,3},{8,12},{9,13},{10,... | collective-permute-start | bytes 196616 | tf_op jit(solution)/shard_map/ppermute | solution.py:438
  26.0 8.2 %collective-permute-start.16 = (bf16[64,256]{1,0:T(8,128)(2,1)S(1)}, bf16[64,256]{1,0:T(8,128)(2,1)S(1)}, u32[]{:S(2)}, u32[]{:S(2)}) collective-permute-start(bf16[64,256]{1,0:T(8,128)(2,1)S(1)} %slice_select_fusion.1), channel_id=1, source_target_pairs={{0,16},{16,0},{1,17},{17,1},{2,18},{18,2},{3,19},{19,3},{4,20},{20... | collective-permute-start | bytes 98312 | tf_op jit(solution)/shard_map/ppermute | solution.py:443
  30.3 4.3 %collective-permute-start.17 = (bf16[64,256]{1,0:T(8,128)(2,1)S(1)}, bf16[64,256]{1,0:T(8,128)(2,1)S(1)}, u32[]{:S(2)}, u32[]{:S(2)}) collective-permute-start(bf16[64,256]{1,0:T(8,128)(2,1)S(1)} %slice_select_fusion), channel_id=1, source_target_pairs={{0,16},{16,0},{1,17},{17,1},{2,18},{18,2},{3,19},{19,3},{4,20},{20... | collective-permute-start | bytes 98312 | tf_op jit(solution)/shard_map/ppermute | solution.py:443
  34.6 4.3 %collective-permute-start.18 = (bf16[128,256]{1,0:T(8,128)(2,1)S(1)}, bf16[128,256]{1,0:T(8,128)(2,1)S(1)}, u32[]{:S(2)}, u32[]{:S(2)}) collective-permute-start(bf16[128,256]{1,0:T(8,128)(2,1)S(1)} %join.1.own), channel_id=1, source_target_pairs={{0,4},{1,5},{2,6},{3,7},{4,0},{5,1},{6,2},{7,3},{8,12},{9,13},{10,... | collective-permute-start | bytes 196616 | tf_op jit(solution)/shard_map/ppermute | solution.py:469
  36.4 5.0 %collective-permute-start.5 = (bf16[128,256]{1,0:T(8,128)(2,1)S(1)}, bf16[128,256]{1,0:T(8,128)(2,1)S(1)}, u32[]{:S(2)}, u32[]{:S(2)}) collective-permute-start(bf16[128,256]{1,0:T(8,128)(2,1)S(1)} %multiply_convert_fusion.1.refs_0_.r00), channel_id=1, source_target_pairs={{0,2},{1,3},{2,0},{3,1},{4,6},{5,7},{6,4},{7,5},{8,10},{9,11},{10,... | collective-permute-start | bytes 196616 | tf_op jit(solution)/shard_map/ppermute | solution.py:440
  38.9 11.5 %collective-permute-start.19 = (bf16[256,256]{1,0:T(8,128)(2,1)S(1)}, bf16[256,256]{1,0:T(8,128)(2,1)S(1)}, u32[]{:S(2)}, u32[]{:S(2)}) collective-permute-start(bf16[256,256]{1,0:T(8,128)(2,1)S(1)} %interleave.1.refs_8_), channel_id=1, source_target_pairs={{0,2},{1,3},{2,0},{3,1},{4,6},{5,7},{6,4},{7,5},{8,10},{9,11},{10,... | collective-permute-start | bytes 393224 | tf_op jit(solution)/shard_map/ppermute | solution.py:471
  40.7 1.3 %collective-permute-start.6 = (bf16[128,256]{1,0:T(8,128)(2,1)S(1)}, bf16[128,256]{1,0:T(8,128)(2,1)S(1)}, u32[]{:S(2)}, u32[]{:S(2)}) collective-permute-start(bf16[128,256]{1,0:T(8,128)(2,1)S(1)} %multiply_convert_fusion.1.refs_0_.r00), channel_id=1, source_target_pairs={{0,1},{1,0},{2,3},{3,2},{4,5},{5,4},{6,7},{7,6},{8,9},{9,8},{10,11... | collective-permute-start | bytes 196616 | tf_op jit(solution)/shard_map/ppermute | solution.py:447
  40.7 4.7 %collective-permute-start.13 = (bf16[128,256]{1,0:T(8,128)(2,1)S(1)}, bf16[128,256]{1,0:T(8,128)(2,1)S(1)}, u32[]{:S(2)}, u32[]{:S(2)}) collective-permute-start(bf16[128,256]{1,0:T(8,128)(2,1)S(1)} %multiply_convert_fusion.refs_4_.r00), channel_id=1, source_target_pairs={{0,2},{1,3},{2,0},{3,1},{4,6},{5,7},{6,4},{7,5},{8,10},{9,11},{10,... | collective-permute-start | bytes 196616 | tf_op jit(solution)/shard_map/ppermute | solution.py:440
  41.4 8.4 %collective-permute-start.7 = (bf16[128,256]{1,0:T(8,128)(2,1)S(1)}, bf16[128,256]{1,0:T(8,128)(2,1)S(1)}, u32[]{:S(2)}, u32[]{:S(2)}) collective-permute-start(bf16[128,256]{1,0:T(8,128)(2,1)S(1)} %collective-permute-done.5.refs_1_.r01), channel_id=1, source_target_pairs={{0,1},{1,0},{2,3},{3,2},{4,5},{5,4},{6,7},{7,6},{8,9},{9,8},{10,11... | collective-permute-start | bytes 196616 | tf_op jit(solution)/shard_map/ppermute | solution.py:447
  41.9 10.1 %collective-permute-start.14 = (bf16[128,256]{1,0:T(8,128)(2,1)S(1)}, bf16[128,256]{1,0:T(8,128)(2,1)S(1)}, u32[]{:S(2)}, u32[]{:S(2)}) collective-permute-start(bf16[128,256]{1,0:T(8,128)(2,1)S(1)} %multiply_convert_fusion.refs_4_.r00), channel_id=1, source_target_pairs={{0,1},{1,0},{2,3},{3,2},{4,5},{5,4},{6,7},{7,6},{8,9},{9,8},{10,11... | collective-permute-start | bytes 196616 | tf_op jit(solution)/shard_map/ppermute | solution.py:447
  45.3 8.5 %collective-permute-start.15 = (bf16[128,256]{1,0:T(8,128)(2,1)S(1)}, bf16[128,256]{1,0:T(8,128)(2,1)S(1)}, u32[]{:S(2)}, u32[]{:S(2)}) collective-permute-start(bf16[128,256]{1,0:T(8,128)(2,1)S(1)} %collective-permute-done.13.refs_5_.r01), channel_id=1, source_target_pairs={{0,1},{1,0},{2,3},{3,2},{4,5},{5,4},{6,7},{7,6},{8,9},{9,8},{10,11... | collective-permute-start | bytes 196616 | tf_op jit(solution)/shard_map/ppermute | solution.py:447
  47.5 2.9 %copy-start = (s32[2,8]{1,0:T(2,128)S(1)}, s32[2,8]{1,0:T(2,128)}, u32[]{:S(2)}) copy-start(s32[2,8]{1,0:T(2,128)} %ranks.11) | copy-start | bytes 196
  49.8 9.2 %collective-permute-start.20 = (bf16[256,256]{1,0:T(8,128)(2,1)S(1)}, bf16[256,256]{1,0:T(8,128)(2,1)S(1)}, u32[]{:S(2)}, u32[]{:S(2)}) collective-permute-start(bf16[256,256]{1,0:T(8,128)(2,1)S(1)} %interleave.1.refs_8_), channel_id=1, source_target_pairs={{0,1},{1,0},{2,3},{3,2},{4,5},{5,4},{6,7},{7,6},{8,9},{9,8},{10,11... | collective-permute-start | bytes 393224 | tf_op jit(solution)/shard_map/ppermute | solution.py:447
  50.4 10.4 %collective-permute-start.21 = (bf16[256,256]{1,0:T(8,128)(2,1)S(1)}, bf16[256,256]{1,0:T(8,128)(2,1)S(1)}, u32[]{:S(2)}, u32[]{:S(2)}) collective-permute-start(bf16[256,256]{1,0:T(8,128)(2,1)S(1)} %collective-permute-done.19.refs_9_), channel_id=1, source_target_pairs={{0,1},{1,0},{2,3},{3,2},{4,5},{5,4},{6,7},{7,6},{8,9},{9,8},{10,11... | collective-permute-start | bytes 393224 | tf_op jit(solution)/shard_map/ppermute | solution.py:447
  52.0 12.5 %collective-permute-start.26 = (bf16[3,128,512]{2,1,0:T(8,128)(2,1)S(1)}, bf16[3,128,512]{2,1,0:T(8,128)(2,1)S(1)}, u32[]{:S(2)}, u32[]{:S(2)}) collective-permute-start(bf16[3,128,512]{2,1,0:T(8,128)(2,1)S(1)} %adjoint.6.refs_0_), channel_id=1, source_target_pairs={{0,16},{16,0},{1,17},{17,1},{2,18},{18,2},{3,19},{19,3},{4,20},{20... | collective-permute-start | bytes 1179656 | tf_op jit(solution)/shard_map/ppermute | solution.py:461
  55.4 17.1 %collective-permute-start.27 = (bf16[3,128,512]{2,1,0:T(8,128)(2,1)S(1)}, bf16[3,128,512]{2,1,0:T(8,128)(2,1)S(1)}, u32[]{:S(2)}, u32[]{:S(2)}) collective-permute-start(bf16[3,128,512]{2,1,0:T(8,128)(2,1)S(1)} %adjoint.7.refs_2_), channel_id=1, source_target_pairs={{0,16},{16,0},{1,17},{17,1},{2,18},{18,2},{3,19},{19,3},{4,20},{20... | collective-permute-start | bytes 1179656 | tf_op jit(solution)/shard_map/ppermute | solution.py:461
  58.9 22.0 %collective-permute-start.24 = (bf16[3,128,512]{2,1,0:T(8,128)(2,1)S(1)}, bf16[3,128,512]{2,1,0:T(8,128)(2,1)S(1)}, u32[]{:S(2)}, u32[]{:S(2)}) collective-permute-start(bf16[3,128,512]{2,1,0:T(8,128)(2,1)S(1)} %adjoint.4.refs_0_), channel_id=1, source_target_pairs={{0,16},{16,0},{1,17},{17,1},{2,18},{18,2},{3,19},{19,3},{4,20},{20... | collective-permute-start | bytes 1179656 | tf_op jit(solution)/shard_map/ppermute | solution.py:461
  60.8 28.6 %collective-permute-start.25 = (bf16[3,128,512]{2,1,0:T(8,128)(2,1)S(1)}, bf16[3,128,512]{2,1,0:T(8,128)(2,1)S(1)}, u32[]{:S(2)}, u32[]{:S(2)}) collective-permute-start(bf16[3,128,512]{2,1,0:T(8,128)(2,1)S(1)} %adjoint.5.refs_2_), channel_id=1, source_target_pairs={{0,16},{16,0},{1,17},{17,1},{2,18},{18,2},{3,19},{19,3},{4,20},{20... | collective-permute-start | bytes 1179656 | tf_op jit(solution)/shard_map/ppermute | solution.py:461
  62.7 31.7 %collective-permute-start.23 = (bf16[256,512]{1,0:T(8,128)(2,1)S(1)}, bf16[256,512]{1,0:T(8,128)(2,1)S(1)}, u32[]{:S(2)}, u32[]{:S(2)}) collective-permute-start(bf16[256,512]{1,0:T(8,128)(2,1)S(1)} %pair.1.g_ref), channel_id=1, source_target_pairs={{0,16},{16,0},{1,17},{17,1},{2,18},{18,2},{3,19},{19,3},{4,20},{20... | collective-permute-start | bytes 786440 | tf_op jit(solution)/shard_map/ppermute | solution.py:474

commit v6 on v5

--- a/solution.py
+++ b/solution.py
@@ -258,7 +258,7 @@
         r = jnp.concatenate([theirs[q][:, span] for q in range(4)], axis=1)
         adj = dot_nn(r, permuted_rows(got[0, a], zs, rb)).astype(BF)
         total = total + dot_nt(adj, got[1, a])
-    g_ref[...] = total.astype(BF)
+    g_ref[...] = total.T.astype(BF)
 
 
 def pair_column(resid, other, got, u, v, ranks, rb, zs):
@@ -272,7 +272,7 @@
         in_specs=[IN_SMEM] + [IN_VMEM] * (len(flat) + 3),
         out_specs=IN_VMEM,
         scratch_shapes=[pltpu.VMEM((4, sources, block), BF)] * 2,
-        out_shape=pltpu.VMEM((sources, width), BF),
+        out_shape=pltpu.VMEM((width, sources), BF),
         compiler_params=pltpu.CompilerParams(vmem_limit_bytes=VMEM_LIMIT),
         cost_estimate=pl.CostEstimate(
             flops=8 * tile_rows * width * cap * sources, bytes_accessed=4 * sources * block, transcendentals=0
@@ -325,30 +325,23 @@
     )(own, rest)
 
 
-def place_kernel(tile_cols, flip, g_ref, _, out, buf, sems):
+def place_kernel(tile_cols, flip, g_ref, _, out, sem):
     row = lax.axis_index("row")
-    width = buf.shape[0]
+    width = g_ref.shape[0]
     col = tile_cols - 2 + (1 - row if flip else row)
-    part = width // 2
-    copies = []
-    for k in range(2):
-        span = slice(k * part, (k + 1) * part)
-        buf[span] = g_ref[:, span].T
-        to = pl.ds(pl.multiple_of(col * width + k * part, part), part)
-        copies.append(pltpu.make_async_copy(buf.at[span], out.at[to], sems.at[k]))
-        copies[-1].start()
-    for copy in copies:
-        copy.wait()
+    copy = pltpu.make_async_copy(g_ref, out.at[pl.ds(pl.multiple_of(col * width, width), width)], sem)
+    copy.start()
+    copy.wait()
 
 
 def place(out, column, tile_cols, flip):
-    sources, width = column.shape
+    width, sources = column.shape
     return pl.pallas_call(
         functools.partial(place_kernel, tile_cols, flip),
         in_specs=[IN_VMEM, IN_HBM],
         out_specs=IN_HBM,
         out_shape=jax.ShapeDtypeStruct(out.shape, BF),
-        scratch_shapes=[pltpu.VMEM((width, sources), BF), pltpu.SemaphoreType.DMA((2,))],
+        scratch_shapes=[pltpu.SemaphoreType.DMA],
         input_output_aliases={1: 0},
         compiler_params=pltpu.CompilerParams(vmem_limit_bytes=VMEM_LIMIT),
         cost_estimate=pl.CostEstimate(flops=0, bytes_accessed=2 * sources * width, transcendentals=0),

time: 95.5 us -> 95.4 us (level)
  no operation moved by 1% of the time
where the time goes in v6:
time: 95.4 us; the launch traced here: 95.2 us
  waiting for transfers between devices  43.9 us (46%)
  starting transfers between devices  28.5 us (30%)
  Pallas kernels  22.1 us (23%)
    ppermute x4, waiting for transfers between devices, local(): swapped[i].append((start, part, lax.ppermute(part, 'row', row_swap)))  23.7 us
    ppermute x6, starting transfers between devices, residual(): total = total + lax.ppermute(mine, 'col', p).astype(F32)  8.21 us
    pallas_call x4, Pallas kernels, adjoint(): pl.pallas_call(functools.partial(adjoint_kernel, dims), in_specs=[IN_SMEM...  6.28 us
    pallas_call x1, Pallas kernels, forward(): pl.pallas_call(functools.partial(forward_kernel, dims), in_specs=[IN_SMEM...  6.22 us
    ppermute x6, waiting for transfers between devices, residual(): total = total + lax.ppermute(mine, 'col', p).astype(F32)  5.89 us
    pallas_call x2, Pallas kernels, hold(): pl.pallas_call(hold_kernel, in_specs=[IN_HBM], out_specs=pl.BlockSpec(mem...  4.4 us
    ppermute x4, starting transfers between devices, local(): swapped[i].append((start, part, lax.ppermute(part, 'row', row_swap)))  4.25 us
    ppermute x2, waiting for transfers between devices, residual(): r01 = lax.ppermute(r00, 'col', x_swap)  3.63 us
  transfers between devices with their start and end apart: 28, of which 14 were waited for; matrix products, arithmetic and copies ran while one was open for 0% of the time, Pallas kernels for 16%

profile of v6, /device:TPU:0, one launch (start us, length us, event | category | flops | bytes accessed | tf_op | source)
XLA Modules:
  0.0 95.2 jit_solution(11354589293014967454)
XLA Ops:
  0.0 6.2 %forward.1 = (f32[2,128,256]{2,1,0:T(8,128)S(1)}, f32[2,128,256]{2,1,0:T(8,128)S(1)}, bf16[2,128,256]{2,1,0:T(8,128)(2,1)S(1)}, bf16[2,128,256]{2,1,0:T(8,128)(2,1)S(1)}, bf16[2,2,512,256]{3,2,1,0:T(8,128)(2,1)S(1)}) custom-call(s32[2,8]{1,0:T(2,128)} %ranks.11, bf16[64,256]{1,0:T(8,128)(2,1)} %obs.1, bf16[4096,256]{1,0:T(8,128)(2,1)} %x_hbm.1, ...), custom_call_target="tpu_custom_call" | custom-call | flops 2147483648 | bytes 10485760 | tf_op jit(solution)/shard_map/forward/pallas_call | solution.py:146
  6.9 2.9 %collective-permute-start.22 = (bf16[2,2,512,256]{3,2,1,0:T(8,128)(2,1)S(1)}, bf16[2,2,512,256]{3,2,1,0:T(8,128)(2,1)S(1)}, u32[]{:S(2)}, u32[]{:S(2)}) collective-permute-start(bf16[2,2,512,256]{3,2,1,0:T(8,128)(2,1)S(1)} %get-tuple-element.14), channel_id=1, source_target_pairs={{0,16},{16,0},{1,17},{17,1},{2,18},{18,2},{3,19},{19,3},{4,20},{20... | collective-permute-start | bytes 3145736 | tf_op jit(solution)/shard_map/ppermute | solution.py:419
  9.9 1.6 %collective-permute-start.1 = (bf16[128,256]{1,0:T(8,128)(2,1)S(1)}, bf16[128,256]{1,0:T(8,128)(2,1)S(1)}, u32[]{:S(2)}, u32[]{:S(2)}) collective-permute-start(bf16[128,256]{1,0:T(8,128)(2,1)S(1)} %fusion.4), channel_id=1, source_target_pairs={{0,2},{1,3},{2,0},{3,1},{4,6},{5,7},{6,4},{7,5},{8,10},{9,11},{10,... | collective-permute-start | bytes 196616 | tf_op jit(solution)/shard_map/ppermute | solution.py:426
  12.1 2.7 %collective-permute-done.1 = bf16[128,256]{1,0:T(8,128)(2,1)S(1)} collective-permute-done((bf16[128,256]{1,0:T(8,128)(2,1)S(1)}, bf16[128,256]{1,0:T(8,128)(2,1)S(1)}, u32[]{:S(2)}, u32[]{:S(2)}) %collective-permute-start.1) | collective-permute-done | bytes 65568 | tf_op jit(solution)/shard_map/ppermute | solution.py:426
  14.8 3.7 %collective-permute-start.4 = (bf16[128,256]{1,0:T(8,128)(2,1)S(1)}, bf16[128,256]{1,0:T(8,128)(2,1)S(1)}, u32[]{:S(2)}, u32[]{:S(2)}) collective-permute-start(bf16[128,256]{1,0:T(8,128)(2,1)S(1)} %fusion.2), channel_id=1, source_target_pairs={{0,12},{1,13},{2,14},{3,15},{4,8},{5,9},{6,10},{7,11},{8,4},{9,5},... | collective-permute-start | bytes 196616 | tf_op jit(solution)/shard_map/ppermute | solution.py:431
  19.2 3.7 %collective-permute-start.12 = (bf16[128,256]{1,0:T(8,128)(2,1)S(1)}, bf16[128,256]{1,0:T(8,128)(2,1)S(1)}, u32[]{:S(2)}, u32[]{:S(2)}) collective-permute-start(bf16[128,256]{1,0:T(8,128)(2,1)S(1)} %fusion.3), channel_id=1, source_target_pairs={{0,12},{1,13},{2,14},{3,15},{4,8},{5,9},{6,10},{7,11},{8,4},{9,5},... | collective-permute-start | bytes 196616 | tf_op jit(solution)/shard_map/ppermute | solution.py:431
  23.0 2.9 %collective-permute-done.3 = bf16[128,256]{1,0:T(8,128)(2,1)S(1)} collective-permute-done((bf16[128,256]{1,0:T(8,128)(2,1)S(1)}, bf16[128,256]{1,0:T(8,128)(2,1)S(1)}, u32[]{:S(2)}, u32[]{:S(2)}) %collective-permute-start.3) | collective-permute-done | bytes 65568 | tf_op jit(solution)/shard_map/ppermute | solution.py:431
  26.0 1.2 %collective-permute-start.16 = (bf16[64,256]{1,0:T(8,128)(2,1)S(1)}, bf16[64,256]{1,0:T(8,128)(2,1)S(1)}, u32[]{:S(2)}, u32[]{:S(2)}) collective-permute-start(bf16[64,256]{1,0:T(8,128)(2,1)S(1)} %slice_select_fusion.1), channel_id=1, source_target_pairs={{0,16},{16,0},{1,17},{17,1},{2,18},{18,2},{3,19},{19,3},{4,20},{20... | collective-permute-start | bytes 98312 | tf_op jit(solution)/shard_map/ppermute | solution.py:436
  27.2 1.7 %collective-permute-done.11 = bf16[128,256]{1,0:T(8,128)(2,1)S(1)} collective-permute-done((bf16[128,256]{1,0:T(8,128)(2,1)S(1)}, bf16[128,256]{1,0:T(8,128)(2,1)S(1)}, u32[]{:S(2)}, u32[]{:S(2)}) %collective-permute-start.11) | collective-permute-done | bytes 65568 | tf_op jit(solution)/shard_map/ppermute | solution.py:431
  28.9 1.3 %collective-permute-done.10 = bf16[128,256]{1,0:T(8,128)(2,1)S(1)} collective-permute-done((bf16[128,256]{1,0:T(8,128)(2,1)S(1)}, bf16[128,256]{1,0:T(8,128)(2,1)S(1)}, u32[]{:S(2)}, u32[]{:S(2)}) %collective-permute-start.10) | collective-permute-done | bytes 65568 | tf_op jit(solution)/shard_map/ppermute | solution.py:431
  30.3 1.2 %collective-permute-start.17 = (bf16[64,256]{1,0:T(8,128)(2,1)S(1)}, bf16[64,256]{1,0:T(8,128)(2,1)S(1)}, u32[]{:S(2)}, u32[]{:S(2)}) collective-permute-start(bf16[64,256]{1,0:T(8,128)(2,1)S(1)} %slice_select_fusion), channel_id=1, source_target_pairs={{0,16},{16,0},{1,17},{17,1},{2,18},{18,2},{3,19},{19,3},{4,20},{20... | collective-permute-start | bytes 98312 | tf_op jit(solution)/shard_map/ppermute | solution.py:436
  31.5 2.8 %collective-permute-done.16.refs_0_ = bf16[64,256]{1,0:T(8,128)(2,1)S(1)} collective-permute-done((bf16[64,256]{1,0:T(8,128)(2,1)S(1)}, bf16[64,256]{1,0:T(8,128)(2,1)S(1)}, u32[]{:S(2)}, u32[]{:S(2)}) %collective-permute-start.16) | collective-permute-done | bytes 32800 | tf_op jit(solution)/shard_map/ppermute | solution.py:436
  34.6 1.8 %collective-permute-start.18 = (bf16[128,256]{1,0:T(8,128)(2,1)S(1)}, bf16[128,256]{1,0:T(8,128)(2,1)S(1)}, u32[]{:S(2)}, u32[]{:S(2)}) collective-permute-start(bf16[128,256]{1,0:T(8,128)(2,1)S(1)} %join.1.own), channel_id=1, source_target_pairs={{0,4},{1,5},{2,6},{3,7},{4,0},{5,1},{6,2},{7,3},{8,12},{9,13},{10,... | collective-permute-start | bytes 196616 | tf_op jit(solution)/shard_map/ppermute | solution.py:462
  36.4 1.5 %collective-permute-start.5 = (bf16[128,256]{1,0:T(8,128)(2,1)S(1)}, bf16[128,256]{1,0:T(8,128)(2,1)S(1)}, u32[]{:S(2)}, u32[]{:S(2)}) collective-permute-start(bf16[128,256]{1,0:T(8,128)(2,1)S(1)} %multiply_convert_fusion.1.refs_0_.r00), channel_id=1, source_target_pairs={{0,2},{1,3},{2,0},{3,1},{4,6},{5,7},{6,4},{7,5},{8,10},{9,11},{10,... | collective-permute-start | bytes 196616 | tf_op jit(solution)/shard_map/ppermute | solution.py:433
  38.9 1.8 %collective-permute-start.19 = (bf16[256,256]{1,0:T(8,128)(2,1)S(1)}, bf16[256,256]{1,0:T(8,128)(2,1)S(1)}, u32[]{:S(2)}, u32[]{:S(2)}) collective-permute-start(bf16[256,256]{1,0:T(8,128)(2,1)S(1)} %interleave.1.refs_8_), channel_id=1, source_target_pairs={{0,2},{1,3},{2,0},{3,1},{4,6},{5,7},{6,4},{7,5},{8,10},{9,11},{10,... | collective-permute-start | bytes 393224 | tf_op jit(solution)/shard_map/ppermute | solution.py:464
  42.1 3.2 %collective-permute-done.13.refs_5_.r01 = bf16[128,256]{1,0:T(8,128)(2,1)S(1)} collective-permute-done((bf16[128,256]{1,0:T(8,128)(2,1)S(1)}, bf16[128,256]{1,0:T(8,128)(2,1)S(1)}, u32[]{:S(2)}, u32[]{:S(2)}) %collective-permute-start.13) | collective-permute-done | bytes 65568 | tf_op jit(solution)/shard_map/ppermute | solution.py:433
  45.3 2.2 %hold.2.refs_13_.u_ref = bf16[2,8,512,256]{3,2,1,0:T(8,128)(2,1)S(1)} custom-call(bf16[2,8,512,256]{3,2,1,0:T(8,128)(2,1)} %src.2), custom_call_target="tpu_custom_call" | custom-call | bytes 4194304 | tf_op jit(solution)/shard_map/hold/pallas_call | solution.py:179
  47.6 2.2 %hold.3.refs_14_.v_ref = bf16[2,8,512,256]{3,2,1,0:T(8,128)(2,1)S(1)} custom-call(bf16[2,8,512,256]{3,2,1,0:T(8,128)(2,1)} %src.3), custom_call_target="tpu_custom_call" | custom-call | bytes 4194304 | tf_op jit(solution)/shard_map/hold/pallas_call | solution.py:179
  50.4 1.6 %adjoint.6.refs_0_ = bf16[3,128,512]{2,1,0:T(8,128)(2,1)S(1)} custom-call(s32[2,8]{1,0:T(2,128)S(1)} %copy-done, bf16[128,256]{1,0:T(8,128)(2,1)S(1)} %multiply_convert_fusion.1.refs_0_.r00, bf16[128,256]{1,0:T(8,128)(2,1)S(1)} %collective-permute-done.5.refs_1_.r01, bf16[128,256]{1,0:T(8,128)(2,1)S(1)} %collective-permute-done.6.refs_2_.r10, ...), custom_call_target="tpu_custom_call" | custom-call | flops 402653184 | bytes 131072 | tf_op jit(solution)/shard_map/adjoint/pallas_call | solution.py:219
  52.0 1.8 %collective-permute-start.26 = (bf16[3,128,512]{2,1,0:T(8,128)(2,1)S(1)}, bf16[3,128,512]{2,1,0:T(8,128)(2,1)S(1)}, u32[]{:S(2)}, u32[]{:S(2)}) collective-permute-start(bf16[3,128,512]{2,1,0:T(8,128)(2,1)S(1)} %adjoint.6.refs_0_), channel_id=1, source_target_pairs={{0,16},{16,0},{1,17},{17,1},{2,18},{18,2},{3,19},{19,3},{4,20},{20... | collective-permute-start | bytes 1179656 | tf_op jit(solution)/shard_map/ppermute | solution.py:454
  53.8 1.6 %adjoint.7.refs_2_ = bf16[3,128,512]{2,1,0:T(8,128)(2,1)S(1)} custom-call(s32[2,8]{1,0:T(2,128)S(1)} %copy-done, bf16[128,256]{1,0:T(8,128)(2,1)S(1)} %multiply_convert_fusion.refs_4_.r00, bf16[128,256]{1,0:T(8,128)(2,1)S(1)} %collective-permute-done.13.refs_5_.r01, bf16[128,256]{1,0:T(8,128)(2,1)S(1)} %collective-permute-done.14.refs_6_.r10, ...), custom_call_target="tpu_custom_call" | custom-call | flops 402653184 | bytes 131072 | tf_op jit(solution)/shard_map/adjoint/pallas_call | solution.py:219
  55.8 1.6 %adjoint.5.refs_2_ = bf16[3,128,512]{2,1,0:T(8,128)(2,1)S(1)} custom-call(s32[2,8]{1,0:T(2,128)S(1)} %copy-done, bf16[128,256]{1,0:T(8,128)(2,1)S(1)} %multiply_convert_fusion.refs_4_.r00, bf16[128,256]{1,0:T(8,128)(2,1)S(1)} %collective-permute-done.13.refs_5_.r01, bf16[128,256]{1,0:T(8,128)(2,1)S(1)} %collective-permute-done.14.refs_6_.r10, ...), custom_call_target="tpu_custom_call" | custom-call | flops 402653184 | bytes 131072 | tf_op jit(solution)/shard_map/adjoint/pallas_call | solution.py:219
  57.3 1.6 %adjoint.4.refs_0_ = bf16[3,128,512]{2,1,0:T(8,128)(2,1)S(1)} custom-call(s32[2,8]{1,0:T(2,128)S(1)} %copy-done, bf16[128,256]{1,0:T(8,128)(2,1)S(1)} %multiply_convert_fusion.1.refs_0_.r00, bf16[128,256]{1,0:T(8,128)(2,1)S(1)} %collective-permute-done.5.refs_1_.r01, bf16[128,256]{1,0:T(8,128)(2,1)S(1)} %collective-permute-done.6.refs_2_.r10, ...), custom_call_target="tpu_custom_call" | custom-call | flops 402653184 | bytes 131072 | tf_op jit(solution)/shard_map/adjoint/pallas_call | solution.py:219
  58.9 1.8 %collective-permute-start.24 = (bf16[3,128,512]{2,1,0:T(8,128)(2,1)S(1)}, bf16[3,128,512]{2,1,0:T(8,128)(2,1)S(1)}, u32[]{:S(2)}, u32[]{:S(2)}) collective-permute-start(bf16[3,128,512]{2,1,0:T(8,128)(2,1)S(1)} %adjoint.4.refs_0_), channel_id=1, source_target_pairs={{0,16},{16,0},{1,17},{17,1},{2,18},{18,2},{3,19},{19,3},{4,20},{20... | collective-permute-start | bytes 1179656 | tf_op jit(solution)/shard_map/ppermute | solution.py:454
  61.0 1.7 %pair.1.g_ref = bf16[512,256]{1,0:T(8,128)(2,1)S(1)} custom-call(s32[2,8]{1,0:T(2,128)S(1)} %copy-done, bf16[128,256]{1,0:T(8,128)(2,1)S(1)} %multiply_convert_fusion.1.refs_0_.r00, bf16[128,256]{1,0:T(8,128)(2,1)S(1)} %collective-permute-done.5.refs_1_.r01, bf16[128,256]{1,0:T(8,128)(2,1)S(1)} %collective-permute-done.6.refs_2_.r10, ...), custom_call_target="tpu_custom_call" | custom-call | flops 536870912 | bytes 262144 | tf_op jit(solution)/shard_map/pair/pallas_call | solution.py:270
  62.8 1.8 %collective-permute-start.23 = (bf16[512,256]{1,0:T(8,128)(2,1)S(1)}, bf16[512,256]{1,0:T(8,128)(2,1)S(1)}, u32[]{:S(2)}, u32[]{:S(2)}) collective-permute-start(bf16[512,256]{1,0:T(8,128)(2,1)S(1)} %pair.1.g_ref), channel_id=1, source_target_pairs={{0,16},{16,0},{1,17},{17,1},{2,18},{18,2},{3,19},{19,3},{4,20},{20... | collective-permute-start | bytes 786440 | tf_op jit(solution)/shard_map/ppermute | solution.py:467
  64.6 7.9 %collective-permute-done.27.refs_3_ = bf16[3,128,512]{2,1,0:T(8,128)(2,1)S(1)} collective-permute-done((bf16[3,128,512]{2,1,0:T(8,128)(2,1)S(1)}, bf16[3,128,512]{2,1,0:T(8,128)(2,1)S(1)}, u32[]{:S(2)}, u32[]{:S(2)}) %collective-permute-start.27) | collective-permute-done | bytes 393248 | tf_op jit(solution)/shard_map/ppermute | solution.py:454
  72.5 1.0 %finish.2.refs_4_ = bf16[4096,256]{1,0:T(8,128)(2,1)} custom-call(bf16[3,128,512]{2,1,0:T(8,128)(2,1)S(1)} %adjoint.6.refs_0_, bf16[3,128,512]{2,1,0:T(8,128)(2,1)S(1)} %collective-permute-done.26.refs_1_, bf16[3,128,512]{2,1,0:T(8,128)(2,1)S(1)} %adjoint.7.refs_2_, bf16[3,128,512]{2,1,0:T(8,128)(2,1)S(1)} %collective-permute-done.27.refs_3_), custom_call_target="tpu_custom_call" | custom-call | bytes 786432 | tf_op jit(solution)/shard_map/finish/pallas_call | solution.py:385
  73.5 7.4 %collective-permute-done.24.refs_1_ = bf16[3,128,512]{2,1,0:T(8,128)(2,1)S(1)} collective-permute-done((bf16[3,128,512]{2,1,0:T(8,128)(2,1)S(1)}, bf16[3,128,512]{2,1,0:T(8,128)(2,1)S(1)}, u32[]{:S(2)}, u32[]{:S(2)}) %collective-permute-start.24) | collective-permute-done | bytes 393248 | tf_op jit(solution)/shard_map/ppermute | solution.py:454
  80.9 8.4 %collective-permute-done.25.refs_3_ = bf16[3,128,512]{2,1,0:T(8,128)(2,1)S(1)} collective-permute-done((bf16[3,128,512]{2,1,0:T(8,128)(2,1)S(1)}, bf16[3,128,512]{2,1,0:T(8,128)(2,1)S(1)}, u32[]{:S(2)}, u32[]{:S(2)}) %collective-permute-start.25) | collective-permute-done | bytes 393248 | tf_op jit(solution)/shard_map/ppermute | solution.py:454
  89.4 1.0 %finish.3._ = bf16[4096,256]{1,0:T(8,128)(2,1)} custom-call(bf16[3,128,512]{2,1,0:T(8,128)(2,1)S(1)} %adjoint.4.refs_0_, bf16[3,128,512]{2,1,0:T(8,128)(2,1)S(1)} %collective-permute-done.24.refs_1_, bf16[3,128,512]{2,1,0:T(8,128)(2,1)S(1)} %adjoint.5.refs_2_, ...), custom_call_target="tpu_custom_call", output_to_operand_aliasing={{}: (4, {})} | custom-call | bytes 786432 | tf_op jit(solution)/shard_map/finish/pallas_call | solution.py:385
  91.1 3.3 %collective-permute-done.23.g_ref = bf16[512,256]{1,0:T(8,128)(2,1)S(1)} collective-permute-done((bf16[512,256]{1,0:T(8,128)(2,1)S(1)}, bf16[512,256]{1,0:T(8,128)(2,1)S(1)}, u32[]{:S(2)}, u32[]{:S(2)}) %collective-permute-start.23) | collective-permute-done | bytes 262176 | tf_op jit(solution)/shard_map/ppermute | solution.py:467
  (53 shorter events, 7.9 us)
Async XLA Ops:
  0.0 9.8 %copy-start.1 = (f32[256]{0:T(256)S(1)}, f32[256]{0:T(256)}, u32[]{:S(2)}) copy-start(f32[256]{0:T(256)} %param.8) | copy-start | bytes 3076
  6.2 3.6 %collective-permute-start = (bf16[2,128,256]{2,1,0:T(8,128)(2,1)S(1)}, bf16[2,128,256]{2,1,0:T(8,128)(2,1)S(1)}, u32[]{:S(2)}, u32[]{:S(2)}) collective-permute-start(bf16[2,128,256]{2,1,0:T(8,128)(2,1)S(1)} %get-tuple-element.11), channel_id=1, source_target_pairs={{0,1},{1,0},{2,3},{3,2},{4,5},{5,4},{6,7},{7,6},{8,9},{9,8},{10,11... | collective-permute-start | bytes 393224 | tf_op jit(solution)/shard_map/ppermute | solution.py:424
  6.8 4.6 %collective-permute-start.8 = (bf16[2,128,256]{2,1,0:T(8,128)(2,1)S(1)}, bf16[2,128,256]{2,1,0:T(8,128)(2,1)S(1)}, u32[]{:S(2)}, u32[]{:S(2)}) collective-permute-start(bf16[2,128,256]{2,1,0:T(8,128)(2,1)S(1)} %get-tuple-element.13), channel_id=1, source_target_pairs={{0,1},{1,0},{2,3},{3,2},{4,5},{5,4},{6,7},{7,6},{8,9},{9,8},{10,11... | collective-permute-start | bytes 393224 | tf_op jit(solution)/shard_map/ppermute | solution.py:424
  6.9 54.2 %collective-permute-start.22 = (bf16[2,2,512,256]{3,2,1,0:T(8,128)(2,1)S(1)}, bf16[2,2,512,256]{3,2,1,0:T(8,128)(2,1)S(1)}, u32[]{:S(2)}, u32[]{:S(2)}) collective-permute-start(bf16[2,2,512,256]{3,2,1,0:T(8,128)(2,1)S(1)} %get-tuple-element.14), channel_id=1, source_target_pairs={{0,16},{16,0},{1,17},{17,1},{2,18},{18,2},{3,19},{19,3},{4,20},{20... | collective-permute-start | bytes 3145736 | tf_op jit(solution)/shard_map/ppermute | solution.py:419
  9.9 4.9 %collective-permute-start.1 = (bf16[128,256]{1,0:T(8,128)(2,1)S(1)}, bf16[128,256]{1,0:T(8,128)(2,1)S(1)}, u32[]{:S(2)}, u32[]{:S(2)}) collective-permute-start(bf16[128,256]{1,0:T(8,128)(2,1)S(1)} %fusion.4), channel_id=1, source_target_pairs={{0,2},{1,3},{2,0},{3,1},{4,6},{5,7},{6,4},{7,5},{8,10},{9,11},{10,... | collective-permute-start | bytes 196616 | tf_op jit(solution)/shard_map/ppermute | solution.py:426
  11.5 7.7 %collective-permute-start.9 = (bf16[128,256]{1,0:T(8,128)(2,1)S(1)}, bf16[128,256]{1,0:T(8,128)(2,1)S(1)}, u32[]{:S(2)}, u32[]{:S(2)}) collective-permute-start(bf16[128,256]{1,0:T(8,128)(2,1)S(1)} %fusion.5), channel_id=1, source_target_pairs={{0,2},{1,3},{2,0},{3,1},{4,6},{5,7},{6,4},{7,5},{8,10},{9,11},{10,... | collective-permute-start | bytes 196616 | tf_op jit(solution)/shard_map/ppermute | solution.py:426
  14.8 8.2 %collective-permute-start.4 = (bf16[128,256]{1,0:T(8,128)(2,1)S(1)}, bf16[128,256]{1,0:T(8,128)(2,1)S(1)}, u32[]{:S(2)}, u32[]{:S(2)}) collective-permute-start(bf16[128,256]{1,0:T(8,128)(2,1)S(1)} %fusion.2), channel_id=1, source_target_pairs={{0,12},{1,13},{2,14},{3,15},{4,8},{5,9},{6,10},{7,11},{8,4},{9,5},... | collective-permute-start | bytes 196616 | tf_op jit(solution)/shard_map/ppermute | solution.py:431
  18.4 7.5 %collective-permute-start.3 = (bf16[128,256]{1,0:T(8,128)(2,1)S(1)}, bf16[128,256]{1,0:T(8,128)(2,1)S(1)}, u32[]{:S(2)}, u32[]{:S(2)}) collective-permute-start(bf16[128,256]{1,0:T(8,128)(2,1)S(1)} %fusion.2), channel_id=1, source_target_pairs={{0,8},{1,9},{2,10},{3,11},{4,12},{5,13},{6,14},{7,15},{8,0},{9,1},... | collective-permute-start | bytes 196616 | tf_op jit(solution)/shard_map/ppermute | solution.py:431
  18.4 7.5 %collective-permute-start.2 = (bf16[128,256]{1,0:T(8,128)(2,1)S(1)}, bf16[128,256]{1,0:T(8,128)(2,1)S(1)}, u32[]{:S(2)}, u32[]{:S(2)}) collective-permute-start(bf16[128,256]{1,0:T(8,128)(2,1)S(1)} %fusion.2), channel_id=1, source_target_pairs={{0,4},{1,5},{2,6},{3,7},{4,0},{5,1},{6,2},{7,3},{8,12},{9,13},{10,... | collective-permute-start | bytes 196616 | tf_op jit(solution)/shard_map/ppermute | solution.py:431
  19.2 8.0 %collective-permute-start.12 = (bf16[128,256]{1,0:T(8,128)(2,1)S(1)}, bf16[128,256]{1,0:T(8,128)(2,1)S(1)}, u32[]{:S(2)}, u32[]{:S(2)}) collective-permute-start(bf16[128,256]{1,0:T(8,128)(2,1)S(1)} %fusion.3), channel_id=1, source_target_pairs={{0,12},{1,13},{2,14},{3,15},{4,8},{5,9},{6,10},{7,11},{8,4},{9,5},... | collective-permute-start | bytes 196616 | tf_op jit(solution)/shard_map/ppermute | solution.py:431
  22.9 5.9 %collective-permute-start.11 = (bf16[128,256]{1,0:T(8,128)(2,1)S(1)}, bf16[128,256]{1,0:T(8,128)(2,1)S(1)}, u32[]{:S(2)}, u32[]{:S(2)}) collective-permute-start(bf16[128,256]{1,0:T(8,128)(2,1)S(1)} %fusion.3), channel_id=1, source_target_pairs={{0,8},{1,9},{2,10},{3,11},{4,12},{5,13},{6,14},{7,15},{8,0},{9,1},... | collective-permute-start | bytes 196616 | tf_op jit(solution)/shard_map/ppermute | solution.py:431
  25.9 4.3 %collective-permute-start.10 = (bf16[128,256]{1,0:T(8,128)(2,1)S(1)}, bf16[128,256]{1,0:T(8,128)(2,1)S(1)}, u32[]{:S(2)}, u32[]{:S(2)}) collective-permute-start(bf16[128,256]{1,0:T(8,128)(2,1)S(1)} %fusion.3), channel_id=1, source_target_pairs={{0,4},{1,5},{2,6},{3,7},{4,0},{5,1},{6,2},{7,3},{8,12},{9,13},{10,... | collective-permute-start | bytes 196616 | tf_op jit(solution)/shard_map/ppermute | solution.py:431
  26.0 8.2 %collective-permute-start.16 = (bf16[64,256]{1,0:T(8,128)(2,1)S(1)}, bf16[64,256]{1,0:T(8,128)(2,1)S(1)}, u32[]{:S(2)}, u32[]{:S(2)}) collective-permute-start(bf16[64,256]{1,0:T(8,128)(2,1)S(1)} %slice_select_fusion.1), channel_id=1, source_target_pairs={{0,16},{16,0},{1,17},{17,1},{2,18},{18,2},{3,19},{19,3},{4,20},{20... | collective-permute-start | bytes 98312 | tf_op jit(solution)/shard_map/ppermute | solution.py:436
  30.3 4.3 %collective-permute-start.17 = (bf16[64,256]{1,0:T(8,128)(2,1)S(1)}, bf16[64,256]{1,0:T(8,128)(2,1)S(1)}, u32[]{:S(2)}, u32[]{:S(2)}) collective-permute-start(bf16[64,256]{1,0:T(8,128)(2,1)S(1)} %slice_select_fusion), channel_id=1, source_target_pairs={{0,16},{16,0},{1,17},{17,1},{2,18},{18,2},{3,19},{19,3},{4,20},{20... | collective-permute-start | bytes 98312 | tf_op jit(solution)/shard_map/ppermute | solution.py:436
  34.6 4.3 %collective-permute-start.18 = (bf16[128,256]{1,0:T(8,128)(2,1)S(1)}, bf16[128,256]{1,0:T(8,128)(2,1)S(1)}, u32[]{:S(2)}, u32[]{:S(2)}) collective-permute-start(bf16[128,256]{1,0:T(8,128)(2,1)S(1)} %join.1.own), channel_id=1, source_target_pairs={{0,4},{1,5},{2,6},{3,7},{4,0},{5,1},{6,2},{7,3},{8,12},{9,13},{10,... | collective-permute-start | bytes 196616 | tf_op jit(solution)/shard_map/ppermute | solution.py:462
  36.4 5.0 %collective-permute-start.5 = (bf16[128,256]{1,0:T(8,128)(2,1)S(1)}, bf16[128,256]{1,0:T(8,128)(2,1)S(1)}, u32[]{:S(2)}, u32[]{:S(2)}) collective-permute-start(bf16[128,256]{1,0:T(8,128)(2,1)S(1)} %multiply_convert_fusion.1.refs_0_.r00), channel_id=1, source_target_pairs={{0,2},{1,3},{2,0},{3,1},{4,6},{5,7},{6,4},{7,5},{8,10},{9,11},{10,... | collective-permute-start | bytes 196616 | tf_op jit(solution)/shard_map/ppermute | solution.py:433
  38.9 11.5 %collective-permute-start.19 = (bf16[256,256]{1,0:T(8,128)(2,1)S(1)}, bf16[256,256]{1,0:T(8,128)(2,1)S(1)}, u32[]{:S(2)}, u32[]{:S(2)}) collective-permute-start(bf16[256,256]{1,0:T(8,128)(2,1)S(1)} %interleave.1.refs_8_), channel_id=1, source_target_pairs={{0,2},{1,3},{2,0},{3,1},{4,6},{5,7},{6,4},{7,5},{8,10},{9,11},{10,... | collective-permute-start | bytes 393224 | tf_op jit(solution)/shard_map/ppermute | solution.py:464
  40.7 1.3 %collective-permute-start.6 = (bf16[128,256]{1,0:T(8,128)(2,1)S(1)}, bf16[128,256]{1,0:T(8,128)(2,1)S(1)}, u32[]{:S(2)}, u32[]{:S(2)}) collective-permute-start(bf16[128,256]{1,0:T(8,128)(2,1)S(1)} %multiply_convert_fusion.1.refs_0_.r00), channel_id=1, source_target_pairs={{0,1},{1,0},{2,3},{3,2},{4,5},{5,4},{6,7},{7,6},{8,9},{9,8},{10,11... | collective-permute-start | bytes 196616 | tf_op jit(solution)/shard_map/ppermute | solution.py:440
  40.7 4.7 %collective-permute-start.13 = (bf16[128,256]{1,0:T(8,128)(2,1)S(1)}, bf16[128,256]{1,0:T(8,128)(2,1)S(1)}, u32[]{:S(2)}, u32[]{:S(2)}) collective-permute-start(bf16[128,256]{1,0:T(8,128)(2,1)S(1)} %multiply_convert_fusion.refs_4_.r00), channel_id=1, source_target_pairs={{0,2},{1,3},{2,0},{3,1},{4,6},{5,7},{6,4},{7,5},{8,10},{9,11},{10,... | collective-permute-start | bytes 196616 | tf_op jit(solution)/shard_map/ppermute | solution.py:433
  41.4 8.4 %collective-permute-start.7 = (bf16[128,256]{1,0:T(8,128)(2,1)S(1)}, bf16[128,256]{1,0:T(8,128)(2,1)S(1)}, u32[]{:S(2)}, u32[]{:S(2)}) collective-permute-start(bf16[128,256]{1,0:T(8,128)(2,1)S(1)} %collective-permute-done.5.refs_1_.r01), channel_id=1, source_target_pairs={{0,1},{1,0},{2,3},{3,2},{4,5},{5,4},{6,7},{7,6},{8,9},{9,8},{10,11... | collective-permute-start | bytes 196616 | tf_op jit(solution)/shard_map/ppermute | solution.py:440
  41.9 10.1 %collective-permute-start.14 = (bf16[128,256]{1,0:T(8,128)(2,1)S(1)}, bf16[128,256]{1,0:T(8,128)(2,1)S(1)}, u32[]{:S(2)}, u32[]{:S(2)}) collective-permute-start(bf16[128,256]{1,0:T(8,128)(2,1)S(1)} %multiply_convert_fusion.refs_4_.r00), channel_id=1, source_target_pairs={{0,1},{1,0},{2,3},{3,2},{4,5},{5,4},{6,7},{7,6},{8,9},{9,8},{10,11... | collective-permute-start | bytes 196616 | tf_op jit(solution)/shard_map/ppermute | solution.py:440
  45.3 8.5 %collective-permute-start.15 = (bf16[128,256]{1,0:T(8,128)(2,1)S(1)}, bf16[128,256]{1,0:T(8,128)(2,1)S(1)}, u32[]{:S(2)}, u32[]{:S(2)}) collective-permute-start(bf16[128,256]{1,0:T(8,128)(2,1)S(1)} %collective-permute-done.13.refs_5_.r01), channel_id=1, source_target_pairs={{0,1},{1,0},{2,3},{3,2},{4,5},{5,4},{6,7},{7,6},{8,9},{9,8},{10,11... | collective-permute-start | bytes 196616 | tf_op jit(solution)/shard_map/ppermute | solution.py:440
  47.5 2.9 %copy-start = (s32[2,8]{1,0:T(2,128)S(1)}, s32[2,8]{1,0:T(2,128)}, u32[]{:S(2)}) copy-start(s32[2,8]{1,0:T(2,128)} %ranks.11) | copy-start | bytes 196
  49.8 9.2 %collective-permute-start.20 = (bf16[256,256]{1,0:T(8,128)(2,1)S(1)}, bf16[256,256]{1,0:T(8,128)(2,1)S(1)}, u32[]{:S(2)}, u32[]{:S(2)}) collective-permute-start(bf16[256,256]{1,0:T(8,128)(2,1)S(1)} %interleave.1.refs_8_), channel_id=1, source_target_pairs={{0,1},{1,0},{2,3},{3,2},{4,5},{5,4},{6,7},{7,6},{8,9},{9,8},{10,11... | collective-permute-start | bytes 393224 | tf_op jit(solution)/shard_map/ppermute | solution.py:440
  50.4 10.4 %collective-permute-start.21 = (bf16[256,256]{1,0:T(8,128)(2,1)S(1)}, bf16[256,256]{1,0:T(8,128)(2,1)S(1)}, u32[]{:S(2)}, u32[]{:S(2)}) collective-permute-start(bf16[256,256]{1,0:T(8,128)(2,1)S(1)} %collective-permute-done.19.refs_9_), channel_id=1, source_target_pairs={{0,1},{1,0},{2,3},{3,2},{4,5},{5,4},{6,7},{7,6},{8,9},{9,8},{10,11... | collective-permute-start | bytes 393224 | tf_op jit(solution)/shard_map/ppermute | solution.py:440
  52.0 12.6 %collective-permute-start.26 = (bf16[3,128,512]{2,1,0:T(8,128)(2,1)S(1)}, bf16[3,128,512]{2,1,0:T(8,128)(2,1)S(1)}, u32[]{:S(2)}, u32[]{:S(2)}) collective-permute-start(bf16[3,128,512]{2,1,0:T(8,128)(2,1)S(1)} %adjoint.6.refs_0_), channel_id=1, source_target_pairs={{0,16},{16,0},{1,17},{17,1},{2,18},{18,2},{3,19},{19,3},{4,20},{20... | collective-permute-start | bytes 1179656 | tf_op jit(solution)/shard_map/ppermute | solution.py:454
  55.4 17.1 %collective-permute-start.27 = (bf16[3,128,512]{2,1,0:T(8,128)(2,1)S(1)}, bf16[3,128,512]{2,1,0:T(8,128)(2,1)S(1)}, u32[]{:S(2)}, u32[]{:S(2)}) collective-permute-start(bf16[3,128,512]{2,1,0:T(8,128)(2,1)S(1)} %adjoint.7.refs_2_), channel_id=1, source_target_pairs={{0,16},{16,0},{1,17},{17,1},{2,18},{18,2},{3,19},{19,3},{4,20},{20... | collective-permute-start | bytes 1179656 | tf_op jit(solution)/shard_map/ppermute | solution.py:454
  58.9 22.0 %collective-permute-start.24 = (bf16[3,128,512]{2,1,0:T(8,128)(2,1)S(1)}, bf16[3,128,512]{2,1,0:T(8,128)(2,1)S(1)}, u32[]{:S(2)}, u32[]{:S(2)}) collective-permute-start(bf16[3,128,512]{2,1,0:T(8,128)(2,1)S(1)} %adjoint.4.refs_0_), channel_id=1, source_target_pairs={{0,16},{16,0},{1,17},{17,1},{2,18},{18,2},{3,19},{19,3},{4,20},{20... | collective-permute-start | bytes 1179656 | tf_op jit(solution)/shard_map/ppermute | solution.py:454
  60.8 28.6 %collective-permute-start.25 = (bf16[3,128,512]{2,1,0:T(8,128)(2,1)S(1)}, bf16[3,128,512]{2,1,0:T(8,128)(2,1)S(1)}, u32[]{:S(2)}, u32[]{:S(2)}) collective-permute-start(bf16[3,128,512]{2,1,0:T(8,128)(2,1)S(1)} %adjoint.5.refs_2_), channel_id=1, source_target_pairs={{0,16},{16,0},{1,17},{17,1},{2,18},{18,2},{3,19},{19,3},{4,20},{20... | collective-permute-start | bytes 1179656 | tf_op jit(solution)/shard_map/ppermute | solution.py:454
  62.8 31.7 %collective-permute-start.23 = (bf16[512,256]{1,0:T(8,128)(2,1)S(1)}, bf16[512,256]{1,0:T(8,128)(2,1)S(1)}, u32[]{:S(2)}, u32[]{:S(2)}) collective-permute-start(bf16[512,256]{1,0:T(8,128)(2,1)S(1)} %pair.1.g_ref), channel_id=1, source_target_pairs={{0,16},{16,0},{1,17},{17,1},{2,18},{18,2},{3,19},{19,3},{4,20},{20... | collective-permute-start | bytes 786440 | tf_op jit(solution)/shard_map/ppermute | solution.py:467
